TPU v7x, 32 devices: a whole 2x2x4 slice. The times are simulated.
32 devices in a mesh: dp: 8 (over z, y), mem: 4 (over x, core).
Axes of the slice: x: 2, y: 2, z: 4, core: 2. Of those that a mesh axis runs over, the one named last changes fastest.
Arguments:
- dec_in: bfloat16 [8, 1024, 1024], P('dp'), may hold values from -6 to 6
- memory: bfloat16 [8, 1024, 1024], P('dp', 'mem'), may hold values from -6 to 6
- dec_len: int32 [8], P('dp'), may hold values from 512 to 1024, as said below
- mem_len: int32 [8], P('dp'), may hold values from 256 to 1024, as said below
- grad_out: bfloat16 [8, 1024, 1024], P('dp'), may hold values from -6 to 6
- self_qkv: bfloat16 [1024, 3072], replicated, may hold values from -0.1875 to 0.1875
- self_out: bfloat16 [1024, 1024], replicated, may hold values from -3 to 3
- cross_q: bfloat16 [1024, 1024], replicated, may hold values from -0.1875 to 0.1875
- cross_kv: bfloat16 [1024, 2048], replicated, may hold values from -0.1875 to 0.1875
- cross_out: bfloat16 [1024, 1024], replicated, may hold values from -3 to 3
- ffn_in: bfloat16 [1024, 4096], replicated, may hold values from -0.1875 to 0.1875
- ffn_out: bfloat16 [4096, 1024], replicated, may hold values from -0.09375 to 0.09375
- proj_bias: float32 [7, 1024], replicated, may hold values from -3 to 3
- ffn_bias: float32 [4096], replicated, may hold values from -3 to 3
- norm_gain: float32 [3, 1024], replicated, may hold values from 0.5 to 1.5
- norm_shift: float32 [3, 1024], replicated, may hold values from -3 to 3
Outputs:
- layer_out: bfloat16 [8, 1024, 1024], P('dp')
- grad_dec: float32 [8, 1024, 1024], P('dp')
- grad_memory: float32 [8, 1024, 1024], P('dp', 'mem')
- grad_self_qkv: float32 [1024, 3072], P('dp')
- grad_self_out: float32 [1024, 1024], P('dp')
- grad_cross_q: float32 [1024, 1024], P('dp')
- grad_cross_kv: float32 [1024, 2048], P('dp')
- grad_cross_out: float32 [1024, 1024], P('dp')
- grad_ffn_in: float32 [1024, 4096], P('dp')
- grad_ffn_out: float32 [4096, 1024], P('dp')
- grad_proj_bias: float32 [7, 1024], replicated
- grad_ffn_bias: float32 [4096], replicated
- grad_norm_gain: float32 [3, 1024], replicated
- grad_norm_shift: float32 [3, 1024], replicated
Inputs may be any that keep to these rules, and one draw needn't show every extreme that they name: `dec_len`: live decoder positions of an item; in every draw some item has all 1024. `mem_len`: valid memory positions of an item, the first ones; in every draw some item has all 1024.
All inputs are finite; a program needn't handle non-finite values.
Results may differ from a plain program's by a relative error of at most 0.023.
Values may be sent and summed in bfloat16 or wider, within the bound.
A program may use at most 448 MiB of HBM per device.

v0:
```python
import jax
import jax.numpy as jnp
from jax import lax
from jax.sharding import PartitionSpec as P

HEAD_DIM = 64


norm_eps = 1e-05
neg_fill = -1e30


def merged(part, axis, combine):
    gathered = jax.tree.map(lambda a: lax.all_gather(a, axis), part)

    def take(source):
        return jax.tree.map(lambda a: lax.dynamic_index_in_dim(a, source, 0, False), gathered)

    return lax.fori_loop(
        1, lax.axis_size(axis), lambda source, state: combine(state, take(source)), take(0)
    )


def product(left_rows, right_rows):
    return jnp.dot(left_rows, right_rows, preferred_element_type=jnp.float32)


def product_tn(left_rows, right_rows):
    return lax.dot_general(
        left_rows, right_rows, (((0,), (0,)), ((), ())), preferred_element_type=jnp.float32
    )


def product_nt(left_rows, right_rows):
    return lax.dot_general(
        left_rows, right_rows, (((1,), (1,)), ((), ())), preferred_element_type=jnp.float32
    )


def split_heads(matrix):
    return matrix.reshape(matrix.shape[0], matrix.shape[1] // HEAD_DIM, HEAD_DIM)


def normalize(hidden, scale_row, shift_row):
    row_mean = jnp.mean(hidden, axis=-1, keepdims=True)
    centered = hidden - row_mean
    variance = jnp.mean(centered * centered, axis=-1, keepdims=True)
    inverse = lax.rsqrt(variance + norm_eps)
    normed = centered * inverse
    return (normed * scale_row + shift_row, normed, inverse)


def norm_back(grad_rows, normed, inverse, scale_row):
    scaled = grad_rows * scale_row
    grad_hidden = inverse * (
        scaled
        - jnp.mean(scaled, axis=-1, keepdims=True)
        - normed * jnp.mean(scaled * normed, axis=-1, keepdims=True)
    )
    return (grad_hidden, jnp.sum(grad_rows * normed, axis=0), jnp.sum(grad_rows, axis=0))


def softmax_rows(scores, allowed, row_max, row_sum):
    masked = jnp.where(allowed, scores, neg_fill)
    return jnp.where(allowed, jnp.exp(masked - row_max), 0.0) / row_sum


def gelu_exact(values):
    return jax.nn.gelu(values, approximate=False)


def merge_stats(first_pair, second_pair):
    larger = jnp.maximum(first_pair[0], second_pair[0])
    return (
        larger,
        first_pair[1] * jnp.exp(first_pair[0] - larger)
        + second_pair[1] * jnp.exp(second_pair[0] - larger),
    )


def column_sum(matrix):
    return jnp.sum(matrix.astype(jnp.float32), axis=0)


def per_device(
    dec_in,
    memory,
    dec_len,
    mem_len,
    grad_out,
    self_qkv,
    self_out,
    cross_q,
    cross_kv,
    cross_out,
    ffn_in,
    ffn_out,
    proj_bias,
    ffn_bias,
    norm_gain,
    norm_shift,
):
    full_rows = dec_in.shape[1]
    model_width = dec_in.shape[2]
    x_rows = dec_in[0]
    mem_rows = memory[0]
    mem_count = mem_rows.shape[0]
    mem_start = lax.axis_index("mem") * mem_count
    zero_bias = jnp.zeros((model_width,), jnp.float32)
    query_pos = jnp.arange(full_rows, dtype=jnp.int32)
    key_pos = jnp.arange(full_rows, dtype=jnp.int32)
    causal = ((key_pos[None, :] <= query_pos[:, None]) & (key_pos[None, :] < dec_len[0]))[None]
    qkv_rows = product(x_rows, self_qkv) + jnp.concatenate([proj_bias[0], zero_bias, proj_bias[1]])
    q_heads = split_heads((qkv_rows[:, :model_width] * 0.125).astype(jnp.bfloat16))
    key_low = qkv_rows[:, model_width : 2 * model_width].astype(jnp.bfloat16)
    value_low = qkv_rows[:, 2 * model_width :].astype(jnp.bfloat16)
    key_all, value_all = (key_low, value_low)
    k_heads = split_heads(key_all)
    v_heads = split_heads(value_all)
    self_scores = jnp.einsum("rhe,che->hrc", q_heads, k_heads, preferred_element_type=jnp.float32)
    self_max = jnp.max(jnp.where(causal, self_scores, neg_fill), axis=-1, keepdims=True)
    self_sum = jnp.sum(
        jnp.where(causal, jnp.exp(jnp.where(causal, self_scores, neg_fill) - self_max), 0.0),
        axis=-1,
        keepdims=True,
    )
    self_weights = softmax_rows(self_scores, causal, self_max, self_sum)
    attended = (
        jnp.einsum(
            "hrc,che->rhe",
            self_weights.astype(jnp.bfloat16),
            v_heads,
            preferred_element_type=jnp.float32,
        )
        .reshape(full_rows, model_width)
        .astype(jnp.bfloat16)
    )
    first_out, first_norm, first_inv = normalize(
        x_rows.astype(jnp.float32) + product(attended, self_out) + proj_bias[2],
        norm_gain[0],
        norm_shift[0],
    )
    first_low = first_out.astype(jnp.bfloat16)
    cq_heads = split_heads(
        ((product(first_low, cross_q) + proj_bias[3]) * 0.125).astype(jnp.bfloat16)
    )
    block_len = mem_rows.shape[0]
    mem_reach = (mem_start + jnp.arange(block_len, dtype=jnp.int32) < mem_len[0])[None, None, :]
    mem_kv = product(mem_rows, cross_kv) + jnp.concatenate([zero_bias, proj_bias[4]])
    kc_heads = split_heads(mem_kv[:, :model_width].astype(jnp.bfloat16))
    vc_heads = split_heads(mem_kv[:, model_width:].astype(jnp.bfloat16))
    cross_scores = jnp.einsum(
        "rhe,che->hrc", cq_heads, kc_heads, preferred_element_type=jnp.float32
    )
    cross_masked = jnp.where(mem_reach, cross_scores, neg_fill)
    local_max = jnp.max(cross_masked, axis=-1)
    local_sum = jnp.sum(
        jnp.where(mem_reach, jnp.exp(cross_masked - local_max[..., None]), 0.0), axis=-1
    )
    cross_max, cross_sum = merged((local_max, local_sum), "mem", merge_stats)
    cross_weights = softmax_rows(
        cross_scores, mem_reach, cross_max[..., None], cross_sum[..., None]
    )
    cross_low = cross_weights.astype(jnp.bfloat16)
    cross_part = jnp.einsum(
        "hrc,che->rhe", cross_low, vc_heads, preferred_element_type=jnp.float32
    ).reshape(full_rows, model_width)
    crossed = lax.psum(cross_part, "mem")
    crossed_low = crossed.astype(jnp.bfloat16)
    second, second_norm, second_inv = normalize(
        first_out + product(crossed_low, cross_out) + proj_bias[5], norm_gain[1], norm_shift[1]
    )
    second_low = second.astype(jnp.bfloat16)
    hidden_pre = product(second_low, ffn_in) + ffn_bias
    activated = gelu_exact(hidden_pre).astype(jnp.bfloat16)
    third_out, third_norm, third_inv = normalize(
        second + product(activated, ffn_out) + proj_bias[6], norm_gain[2], norm_shift[2]
    )
    out_low = third_out.astype(jnp.bfloat16)
    grad_rows_in = grad_out[0]
    cotangent = jnp.where((query_pos < dec_len[0])[:, None], grad_rows_in.astype(jnp.float32), 0.0)
    grad_third, gain_three, shift_three = norm_back(cotangent, third_norm, third_inv, norm_gain[2])
    ffn_grad = grad_third.astype(jnp.bfloat16)
    grad_hidden = product_nt(ffn_grad, ffn_out)
    hidden_grad = jax.vjp(gelu_exact, hidden_pre)[1](grad_hidden)[0].astype(jnp.bfloat16)
    grad_second, gain_two, shift_two = norm_back(
        grad_third + product_nt(hidden_grad, ffn_in), second_norm, second_inv, norm_gain[1]
    )
    cross_grad = grad_second.astype(jnp.bfloat16)
    crossed_grad = split_heads(product_nt(cross_grad, cross_out).astype(jnp.bfloat16))
    grad_vc = jnp.einsum(
        "hrc,rhe->che", cross_low, crossed_grad, preferred_element_type=jnp.float32
    ).reshape(block_len, model_width)
    grad_cw = jnp.einsum("rhe,che->hrc", crossed_grad, vc_heads, preferred_element_type=jnp.float32)
    delta_part = jnp.sum(cross_weights * grad_cw, axis=-1)
    cross_delta = lax.psum(delta_part, "mem")
    cross_ds = (cross_weights * (grad_cw - cross_delta[..., None])).astype(jnp.bfloat16)
    cq_part = jnp.einsum(
        "hrc,che->rhe", cross_ds, kc_heads, preferred_element_type=jnp.float32
    ).reshape(full_rows, model_width)
    cq_total = lax.psum(cq_part, "mem")
    cq_grad = (cq_total * 0.125).astype(jnp.bfloat16)
    grad_kc = jnp.einsum(
        "hrc,rhe->che", cross_ds, cq_heads, preferred_element_type=jnp.float32
    ).reshape(block_len, model_width)
    kv_full = jnp.concatenate([grad_kc, grad_vc], axis=1)
    own_kv = kv_full.astype(jnp.bfloat16)
    grad_memory = product_nt(own_kv, cross_kv)[None]
    grad_first, gain_one, shift_one = norm_back(
        grad_second + product_nt(cq_grad, cross_q), first_norm, first_inv, norm_gain[0]
    )
    self_grad = grad_first.astype(jnp.bfloat16)
    attended_grad = split_heads(product_nt(self_grad, self_out).astype(jnp.bfloat16))
    scores_again = jnp.einsum("rhe,che->hrc", q_heads, k_heads, preferred_element_type=jnp.float32)
    weights_again = softmax_rows(scores_again, causal, self_max, self_sum)
    grad_v = jnp.einsum(
        "hrc,rhe->che",
        weights_again.astype(jnp.bfloat16),
        attended_grad,
        preferred_element_type=jnp.float32,
    ).reshape(full_rows, model_width)
    grad_sw = jnp.einsum("rhe,che->hrc", attended_grad, v_heads, preferred_element_type=jnp.float32)
    self_ds = (
        weights_again * (grad_sw - jnp.sum(weights_again * grad_sw, axis=-1, keepdims=True))
    ).astype(jnp.bfloat16)
    grad_q = (
        jnp.einsum("hrc,che->rhe", self_ds, k_heads, preferred_element_type=jnp.float32).reshape(
            full_rows, model_width
        )
        * 0.125
    )
    grad_k = jnp.einsum(
        "hrc,rhe->che", self_ds, q_heads, preferred_element_type=jnp.float32
    ).reshape(full_rows, model_width)
    grad_k_own, grad_v_own = (grad_k, grad_v)
    qkv_grad = jnp.concatenate([grad_q, grad_k_own, grad_v_own], axis=1).astype(jnp.bfloat16)
    grad_dec_rows = grad_first + product_nt(qkv_grad, self_qkv)
    layer_out = out_low[None]
    grad_dec = grad_dec_rows[None]
    qkv_weight_grad = product_tn(x_rows, qkv_grad)
    self_out_grad = product_tn(attended, self_grad)
    cross_q_grad = product_tn(first_low, cq_grad)
    cross_kv_grad = product_tn(mem_rows, own_kv)
    cross_out_grad = product_tn(crossed_low, cross_grad)
    ffn_in_grad = product_tn(second_low, hidden_grad)
    ffn_out_grad = product_tn(activated, ffn_grad)
    qkv_sums = column_sum(qkv_grad)
    bias_rest = jnp.stack(
        [
            qkv_sums[:model_width],
            qkv_sums[2 * model_width :],
            column_sum(self_grad),
            column_sum(cq_grad),
            column_sum(cross_grad),
            column_sum(ffn_grad),
        ]
    )
    value_bias = column_sum(own_kv[:, model_width:])
    ffn_bias_grad = column_sum(hidden_grad)
    gain_rows = jnp.stack([gain_one, gain_two, gain_three])
    shift_rows = jnp.stack([shift_one, shift_two, shift_three])
    matrices = (
        lax.psum_scatter(qkv_weight_grad, "dp", scatter_dimension=0, tiled=True),
        lax.psum_scatter(self_out_grad, "dp", scatter_dimension=0, tiled=True),
        lax.psum_scatter(cross_q_grad, "dp", scatter_dimension=0, tiled=True),
        lax.psum_scatter(cross_kv_grad, "dp", scatter_dimension=0, tiled=True),
        lax.psum_scatter(cross_out_grad, "dp", scatter_dimension=0, tiled=True),
        lax.psum_scatter(ffn_in_grad, "dp", scatter_dimension=0, tiled=True),
        lax.psum_scatter(ffn_out_grad, "dp", scatter_dimension=0, tiled=True),
    )
    vectors = lax.psum((bias_rest, ffn_bias_grad, gain_rows, shift_rows, value_bias), "dp")
    kv_total, value_total = (
        lax.psum(matrices[3].astype(jnp.bfloat16), "mem").astype(jnp.float32),
        lax.psum(vectors[4].astype(jnp.bfloat16), "mem").astype(jnp.float32),
    )
    matrices = (
        matrices[0],
        matrices[1],
        matrices[2],
        kv_total,
        matrices[4],
        matrices[5],
        matrices[6],
    )
    vectors = (vectors[0], vectors[1], vectors[2], vectors[3], value_total)
    bias_grad = jnp.concatenate([vectors[0][:4], vectors[4][None], vectors[0][4:]], axis=0)
    return (
        layer_out,
        grad_dec,
        grad_memory,
        matrices[0],
        matrices[1],
        matrices[2],
        matrices[3],
        matrices[4],
        matrices[5],
        matrices[6],
        bias_grad,
        vectors[1],
        vectors[2],
        vectors[3],
    )


def solution(mesh):
    in_specs = (
        P("dp", None, None),
        P("dp", "mem", None),
        P("dp"),
        P("dp"),
        P("dp", None, None),
        P(),
        P(),
        P(),
        P(),
        P(),
        P(),
        P(),
        P(),
        P(),
        P(),
        P(),
    )
    out_specs = (
        P("dp", None, None),
        P("dp", None, None),
        P("dp", "mem", None),
        P("dp", None),
        P("dp", None),
        P("dp", None),
        P("dp", None),
        P("dp", None),
        P("dp", None),
        P("dp", None),
        P(),
        P(),
        P(),
        P(),
    )
    return jax.shard_map(
        per_device, mesh=mesh, in_specs=in_specs, out_specs=out_specs, check_vma=False
    )
```

profile of v0, /device:TPU:0, one launch (start us, length us, event | category | flops | bytes accessed | tf_op | source)
XLA Modules:
  0.0 1810.6 jit_solution(15955320089730400923)
XLA Ops:
  13.2 3.6 fusion.38
  19.3 3.9 copy.73
  23.2 3.9 copy.62
  27.2 12.1 fusion.80
  39.3 2.4 fusion.74
  41.8 4.0 copy.65
  45.7 3.9 copy.63
  49.7 4.1 fusion.20
  53.8 3.9 copy.64
  57.7 35.8 %fusion.81 = (f32[16,1024]{1,0:T(8,128)S(1)}, f32[16,1024,1024]{1,2,0:T(8,128)}) fusion(pred[1024,1024]{0,1:T(8,128)(4,1)S(1)} %fusion.35, bf16[1024,16,64]{0,2,1:T(8,128)(2,1)} %bitcast.166, bf16[1024,16,64]{0,2,1:T(8,128)(2,1)} %bitcast.171), kind=kOutput, calls=%fused_computation.155 | convolution fusion | flops 2214593536 | bytes 72417280 | tf_op jit(solution)/shard_map/sub | solution.py:65
  93.5 24.5 %fusion.42 = bf16[16,64,1024]{2,1,0:T(8,128)(2,1)} fusion(bf16[1024,16,64]{0,2,1:T(8,128)(2,1)} %bitcast.181, f32[16,1024,1024]{1,2,0:T(8,128)} %get-tuple-element.239, f32[16,1024]{1,0:T(8,128)S(1)} %get-tuple-element.238), kind=kOutput, calls=%fused_computation.103 | convolution fusion | flops 2182086656 | bytes 71368704 | tf_op jit(solution)/shard_map/hrc,che->rhe/dot_general | solution.py:129
  118.1 4.3 fusion.82
  124.3 4.0 multiply_convert_fusion.5
  128.3 4.0 copy.69
  132.4 8.9 select_reduce_fusion.2
  141.2 7.2 all-gather
  148.4 9.6 select_reduce_fusion.1
  158.0 5.9 all-gather.1
  164.2 10.4 fusion.33
  174.6 77.7 %all-reduce.13 = bf16[1024,1024]{0,1:T(8,128)(2,1)} all-reduce(f32[1024,1024]{0,1:T(8,128)} %bitcast.178), channel_id=1, replica_groups=mesh['dp'=8,'mem'=4] {'mem'}, use_global_device_ids=true, to_apply=%region_8.9 | all-reduce | flops 1048576 | bytes 6291456 | tf_op jit(solution)/shard_map/psum | solution.py:168
  252.3 6.5 fusion.83
  260.9 47.8 %multiply_convert_fusion.2 = (bf16[1024,4096]{1,0:T(8,128)(2,1)}, f32[1024,4096]{1,0:T(8,128)}, f32[1024,4096]{1,0:T(8,128)}) fusion(f32[4096]{0:T(1024)S(1)} %copy-done.76, bf16[1024,4096]{1,0:T(8,128)(2,1)} %param.28, bf16[1024,1024]{0,1:T(8,128)(2,1)S(1)} %fusion.69.clone.4), kind=kOutput, calls=%fused_computation.20 | convolution fusion | flops 8866758656 | bytes 52445184 | tf_op jit(solution)/shard_map/dot_general | solution.py:25
  308.7 16.6 fusion.84
  325.3 2.8 multiply_reduce_fusion.6
  328.7 3.0 fusion.30
  331.7 4.3 convert_reduce_fusion.2
  335.9 24.7 %convert_reduce_fusion = (f32[4096]{0:T(1024)}, bf16[1024,4096]{1,0:T(8,128)(2,1)}) fusion(f32[1024,4096]{1,0:T(8,128)} %get-tuple-element.215, f32[1024,4096]{1,0:T(8,128)} %get-tuple-element.246, f32[4096]{0:T(1024)S(1)} %copy-done.76, bf16[1024,1024]{0,1:T(8,128)(2,1)} %get-tuple-element.209, bf16[4096,1024]{1,0:T(8,128)(2,1)} %param.29), kind=kOutput, calls=%fused_computation.16 | convolution fusion | flops 8661233664 | bytes 52461568 | tf_op jit(solution)/shard_map/dot_general | solution.py:35
  360.7 18.4 %multiply_reduce_fusion.2 = (f32[1024]{0:T(1024)}, f32[1024]{0:T(1024)S(1)}, f32[1024]{0:T(1024)S(1)}, f32[1024]{0:T(1024)}, f32[1024,1024]{0,1:T(8,128)S(1)}) fusion(f32[1024,1024]{0,1:T(8,128)S(1)} %copy-done.4, f32[1024]{0:T(1024)S(1)} %add_rsqrt_fusion.1, f32[1024]{0:T(1024)S(1)} %broadcast_multiply_fusion.7, f32[1024]{0:T(1024)S(1)} %bitcast.194, ...), kind=kOutput, calls=%fused_computation.60 | convolution fusion | flops 8609853440 | bytes 31507456 | tf_op jit(solution)/shard_map/dot_general | solution.py:35
  381.2 2.4 convolution_convert_fusion.2
  383.6 14.5 multiply_reduce_fusion.1
  398.3 31.9 %all-reduce.8.cloned.1.call-done = f32[16,1024]{1,0:T(8,128)} async-done(((f32[16,1024]{1,0:T(8,128)}), f32[16,1024]{1,0:T(8,128)}) %all-reduce.8.cloned.1.call-update) | async-done | bytes 65552 | tf_op jit(solution)/shard_map/psum | solution.py:196
  430.2 12.4 multiply_convert_fusion.1
  442.6 4.0 fusion.85
  447.0 5.3 copy.76
  452.4 9.6 fusion.48
  462.1 6.3 convolution_convert_fusion.3
  469.2 4.5 convolution_bitcast_fusion.1
  473.8 64.2 %all-reduce.10.cloned.1.call-done = f32[1024,1024]{1,0:T(8,128)} async-done(((f32[1024,1024]{1,0:T(8,128)}), f32[1024,1024]{1,0:T(8,128)}) %all-reduce.10.cloned.1.call-update) | async-done | bytes 4194320 | tf_op jit(solution)/shard_map/psum | solution.py:201
  538.0 8.2 multiply_reduce_fusion.3
  551.5 43.5 %multiply_reduce_fusion = (f32[16,1024]{1,0:T(8,128)S(1)}, f32[16,1024,1024]{1,2,0:T(8,128)}) fusion(f32[16,1024,1024]{1,2,0:T(8,128)} %get-tuple-element.239, f32[16,1024]{1,0:T(8,128)S(1)} %copy-done.33, bf16[1024,16,64]{0,2,1:T(8,128)(2,1)S(1)} %bitcast.235, bf16[1024,16,64]{0,2,1:T(8,128)(2,1)S(1)} %bitcast.182), kind=kOutput, calls=%fused_computation.7 | convolution fusion | flops 2197798912 | bytes 138543104 | tf_op jit(solution)/shard_map/rhe,che->hrc/dot_general | solution.py:222
  595.0 54.7 %multiply_convert_fusion = bf16[16,1024,1024]{1,2,0:T(8,128)(2,1)} fusion(f32[16,1024,1024]{1,2,0:T(8,128)} %get-tuple-element.254, f32[16,1024]{1,0:T(8,128)S(1)} %get-tuple-element.253, f32[16,1024,1024]{1,2,0:T(8,128)} %get-tuple-element.239, f32[16,1024]{1,0:T(8,128)S(1)} %copy-done.33), kind=kLoop, calls=%fused_computation.6 | loop fusion | flops 67108864 | bytes 167903232 | tf_op jit(solution)/shard_map/convert_element_type | solution.py:225
  649.7 17.6 convolution_convert_fusion
  667.3 18.7 %multiply_convert_fusion.3 = bf16[16,64,1024]{2,1,0:T(8,128)(2,1)} fusion(bf16[1024,16,64]{0,2,1:T(8,128)(2,1)} %bitcast.172, bf16[16,1024,1024]{1,2,0:T(8,128)(2,1)} %multiply_convert_fusion), kind=kOutput, calls=%fused_computation.67 | convolution fusion | flops 2149580800 | bytes 37748736 | tf_op jit(solution)/shard_map/hrc,che->rhe/dot_general | solution.py:227
  686.1 25.3 %fusion.45 = bf16[16,64,1024]{2,1,0:T(8,128)(2,1)} fusion(bf16[1024,16,64]{0,2,1:T(8,128)(2,1)} %bitcast.236, f32[16,1024,1024]{1,2,0:T(8,128)} %get-tuple-element.239, f32[16,1024]{1,0:T(8,128)S(1)} %copy-done.33), kind=kOutput, calls=%fused_computation.104 | convolution fusion | flops 2182086656 | bytes 71368704 | tf_op jit(solution)/shard_map/hrc,rhe->che/dot_general | solution.py:216
  713.5 13.7 convolution_bitcast_fusion
  727.4 7.3 fusion.51
  735.4 7.9 fusion.65
  743.4 7.1 fusion.59
  751.2 16.6 fusion.66
  768.2 16.3 fusion.86
  785.7 4.0 copy.84
  789.7 4.6 convolution_bitcast_fusion.2
  794.4 4.6 convert_reduce_fusion.1
  799.6 41.7 %all-reduce.14 = (f32[6,1024]{1,0:T(8,128)S(1)}, bf16[1024]{0:T(1024)(128)(2,1)S(1)}, f32[4096]{0:T(1024)}, f32[3,1024]{1,0:T(4,128)}, f32[3,1024]{1,0:T(4,128)}) all-reduce(f32[6,1024]{1,0:T(8,128)S(1)} %stack.51, f32[1024]{0:T(1024)S(1)} %convert_reduce_fusion.6, f32[4096]{0:T(1024)S(1)} %copy-done.58, ...), channel_id=1, replica_groups=mesh['dp'=8,'mem'=4] {'dp'}, use_global_device_ids=true, to_apply=%region_36.37 | all-reduce | flops 17408 | bytes 137216 | tf_op jit(solution)/shard_map/psum | solution.py:271
  841.3 12.4 add_bitcast_fusion
  853.7 5.5 copy.85
  859.3 6.1 psum.76
  868.2 91.5 %reduce-scatter.8.cloned.1.call-done = f32[128,3072]{0,1:T(8,128)} async-done(((f32[1024,3072]{0,1:T(8,128)}), f32[128,3072]{0,1:T(8,128)}) %reduce-scatter.8.cloned.1.call-update) | async-done | bytes 1572880 | tf_op jit(solution)/shard_map/reduce_scatter | solution.py:263
  959.7 3.0 copy.86
  962.8 88.5 %reduce-scatter.16.cloned.1.call-done = f32[128,1024]{1,0:T(8,128)} async-done(((f32[1024,1024]{1,0:T(8,128)}), f32[128,1024]{1,0:T(8,128)}) %reduce-scatter.16.cloned.1.call-update) | async-done | bytes 524304 | tf_op jit(solution)/shard_map/reduce_scatter | solution.py:267
  1051.3 92.2 %reduce-scatter.12.cloned.1.call-done = f32[128,1024]{1,0:T(8,128)} async-done(((f32[1024,1024]{1,0:T(8,128)}), f32[128,1024]{1,0:T(8,128)}) %reduce-scatter.12.cloned.1.call-update) | async-done | bytes 524304 | tf_op jit(solution)/shard_map/reduce_scatter | solution.py:265
  1143.5 92.2 %reduce-scatter.10.cloned.1.call-done = f32[128,1024]{1,0:T(8,128)} async-done(((f32[1024,1024]{1,0:T(8,128)}), f32[128,1024]{1,0:T(8,128)}) %reduce-scatter.10.cloned.1.call-update) | async-done | bytes 524304 | tf_op jit(solution)/shard_map/reduce_scatter | solution.py:264
  1235.7 284.2 %reduce-scatter.18.cloned.1.call-done = f32[128,4096]{1,0:T(8,128)} async-done(((f32[1024,4096]{1,0:T(8,128)}), f32[128,4096]{1,0:T(8,128)}) %reduce-scatter.18.cloned.1.call-update) | async-done | bytes 2097168 | tf_op jit(solution)/shard_map/reduce_scatter | solution.py:268
  1520.0 283.5 %reduce-scatter.20.cloned.1.call-done = f32[512,1024]{1,0:T(8,128)} async-done(((f32[4096,1024]{1,0:T(8,128)}), f32[512,1024]{1,0:T(8,128)}) %reduce-scatter.20.cloned.1.call-update) | async-done | bytes 2097168 | tf_op jit(solution)/shard_map/reduce_scatter | solution.py:269
  (228 shorter events, 29.4 us)
Async XLA Ops:
  7.2 117.1 %copy-start = (bf16[1024,1024]{1,0:T(8,128)(2,1)S(1)}, bf16[1024,1024]{1,0:T(8,128)(2,1)}, u32[]{:S(2)}) copy-start(bf16[1024,1024]{1,0:T(8,128)(2,1)} %param.25) | copy-start | bytes 6291460
  7.2 423.0 %all-reduce.8.cloned.1.call-start = ((), (), s32[]{:S(2)}) async-start(), calls=%async_computation.7 | async-start | bytes 131072 | tf_op jit(solution)/shard_map/psum | solution.py:196
  8.7 10.3 copy-start.59
  93.5 24.5 %copy-start.32 = (f32[16,1024]{1,0:T(8,128)}, f32[16,1024]{1,0:T(8,128)S(1)}, u32[]{:S(2)}) copy-start(f32[16,1024]{1,0:T(8,128)S(1)} %get-tuple-element.238) | copy-start | bytes 196612
  93.5 24.5 %copy-start.26 = (bf16[1,1024,1024]{1,2,0:T(8,128)(2,1)S(1)}, bf16[1,1024,1024]{1,2,0:T(8,128)(2,1)}, u32[]{:S(2)}) copy-start(bf16[1,1024,1024]{1,2,0:T(8,128)(2,1)} %copy.62) | copy-start | bytes 6291460
  93.5 24.5 %copy-start.66 = (f32[1,1024]{1,0:T(1,128)S(1)}, f32[1,1024]{1,0:T(1,128)}, u32[]{:S(2)}) copy-start(f32[1,1024]{1,0:T(1,128)} %get-tuple-element.224) | copy-start | bytes 12292
  93.5 24.5 %copy-start.74 = (bf16[1024,1024]{1,0:T(8,128)(2,1)S(1)}, bf16[1024,1024]{1,0:T(8,128)(2,1)}, u32[]{:S(2)}) copy-start(bf16[1024,1024]{1,0:T(8,128)(2,1)} %param.24) | copy-start | bytes 6291460
  122.4 129.9 %copy-start.41 = (f32[1024]{0:T(1024)}, f32[1024]{0:T(1024)S(1)}, u32[]{:S(2)}) copy-start(f32[1024]{0:T(1024)S(1)} %broadcast_multiply_fusion.8) | copy-start | bytes 12292
  122.9 129.4 %copy-start.49 = (f32[1024]{0:T(1024)}, f32[1024]{0:T(1024)S(1)}, u32[]{:S(2)}) copy-start(f32[1024]{0:T(1024)S(1)} %add_rsqrt_fusion.2) | copy-start | bytes 12292
  128.3 4.0 copy-start.13
  132.3 31.8 %copy-start.61 = (pred[256]{0:T(512)(128)(4,1)}, pred[256]{0:T(512)(128)(4,1)S(1)}, u32[]{:S(2)}) copy-start(pred[256]{0:T(512)(128)(4,1)S(1)} %add_compare_fusion) | copy-start | bytes 772
  148.4 15.7 copy-start.30
  164.1 10.5 copy-start.18
  164.1 10.5 copy-start.20
  174.6 77.7 %copy-start.64 = (f32[1,1024]{1,0:T(1,128)S(1)}, f32[1,1024]{1,0:T(1,128)}, u32[]{:S(2)}) copy-start(f32[1,1024]{1,0:T(1,128)} %get-tuple-element.227) | copy-start | bytes 12292
  258.9 120.2 %copy-start.34 = (f32[1024]{0:T(1024)}, f32[1024]{0:T(1024)S(1)}, u32[]{:S(2)}) copy-start(f32[1024]{0:T(1024)S(1)} %broadcast_multiply_fusion.7) | copy-start | bytes 12292
  259.4 119.7 %copy-start.36 = (f32[1024]{0:T(1024)}, f32[1024]{0:T(1024)S(1)}, u32[]{:S(2)}) copy-start(f32[1024]{0:T(1024)S(1)} %add_rsqrt_fusion.1) | copy-start | bytes 12292
  260.9 47.8 %copy-start.63 = (f32[1,1024]{1,0:T(1,128)S(1)}, f32[1,1024]{1,0:T(1,128)}, u32[]{:S(2)}) copy-start(f32[1,1024]{1,0:T(1,128)} %get-tuple-element.221) | copy-start | bytes 12292
  308.7 19.4 %copy-start.6 = (bf16[1,1024,1024]{1,2,0:T(8,128)(2,1)S(1)}, bf16[1,1024,1024]{1,2,0:T(8,128)(2,1)}, u32[]{:S(2)}) copy-start(bf16[1,1024,1024]{1,2,0:T(8,128)(2,1)} %copy.73) | copy-start | bytes 6291460
  325.3 3.4 copy-start.5
  325.3 3.4 copy-start.40
  325.3 3.5 copy-start.60
  328.1 3.6 copy-start.57
  335.9 24.7 %copy-start.4 = (f32[1024,1024]{0,1:T(8,128)S(1)}, f32[1024,1024]{0,1:T(8,128)}, u32[]{:S(2)}) copy-start(f32[1024,1024]{0,1:T(8,128)} %copy-done.3) | copy-start | bytes 12582916
  381.2 2.5 copy-start.31
  383.6 14.6 copy-start.77
  398.2 139.8 %all-reduce.10.cloned.1.call-start = ((), (), s32[]{:S(2)}) async-start(), calls=%async_computation.8 | async-start | bytes 8388608 | tf_op jit(solution)/shard_map/psum | solution.py:201
  430.2 12.4 copy-start.14
  442.5 4.5 copy-start.2
  452.4 259.0 %reduce-scatter.14.cloned.1.call-start = ((), (), s32[]{:S(2)}) async-start(), calls=%async_computation.12 | async-start | bytes 9437184 | tf_op jit(solution)/shard_map/reduce_scatter | solution.py:266
  452.4 9.6 copy-start.7
  462.1 6.4 copy-start.22
  462.1 7.1 copy-start.29
  473.7 64.3 %copy-start.42 = (f32[1024]{0:T(1024)S(1)}, f32[1024]{0:T(1024)}, u32[]{:S(2)}) copy-start(f32[1024]{0:T(1024)} %copy-done.41) | copy-start | bytes 12292
  473.7 64.3 %copy-start.50 = (f32[1024]{0:T(1024)S(1)}, f32[1024]{0:T(1024)}, u32[]{:S(2)}) copy-start(f32[1024]{0:T(1024)} %copy-done.49) | copy-start | bytes 12292
  473.7 64.3 %copy-start.55 = (f32[1,1024]{1,0:T(1,128)S(1)}, f32[1,1024]{1,0:T(1,128)}, u32[]{:S(2)}) copy-start(f32[1,1024]{1,0:T(1,128)} %get-tuple-element.229) | copy-start | bytes 12292
  473.7 392.2 %all-reduce.12.cloned.1.call-start = ((), (), s32[]{:S(2)}) async-start(), calls=%async_computation.13 | async-start | bytes 1048576 | tf_op jit(solution)/shard_map/psum | solution.py:273
  538.0 8.3 copy-start.9
  548.3 3.2 copy-start.24
  548.3 3.2 copy-start.33
  550.7 44.3 %copy-start.78 = (bf16[1024,1024]{0,1:T(8,128)(2,1)}, bf16[1024,1024]{0,1:T(8,128)(2,1)S(1)}, u32[]{:S(2)}) copy-start(bf16[1024,1024]{0,1:T(8,128)(2,1)S(1)} %convolution_convert_fusion.1) | copy-start | bytes 6291460
  595.0 54.8 %copy-start.10 = (bf16[1024,1024]{0,1:T(8,128)(2,1)S(1)}, bf16[1024,1024]{0,1:T(8,128)(2,1)}, u32[]{:S(2)}) copy-start(bf16[1024,1024]{0,1:T(8,128)(2,1)} %copy.64) | copy-start | bytes 6291460
  686.1 27.4 %copy-start.11 = (bf16[16,64,1024]{2,1,0:T(8,128)(2,1)S(1)}, bf16[16,64,1024]{2,1,0:T(8,128)(2,1)}, u32[]{:S(2)}) copy-start(bf16[16,64,1024]{2,1,0:T(8,128)(2,1)} %convolution_convert_fusion) | copy-start | bytes 6291460
  713.4 246.3 %reduce-scatter.8.cloned.1.call-start = ((), (), s32[]{:S(2)}) async-start(), calls=%async_computation.9 | async-start | bytes 14155776 | tf_op jit(solution)/shard_map/reduce_scatter | solution.py:263
  727.2 324.1 %reduce-scatter.16.cloned.1.call-start = ((), (), s32[]{:S(2)}) async-start(), calls=%async_computation.14 | async-start | bytes 4718592 | tf_op jit(solution)/shard_map/reduce_scatter | solution.py:267
  734.7 408.8 %reduce-scatter.12.cloned.1.call-start = ((), (), s32[]{:S(2)}) async-start(), calls=%async_computation.11 | async-start | bytes 4718592 | tf_op jit(solution)/shard_map/reduce_scatter | solution.py:265
  743.4 492.4 %reduce-scatter.10.cloned.1.call-start = ((), (), s32[]{:S(2)}) async-start(), calls=%async_computation.10 | async-start | bytes 4718592 | tf_op jit(solution)/shard_map/reduce_scatter | solution.py:264
  750.6 769.4 %reduce-scatter.18.cloned.1.call-start = ((), (), s32[]{:S(2)}) async-start(), calls=%async_computation.15 | async-start | bytes 18874368 | tf_op jit(solution)/shard_map/reduce_scatter | solution.py:268
  767.9 1035.6 %reduce-scatter.20.cloned.1.call-start = ((), (), s32[]{:S(2)}) async-start(), calls=%async_computation.16 | async-start | bytes 18874368 | tf_op jit(solution)/shard_map/reduce_scatter | solution.py:269
  785.5 4.2 copy-start.28
  789.7 4.6 copy-start.12
  789.7 4.6 copy-start.25
  794.3 4.7 copy-start.15
  794.3 5.1 copy-start.44
  794.3 5.0 copy-start.45
  794.3 5.0 copy-start.46
  794.3 5.1 copy-start.48
  794.4 5.1 copy-start.68
  794.4 5.1 copy-start.70
  794.4 5.1 copy-start.47
  794.4 5.1 copy-start.67
  794.4 5.1 copy-start.69
  794.4 5.1 copy-start.58
  853.7 949.8 %copy-start.1 = (bf16[1024,1024]{1,0:T(8,128)(2,1)S(1)}, bf16[1024,1024]{1,0:T(8,128)(2,1)}, u32[]{:S(2)}) copy-start(bf16[1024,1024]{1,0:T(8,128)(2,1)} %param.25) | copy-start | bytes 6291460
  (25 other events, 36.1 us)
Sparse Core Ops, SparseCore 0:
  398.3 31.7 all-reduce.7
  452.5 85.4 all-reduce.9
  541.7 147.9 reduce-scatter.13
  713.6 33.1 all-reduce.11
  750.2 209.4 reduce-scatter.7
  963.8 87.4 reduce-scatter.15
  1055.5 87.9 reduce-scatter.11
  1147.7 87.9 reduce-scatter.9
  1240.1 279.8 reduce-scatter.17
  1524.2 279.2 reduce-scatter.19
where the time goes:
time: 1820 us; the launch traced here: 1810 us
  waiting for transfers between devices  1030 us (57%)
  matrix products  461 us (25%)
  blocking collectives  139 us (8%)
  other arithmetic  105 us (6%)
  local copies, waits for them, and re-layouts  60.3 us (3%)
    reduce_scatter x1, waiting for transfers between devices, per_device(): lax.psum_scatter(ffn_in_grad, 'dp', scatter_dimension=0, tiled=True)  284 us
    reduce_scatter x1, waiting for transfers between devices, per_device(): lax.psum_scatter(ffn_out_grad, 'dp', scatter_dimension=0, tiled=True)  284 us
    dot_general x7, matrix products, product(): return jnp.dot(left_rows, right_rows, preferred_element_type=jnp.float32)  94.9 us
    reduce_scatter x1, waiting for transfers between devices, per_device(): lax.psum_scatter(self_out_grad, 'dp', scatter_dimension=0, tiled=True)  92.2 us
    reduce_scatter x1, waiting for transfers between devices, per_device(): lax.psum_scatter(cross_q_grad, 'dp', scatter_dimension=0, tiled=True)  92.2 us
    reduce_scatter x1, waiting for transfers between devices, per_device(): lax.psum_scatter(qkv_weight_grad, 'dp', scatter_dimension=0, tiled=True)  91.5 us
    reduce_scatter x1, waiting for transfers between devices, per_device(): lax.psum_scatter(cross_out_grad, 'dp', scatter_dimension=0, tiled=True)  88.5 us
    psum x1, blocking collectives, per_device(): crossed = lax.psum(cross_part, 'mem')  77.7 us
  transfers between devices with their start and end apart: 10, of which 8 were waited for; matrix products, arithmetic and copies ran while one was open for 17% of the time, Pallas kernels for 0%

commit v1 on v0

v1 whole, which is shorter than its diff:
```python
import functools

import jax
import jax.numpy as jnp
from jax import lax
from jax.experimental import pallas as pl
from jax.experimental.pallas import tpu as pltpu
from jax.sharding import PartitionSpec as P

HEAD_DIM = 64
norm_eps = 1e-05
neg_fill = -1e30
low = jnp.bfloat16
VMEM_LIMIT = 56 * 1024 * 1024


def product(left_rows, right_rows):
    return jnp.dot(left_rows, right_rows, preferred_element_type=jnp.float32)


def product_tn(left_rows, right_rows):
    return lax.dot_general(
        left_rows, right_rows, (((0,), (0,)), ((), ())), preferred_element_type=jnp.float32
    )


def product_nt(left_rows, right_rows):
    return lax.dot_general(
        left_rows, right_rows, (((1,), (1,)), ((), ())), preferred_element_type=jnp.float32
    )


def normalize(hidden, scale_row, shift_row):
    row_mean = jnp.mean(hidden, axis=-1, keepdims=True)
    centered = hidden - row_mean
    variance = jnp.mean(centered * centered, axis=-1, keepdims=True)
    inverse = lax.rsqrt(variance + norm_eps)
    normed = centered * inverse
    return (normed * scale_row + shift_row, normed, inverse)


def norm_back(grad_rows, normed, inverse, scale_row):
    scaled = grad_rows * scale_row
    grad_hidden = inverse * (
        scaled
        - jnp.mean(scaled, axis=-1, keepdims=True)
        - normed * jnp.mean(scaled * normed, axis=-1, keepdims=True)
    )
    return (grad_hidden, jnp.sum(grad_rows * normed, axis=0), jnp.sum(grad_rows, axis=0))


def gelu_parts(values):
    cdf = 0.5 * (1.0 + lax.erf(values * 0.7071067811865476))
    density = jnp.exp(-0.5 * values * values) * 0.3989422804014327
    return values * cdf, cdf + values * density


def column_sum(matrix):
    return jnp.sum(matrix.astype(jnp.float32), axis=0)


def lane_head(rows):
    return lax.broadcasted_iota(jnp.int32, (rows, 128), 1) // HEAD_DIM


def pick_head(pair, h):
    return jnp.where(lane_head(pair.shape[0]) == h, pair, jnp.zeros_like(pair))


def self_fwd_kernel(info, q_ref, k_ref, v_ref, o_ref):
    rows = k_ref.shape[0]
    block = rows // 4
    dec_len = info[1]

    def process(qb, slot):
        keys = (qb + 1) * block
        kk, vv = k_ref[:keys, :], v_ref[:keys, :]
        qq = q_ref[qb * block : (qb + 1) * block, :]
        total = None
        for h in range(2):
            s = product_nt(pick_head(qq, h), kk)
            col = lax.broadcasted_iota(jnp.int32, s.shape, 1)
            row = lax.broadcasted_iota(jnp.int32, s.shape, 0) + qb * block
            s = jnp.where((col <= row) & (col < dec_len), s, neg_fill)
            p = jnp.exp(s - jnp.max(s, axis=1, keepdims=True))
            inv = 1.0 / jnp.sum(p, axis=1, keepdims=True)
            part = product(p.astype(low), pick_head(vv, h)) * inv
            total = part if total is None else total + part
        o_ref[slot * block : (slot + 1) * block, :] = total.astype(low)

    @pl.when(info[0] == 0)
    def _():
        process(0, 0)
        process(3, 1)

    @pl.when(info[0] == 1)
    def _():
        process(1, 0)
        process(2, 1)


def self_forward(info, q, k, v):
    rows, width = q.shape
    pairs = width // 128
    spec = pl.BlockSpec((rows, 128), lambda i, s: (0, i))
    return pl.pallas_call(
        self_fwd_kernel,
        out_shape=jax.ShapeDtypeStruct((rows // 2, width), low),
        grid_spec=pltpu.PrefetchScalarGridSpec(
            num_scalar_prefetch=1,
            grid=(pairs,),
            in_specs=[spec, spec, spec],
            out_specs=pl.BlockSpec((rows // 2, 128), lambda i, s: (0, i)),
        ),
        compiler_params=pltpu.CompilerParams(vmem_limit_bytes=VMEM_LIMIT),
        cost_estimate=pl.CostEstimate(
            flops=6 * rows * rows * width, bytes_accessed=8 * rows * width, transcendentals=rows * rows * 3
        ),
        name="self_forward",
    )(info, q, k, v)


def cross_fwd_kernel(q_ref, k_ref, v_ref, bias_ref, o_ref):
    block = 256
    for r in range(q_ref.shape[0] // block):
        qq = q_ref[r * block : (r + 1) * block, :]
        total = None
        for h in range(2):
            s = product_nt(pick_head(qq, h), k_ref[...]) + bias_ref[...]
            p = jnp.exp(s - jnp.max(s, axis=1, keepdims=True))
            inv = 1.0 / jnp.sum(p, axis=1, keepdims=True)
            part = product(p.astype(low), pick_head(v_ref[...], h)) * inv
            total = part if total is None else total + part
        o_ref[r * block : (r + 1) * block, :] = total.astype(low)


def cross_forward(q, k, v, bias_row):
    rows, width = q.shape
    keys = k.shape[0]
    return pl.pallas_call(
        cross_fwd_kernel,
        out_shape=jax.ShapeDtypeStruct((rows, width), low),
        grid=(width // 128,),
        in_specs=[
            pl.BlockSpec((rows, 128), lambda i: (0, i)),
            pl.BlockSpec((keys, 128), lambda i: (0, i)),
            pl.BlockSpec((keys, 128), lambda i: (0, i)),
            pl.BlockSpec((1, keys), lambda i: (0, 0)),
        ],
        out_specs=pl.BlockSpec((rows, 128), lambda i: (0, i)),
        compiler_params=pltpu.CompilerParams(vmem_limit_bytes=VMEM_LIMIT),
        cost_estimate=pl.CostEstimate(
            flops=16 * rows * keys * width, bytes_accessed=8 * rows * width, transcendentals=rows * keys * 8
        ),
        name="cross_forward",
    )(q, k, v, bias_row)


def back_kernel(info, q_ref, k_ref, v_ref, g0_ref, g1_ref, g2_ref, g3_ref, bias_ref, dq_ref, dk_ref, dv_ref, dk_acc, dv_acc, *, causal):
    rows = q_ref.shape[0]
    keys_all = k_ref.shape[0]
    block = rows // 4
    k_t = k_ref[...].T
    dk_acc[...] = jnp.zeros_like(dk_acc)
    dv_acc[...] = jnp.zeros_like(dv_acc)
    for qb in range(4):
        keys = (qb + 1) * block if causal else keys_all
        kk, vv = k_ref[:keys, :], v_ref[:keys, :]
        qq = q_ref[qb * block : (qb + 1) * block, :]
        gg = (g0_ref, g1_ref, g2_ref, g3_ref)[qb][...]
        q_parts = []
        for h in range(2):
            q_h, g_h = pick_head(qq, h), pick_head(gg, h)
            s = product_nt(kk, q_h)
            if causal:
                key = lax.broadcasted_iota(jnp.int32, s.shape, 0)
                row = lax.broadcasted_iota(jnp.int32, s.shape, 1) + qb * block
                s = jnp.where((key <= row) & (key < info[1]), s, neg_fill)
            else:
                s = s + jnp.concatenate([bias_ref[...]] * (block // 128), axis=1)
            p = jnp.exp(s - jnp.max(s, axis=0, keepdims=True))
            p = p * (1.0 / jnp.sum(p, axis=0, keepdims=True))
            dp = product_nt(vv, g_h)
            e = jnp.sum(p * dp, axis=0, keepdims=True)
            ds = (p * (dp - e)).astype(low)
            dv_acc[:keys, :] += product(p.astype(low), g_h)
            dk_acc[:keys, :] += product(ds, q_h)
            q_parts.append(product(k_t[h * HEAD_DIM : (h + 1) * HEAD_DIM, :keys], ds))
        dq_t = jnp.concatenate(q_parts, axis=0) * 0.125
        dq_ref[qb * block : (qb + 1) * block, :] = dq_t.T.astype(low)
    dk_ref[...] = dk_acc[...].astype(low)
    dv_ref[...] = dv_acc[...].astype(low)


def attention_back(info, q, k, v, g, bias, causal):
    rows, width = q.shape
    keys = k.shape[0]
    own = pl.BlockSpec((rows, 128), lambda i, s: (0, i))
    wide = pl.BlockSpec((keys, 128), lambda i, s: (0, s[0] + i))
    mine = pl.BlockSpec((keys, 128), lambda i, s: (0, i))

    def g_block(n):
        return pl.BlockSpec((rows // 4, 128), lambda i, s: (s[2 + n] if causal else n, i))

    q_spec = wide if q.shape[1] == k.shape[1] else own
    width = g.shape[1]
    return pl.pallas_call(
        functools.partial(back_kernel, causal=causal),
        out_shape=[
            jax.ShapeDtypeStruct((rows, width), low),
            jax.ShapeDtypeStruct((keys, width), low),
            jax.ShapeDtypeStruct((keys, width), low),
        ],
        grid_spec=pltpu.PrefetchScalarGridSpec(
            num_scalar_prefetch=1,
            grid=(width // 128,),
            in_specs=[q_spec, wide, wide] + [g_block(n) for n in range(4)] + [pl.BlockSpec(bias.shape, lambda i, s: (0, 0))],
            out_specs=[own, mine, mine],
            scratch_shapes=[pltpu.VMEM((keys, 128), jnp.float32), pltpu.VMEM((keys, 128), jnp.float32)],
        ),
        compiler_params=pltpu.CompilerParams(vmem_limit_bytes=VMEM_LIMIT),
        cost_estimate=pl.CostEstimate(
            flops=40 * rows * keys * width // (2 if causal else 1),
            bytes_accessed=14 * rows * width,
            transcendentals=rows * keys * 4,
        ),
        name="self_back" if causal else "cross_back",
    )(info, q, k, v, g, g, g, g, bias)


def swap(part, axis, distance):
    count = lax.axis_size(axis)
    return lax.ppermute(part, axis, [(i, i ^ distance) for i in range(count)])


def gather_rel(part):
    core = swap(part, "mem", 1)
    across = swap(part, "mem", 2)
    return [part, core, across, swap(across, "mem", 1)]


def scatter_dp(parts):
    count = lax.axis_size("dp")
    me = lax.axis_index("dp")
    kept = [a.reshape(count, a.shape[0] // count, a.shape[1]) for a in parts]
    widths = [a.shape[1] for a in parts]
    distance = 1
    while count > 1:
        bit = (me // distance) % 2
        halves = [a.reshape(count // 2, 2, a.shape[1], a.shape[2]) for a in kept]
        mine = [lax.dynamic_index_in_dim(a, bit, 1, False) for a in halves]
        theirs = [lax.dynamic_index_in_dim(a, 1 - bit, 1, False).astype(low) for a in halves]
        got = swap(jnp.concatenate(theirs, axis=2), "dp", distance)
        start, kept = 0, []
        for a, w in zip(mine, widths):
            kept.append(a + got[:, :, start : start + w].astype(jnp.float32))
            start += w
        count, distance = count // 2, distance * 2
    return [a[0] for a in kept]


def sum_all(vector):
    for axis in ("mem", "dp"):
        distance = 1
        while distance < lax.axis_size(axis):
            vector = vector + swap(vector, axis, distance)
            distance *= 2
    return vector


def per_device(
    dec_in,
    memory,
    dec_len,
    mem_len,
    grad_out,
    self_qkv,
    self_out,
    cross_q,
    cross_kv,
    cross_out,
    ffn_in,
    ffn_out,
    proj_bias,
    ffn_bias,
    norm_gain,
    norm_shift,
):
    x_full = dec_in[0]
    rows, width = x_full.shape
    hidden = ffn_in.shape[1]
    block = rows // 4
    half, quarter = width // 2, width // 4
    groups = lax.axis_size("dp")
    mem_rows = memory[0]
    mem_block = mem_rows.shape[0]
    me = lax.axis_index("mem")
    chip, core = me // 2, me % 2
    quart = 2 * core + chip

    def block_of(m):
        return jnp.where(m // 2 == 0, 3 * (m % 2), 1 + m % 2)

    def columns_half(w, count):
        piece = w.reshape(w.shape[0], count, 2, half)
        return lax.dynamic_index_in_dim(piece, core, 2, False).reshape(w.shape[0], count * half)

    def columns_quarter(w, count):
        piece = w.reshape(w.shape[0], count, 4, quarter)
        return lax.dynamic_index_in_dim(piece, quart, 2, False).reshape(w.shape[0], count * quarter)

    def own_rows(a):
        return lax.dynamic_slice_in_dim(a, block_of(me) * block, block, 0)

    def by_block(slots):
        stacked = jnp.stack(slots)
        order = [0, 2, 3, 1]
        return jnp.concatenate(
            [lax.dynamic_index_in_dim(stacked, me ^ order[n], 0, False) for n in range(4)], axis=0
        )

    def by_quarter(slots):
        stacked = jnp.stack(slots)
        order = [0, 2, 1, 3]
        return [lax.dynamic_index_in_dim(stacked, me ^ order[n], 0, False) for n in range(4)]

    mem_full = jnp.concatenate(gather_rel(mem_rows), axis=0)

    qkv8 = product(x_full, columns_half(self_qkv, 3))
    bias_q8 = lax.dynamic_slice_in_dim(proj_bias[0], core * half, half)
    bias_v8 = lax.dynamic_slice_in_dim(proj_bias[1], core * half, half)
    q8 = ((qkv8[:, :half] + bias_q8) * 0.125).astype(low)
    k8 = qkv8[:, half : 2 * half].astype(low)
    v8 = (qkv8[:, 2 * half :] + bias_v8).astype(low)
    info_f = jnp.stack([chip, dec_len[0]]).astype(jnp.int32)
    att8 = self_forward(info_f, q8, k8, v8)

    def heads_to_rows(a8):
        mine = lax.dynamic_slice_in_dim(a8, core * block, block, 0)
        other = swap(lax.dynamic_slice_in_dim(a8, (1 - core) * block, block, 0), "mem", 1)
        return jnp.where(
            core == 0, jnp.concatenate([mine, other], axis=1), jnp.concatenate([other, mine], axis=1)
        )

    attended = heads_to_rows(att8)
    x_own = own_rows(x_full).astype(jnp.float32)
    first, first_norm, first_inv = normalize(
        x_own + product(attended, self_out) + proj_bias[2], norm_gain[0], norm_shift[0]
    )
    first_low = first.astype(low)
    first_slots = gather_rel(first_low)
    first_chip = jnp.concatenate(
        [
            jnp.where(core == 0, first_slots[0], first_slots[1]),
            jnp.where(core == 0, first_slots[1], first_slots[0]),
        ],
        axis=0,
    )

    bias_cq8 = lax.dynamic_slice_in_dim(proj_bias[3], core * half, half)
    cq8 = ((product(first_chip, columns_half(cross_q, 1)) + bias_cq8) * 0.125).astype(low)
    kv8 = product(mem_full, columns_half(cross_kv, 2))
    bias_cv8 = lax.dynamic_slice_in_dim(proj_bias[4], core * half, half)
    kc8 = kv8[:, :half].astype(low)
    vc8 = (kv8[:, half:] + bias_cv8).astype(low)
    slot_pos = jnp.stack([(me ^ k) * mem_block for k in range(4)])
    mem_pos = (slot_pos[:, None] + jnp.arange(mem_block, dtype=jnp.int32)[None, :]).reshape(-1)
    mem_bias = jnp.where(mem_pos < mem_len[0], 0.0, neg_fill).astype(jnp.float32)
    crossed = heads_to_rows(cross_forward(cq8, kc8, vc8, mem_bias[None, :]))
    second, second_norm, second_inv = normalize(
        first + product(crossed, cross_out) + proj_bias[5], norm_gain[1], norm_shift[1]
    )
    second_low = second.astype(low)

    act, act_grad = gelu_parts(product(second_low, ffn_in) + ffn_bias)
    act, act_grad = act.astype(low), act_grad.astype(low)
    third, third_norm, third_inv = normalize(
        second + product(act, ffn_out) + proj_bias[6], norm_gain[2], norm_shift[2]
    )
    row_pos = block_of(me) * block + jnp.arange(block, dtype=jnp.int32)
    cot = jnp.where((row_pos < dec_len[0])[:, None], own_rows(grad_out[0]).astype(jnp.float32), 0.0)
    dh3, gain_three, shift_three = norm_back(cot, third_norm, third_inv, norm_gain[2])
    dz = dh3.astype(low)
    du = (product_nt(dz, ffn_out) * act_grad.astype(jnp.float32)).astype(low)
    dh2, gain_two, shift_two = norm_back(
        dh3 + product_nt(du, ffn_in), second_norm, second_inv, norm_gain[1]
    )
    dco = dh2.astype(low)

    second_full = jnp.concatenate(gather_rel(second_low), axis=0)
    dz_full = jnp.concatenate(gather_rel(dz), axis=0)
    dco_full = jnp.concatenate(gather_rel(dco), axis=0)
    piece = hidden // groups // 4
    w_in_q = lax.dynamic_index_in_dim(ffn_in.reshape(width, groups, 4, piece), quart, 2, False).reshape(
        width, hidden // 4
    )
    w_out_q = lax.dynamic_index_in_dim(ffn_out.reshape(groups, 4, piece, width), quart, 1, False).reshape(
        hidden // 4, width
    )
    b_in_q = lax.dynamic_index_in_dim(ffn_bias.reshape(groups, 4, piece), quart, 1, False).reshape(-1)
    act_q, slope_q = gelu_parts(product(second_full, w_in_q) + b_in_q)
    act_q = act_q.astype(low)
    du_q = (product_nt(dz_full, w_out_q) * slope_q).astype(low)
    g_in, g_out = scatter_dp([product_tn(second_full, du_q), product_tn(act_q, dz_full)])

    first_full = jnp.concatenate(first_slots, axis=0)
    bias_cq4 = lax.dynamic_slice_in_dim(proj_bias[3], quart * quarter, quarter)
    cq4 = ((product(first_full, columns_quarter(cross_q, 1)) + bias_cq4) * 0.125).astype(low)
    cross_out_q = lax.dynamic_slice_in_dim(cross_out, quart * quarter, quarter, 0)
    dx4 = product_nt(dco_full, cross_out_q).astype(low)
    pair_base = chip * (quarter // 128)
    info_c = jnp.stack([pair_base]).astype(jnp.int32)
    bias_col = jnp.broadcast_to(mem_bias[:, None], (mem_bias.shape[0], 128))
    dq4, dkc4, dvc4 = attention_back(info_c, cq4, kc8, vc8, dx4, bias_col, False)
    dkv4 = jnp.concatenate([dkc4, dvc4], axis=1)

    def to_rows(a, size):
        slots = [a[k * size : (k + 1) * size] for k in range(4)]
        return by_quarter([slots[0]] + [swap(slots[k], "mem", k) for k in (1, 2, 3)])

    dq_own = jnp.concatenate(to_rows(dq4, block), axis=1)
    dkv_parts = to_rows(dkv4, mem_block)
    dkv_own = jnp.concatenate(
        [a[:, :quarter] for a in dkv_parts] + [a[:, quarter:] for a in dkv_parts], axis=1
    )
    grad_memory = product_nt(dkv_own, cross_kv)[None]
    crossed_full = jnp.concatenate(gather_rel(crossed), axis=0)
    dco_q = lax.dynamic_slice_in_dim(dco_full, quart * quarter, quarter, 1)
    g_co, g_cq, g_ckv = scatter_dp(
        [product_tn(crossed_full, dco_q), product_tn(first_full, dq4), product_tn(mem_full, dkv4)]
    )

    dh1, gain_one, shift_one = norm_back(
        dh2 + product_nt(dq_own, cross_q), first_norm, first_inv, norm_gain[0]
    )
    do = dh1.astype(low)
    do_full = jnp.concatenate(gather_rel(do), axis=0)

    self_out_q = lax.dynamic_slice_in_dim(self_out, quart * quarter, quarter, 0)
    da4 = product_nt(do_full, self_out_q).astype(low)
    order = [0, 2, 3, 1]
    info_s = jnp.stack([pair_base, dec_len[0]] + [me ^ order[n] for n in range(4)]).astype(jnp.int32)
    sq4, sk4, sv4 = attention_back(info_s, q8, k8, v8, da4, bias_col[:8], True)
    dqkv4 = jnp.concatenate([sq4, sk4, sv4], axis=1)
    qkv_q = columns_quarter(self_qkv, 3)
    partial = product_nt(dqkv4, qkv_q).reshape(4, block, width)

    def rows_for(m):
        return lax.dynamic_index_in_dim(partial, block_of(m), 0, False)

    sent = jnp.concatenate([rows_for(me ^ 1).astype(low), rows_for(me ^ 3).astype(low)], axis=0)
    got = swap(sent, "mem", 1).astype(jnp.float32)
    across = swap((rows_for(me ^ 2) + got[block:]).astype(low), "mem", 2).astype(jnp.float32)
    grad_own = (dh1 + rows_for(me) + got[:block] + across).astype(low)
    grad_dec = by_block(gather_rel(grad_own)).astype(jnp.float32)[None]
    layer_out = by_block(gather_rel(third.astype(low)))[None]

    attended_full = jnp.concatenate(gather_rel(attended), axis=0)
    do_q = lax.dynamic_slice_in_dim(do_full, quart * quarter, quarter, 1)
    g_qkv, g_so = scatter_dp([product_tn(x_full, dqkv4), product_tn(attended_full, do_q)])

    def gather_parts(parts):
        packed = jnp.concatenate([a.astype(low) for a in parts], axis=1)
        slots = by_quarter(gather_rel(packed))
        out, start = [], 0
        for a in parts:
            out.append([s[:, start : start + a.shape[1]].astype(jnp.float32) for s in slots])
            start += a.shape[1]
        return out

    in_parts, out_parts = gather_parts([g_in, g_out])
    co_parts, cq_parts, ckv_parts = gather_parts([g_co, g_cq, g_ckv])
    qkv_parts, so_parts = gather_parts([g_qkv, g_so])

    def interleave(parts, count):
        r = parts[0].shape[0]
        return jnp.stack([p.reshape(r, count, -1) for p in parts], axis=2).reshape(r, -1)

    place = jnp.zeros((2, width), jnp.float32)
    own_sums = jnp.stack([column_sum(sq4), column_sum(sv4)])
    place = lax.dynamic_update_slice(place, own_sums, (0, quart * quarter))
    packed = jnp.concatenate(
        [
            place,
            jnp.stack(
                [
                    column_sum(do),
                    column_sum(dq_own),
                    column_sum(dkv_own[:, width:]),
                    column_sum(dco),
                    column_sum(dz),
                    gain_one,
                    gain_two,
                    gain_three,
                    shift_one,
                    shift_two,
                    shift_three,
                ]
            ),
            column_sum(du).reshape(hidden // width, width),
        ],
        axis=0,
    )
    packed = sum_all(packed)
    return (
        layer_out,
        grad_dec,
        grad_memory,
        interleave(qkv_parts, 3),
        interleave(so_parts, 1),
        interleave(cq_parts, 1),
        interleave(ckv_parts, 2),
        interleave(co_parts, 1),
        interleave(in_parts, groups),
        jnp.concatenate(out_parts, axis=0),
        packed[:7],
        packed[13:].reshape(hidden),
        packed[7:10],
        packed[10:13],
    )


def solution(mesh):
    in_specs = (
        P("dp", None, None),
        P("dp", "mem", None),
        P("dp"),
        P("dp"),
        P("dp", None, None),
    ) + (P(),) * 11
    out_specs = (
        P("dp", None, None),
        P("dp", None, None),
        P("dp", "mem", None),
    ) + (P("dp", None),) * 7 + (P(),) * 4
    return jax.shard_map(
        per_device, mesh=mesh, in_specs=in_specs, out_specs=out_specs, check_vma=False
    )
```

time: 1820 us -> 502 us (0.28)
  waiting for transfers between devices: 1030 us -> 121 us
  matrix products: 461 us -> 82.4 us
  blocking collectives: 139 us -> 0 us
  local copies, waits for them, and re-layouts: 60.3 us -> 120 us
  Pallas kernels: 0 us -> 57.1 us
  starting transfers between devices: 0.8 us -> 40.7 us
  other arithmetic: 105 us -> 66.8 us
    reduce_scatter x7 -> x0, waiting for transfers between devices: 932 us -> none  [the longest x1 284 us: per_device(): lax.psum_scatter(ffn_in_grad, 'dp', scatter_dimension=0, tiled=True)]
    dot_general x11 -> x0, matrix products: 183 us -> none  [the longest x1 43.5 us: per_device(): jnp.einsum('rhe,che->hrc', attended_grad, v_heads, preferred_element_type...]
    psum x3 -> x0, blocking collectives: 126 us -> none  [the longest x1 77.7 us: per_device(): crossed = lax.psum(cross_part, 'mem')]
    ppermute x0 -> x63, waiting for transfers between devices: none -> 121 us  [swap(): return lax.ppermute(part, axis, [(i, i ^ distance) for i in range(count)])]
    psum x3 -> x0, waiting for transfers between devices: 96.2 us -> none  [the longest x1 64.2 us: per_device(): cq_total = lax.psum(cq_part, 'mem')]
    dot_general x7 -> x9, matrix products: 94.9 us -> 29 us  [product(): return jnp.dot(left_rows, right_rows, preferred_element_type=jnp.float32)]
    pallas_call x0 -> x4, Pallas kernels: none -> 57.1 us  [the longest x2 37.3 us: attention_back(): pl.pallas_call(functools.partial(back_kernel, causal=causal), out_shape=[...]
    convert_element_type x5 -> x13, other arithmetic: 73.9 us -> 17 us  [the longest x1 4.14 us: per_device(): v8 = (qkv8[:, 2 * half:] + bias_v8).astype(low)]
  transfers between devices with their start and end apart: 10 -> 63, of which waited for: 8 -> 18; matrix products, arithmetic and copies ran while one was open for 17% -> 50% of each run, Pallas kernels for 0% -> 10%
where the time goes in v1:
time: 502 us; the launch traced here: 492 us
  waiting for transfers between devices  121 us (24%)
  local copies, waits for them, and re-layouts  120 us (24%)
  matrix products  82.4 us (16%)
  other arithmetic  66.8 us (13%)
  Pallas kernels  57.1 us (11%)
  starting transfers between devices  40.7 us (8%)
    ppermute x63, waiting for transfers between devices, swap(): return lax.ppermute(part, axis, [(i, i ^ distance) for i in range(count)])  121 us
    unnamed x193, local copies, waits for them, and re-layouts  51.1 us
    ppermute x63, starting transfers between devices, swap(): return lax.ppermute(part, axis, [(i, i ^ distance) for i in range(count)])  40.7 us
    pallas_call x2, Pallas kernels, attention_back(): pl.pallas_call(functools.partial(back_kernel, causal=causal), out_shape=[...  37.3 us
    dot_general x7, matrix products, product_tn(): lax.dot_general(left_rows, right_rows, (((0,), (0,)), ((), ())), preferre...  32.3 us
    dot_general x9, matrix products, product(): return jnp.dot(left_rows, right_rows, preferred_element_type=jnp.float32)  29 us
    dot_general x7, matrix products, product_nt(): lax.dot_general(left_rows, right_rows, (((1,), (1,)), ((), ())), preferre...  21 us
    add x10, other arithmetic, scatter_dp(): kept.append(a + got[:, :, start:start + w].astype(jnp.float32))  11.6 us
  transfers between devices with their start and end apart: 63, of which 18 were waited for; matrix products, arithmetic and copies ran while one was open for 50% of the time, Pallas kernels for 10%

profile of v1, /device:TPU:0, one launch (start us, length us, event | category | flops | bytes accessed | tf_op | source)
XLA Modules:
  0.0 492.2 jit_solution(12736536057581124090)
XLA Ops:
  0.7 3.0 collective-permute-start.3
  5.4 8.7 %copy.75 = bf16[1024,3072]{0,1:T(8,128)(2,1)} copy(bf16[1024,3072]{1,0:T(8,128)(2,1)} %param.21) | data formatting | bytes 12582912 | tf_op args[5]
  14.1 2.3 constant_dynamic-slice_fusion.26
  16.6 3.5 convolution_bitcast_fusion
  20.1 2.6 copy-done.9
  24.4 4.1 fusion.15
  28.5 9.5 %self_forward.1 = bf16[512,512]{1,0:T(8,128)(2,1)} custom-call(s32[2]{0:T(128)} %pad_add_fusion.info, bf16[1024,512]{1,0:T(8,128)(2,1)} %get-tuple-element.61.q_ref, bf16[1024,512]{1,0:T(8,128)(2,1)} %slice.517.k_ref, bf16[1024,512]{1,0:T(8,128)(2,1)} %get-tuple-element.60.v_ref), custom_call_target="tpu_custom_call" | custom-call | flops 3221225472 | bytes 4194304 | tf_op jit(solution)/shard_map/self_forward/pallas_call | solution.py:106
  39.8 3.9 copy.77
  43.7 6.4 %copy.79 = bf16[1024,2048]{0,1:T(8,128)(2,1)} copy(bf16[1024,2048]{1,0:T(8,128)(2,1)} %param.24) | data formatting | bytes 8388608 | tf_op args[8]
  51.0 2.7 fusion.136
  55.7 12.1 %copy.104 = bf16[1024,4096]{0,1:T(8,128)(2,1)} copy(bf16[1024,4096]{1,0:T(8,128)(2,1)} %param.26) | data formatting | bytes 16777216 | tf_op args[10]
  73.3 3.8 fusion.86
  79.5 10.3 %cross_forward.1 = bf16[512,512]{1,0:T(8,128)(2,1)} custom-call(bf16[512,512]{1,0:T(8,128)(2,1)} %fusion.48.q_ref, bf16[1024,512]{1,0:T(8,128)(2,1)} %slice.516.k_ref, bf16[1024,512]{1,0:T(8,128)(2,1)} %fusion.14.v_ref, f32[1,1024]{1,0:T(1,128)} %bitcast.518), custom_call_target="tpu_custom_call" | custom-call | flops 4294967296 | bytes 2097152 | tf_op jit(solution)/shard_map/cross_forward/pallas_call | solution.py:140
  91.1 3.1 constant_dynamic-slice_fusion.1
  97.7 6.3 %convolution_add_fusion = f32[256,4096]{1,0:T(8,128)S(1)} fusion(bf16[256,1024]{1,0:T(8,128)(2,1)S(1)} %fusion.70, bf16[1024,4096]{1,0:T(8,128)(2,1)} %param.26, f32[4096]{0:T(1024)S(1)} %copy-done.67), kind=kOutput, calls=%fused_computation.3 | convolution fusion | flops 2148532224 | bytes 13123584 | tf_op jit(solution)/shard_map/dot_general | solution.py:18
  104.0 2.7 fusion.138
  110.0 5.4 %convert_reduce_fusion = (f32[4096]{0:T(1024)S(1)}, bf16[256,4096]{1,0:T(8,128)(2,1)}) fusion(f32[256,4096]{1,0:T(8,128)S(1)} %convolution_add_fusion, bf16[256,1024]{1,0:T(8,128)(2,1)S(1)} %get-tuple-element.53, bf16[4096,1024]{1,0:T(8,128)(2,1)S(1)} %bitcast.462), kind=kOutput, calls=%fused_computation.17 | convolution fusion | flops 2162159616 | bytes 15220736 | tf_op jit(solution)/shard_map/dot_general | solution.py:28
  115.5 5.4 %multiply_reduce_fusion = (f32[1024]{0:T(1024)}, f32[256]{0:T(256)S(1)}, f32[256]{0:T(256)S(1)}, f32[1024]{0:T(1024)}, f32[256,1024]{1,0:T(8,128)S(1)}) fusion(f32[256,1024]{1,0:T(8,128)S(1)} %get-tuple-element.169, f32[256]{0:T(256)S(1)} %add_rsqrt_fusion.1, f32[256]{0:T(256)S(1)} %broadcast_multiply_fusion.7, f32[1024]{0:T(1024)S(1)} %bitcast.494, ...), kind=kOutput, calls=%fused_computation.125 | convolution fusion | flops 2152461824 | bytes 14180612 | tf_op jit(solution)/shard_map/dot_general | solution.py:28
  120.9 2.1 convert_reduce_fusion.2
  123.0 2.0 collective-permute-start.12
  125.2 3.1 constant_dynamic-slice_fusion.2
  130.0 1.9 collective-permute-start.47
  132.0 6.2 %collective-permute-done.12 = bf16[256,1024]{1,0:T(8,128)(2,1)} collective-permute-done((bf16[256,1024]{1,0:T(8,128)(2,1)}, bf16[256,1024]{1,0:T(8,128)(2,1)}, u32[]{:S(2)}, u32[]{:S(2)}) %collective-permute-start.12) | collective-permute-done | bytes 524320 | tf_op jit(solution)/shard_map/ppermute | solution.py:233
  138.7 2.7 constant_dynamic-slice_fusion.15
  141.4 8.0 %collective-permute-done.29 = bf16[256,1024]{1,0:T(8,128)(2,1)} collective-permute-done((bf16[256,1024]{1,0:T(8,128)(2,1)}, bf16[256,1024]{1,0:T(8,128)(2,1)}, u32[]{:S(2)}, u32[]{:S(2)}) %collective-permute-start.29) | collective-permute-done | bytes 524320 | tf_op jit(solution)/shard_map/ppermute | solution.py:233
  149.9 3.3 fusion.47.q_ref
  153.3 6.7 %collective-permute-done.47 = bf16[256,1024]{1,0:T(8,128)(2,1)} collective-permute-done((bf16[256,1024]{1,0:T(8,128)(2,1)}, bf16[256,1024]{1,0:T(8,128)(2,1)}, u32[]{:S(2)}, u32[]{:S(2)}) %collective-permute-start.47) | collective-permute-done | bytes 524320 | tf_op jit(solution)/shard_map/ppermute | solution.py:233
  166.0 21.6 %cross_back.1 = (bf16[1024,256]{1,0:T(8,128)(2,1)}, bf16[1024,256]{1,0:T(8,128)(2,1)}, bf16[1024,256]{1,0:T(8,128)(2,1)}) custom-call(s32[1]{0:T(128)} %bitcast.40.info, bf16[1024,256]{1,0:T(8,128)(2,1)} %fusion.47.q_ref, bf16[1024,512]{1,0:T(8,128)(2,1)} %slice.516.k_ref, bf16[1024,512]{1,0:T(8,128)(2,1)} %fusion.14.v_ref, ...), custom_call_target="tpu_custom_call" | custom-call | flops 10737418240 | bytes 3670016 | tf_op jit(solution)/shard_map/cross_back/pallas_call | solution.py:207
  189.9 2.9 fusion.85
  193.8 3.4 fusion.87
  198.0 3.4 fusion.84
  201.5 10.4 %collective-permute-done.38 = bf16[256,1024]{1,0:T(8,128)(2,1)} collective-permute-done((bf16[256,1024]{1,0:T(8,128)(2,1)}, bf16[256,1024]{1,0:T(8,128)(2,1)}, u32[]{:S(2)}, u32[]{:S(2)}) %collective-permute-start.38) | collective-permute-done | bytes 524320 | tf_op jit(solution)/shard_map/ppermute | solution.py:233
  212.5 4.5 fusion.13
  217.0 10.7 %fusion.71 = f32[1024,1024]{1,0:T(8,128)} fusion(f32[1024,1024]{1,0:T(8,128)} %copy-done.78, bf16[1024,1024]{1,0:T(8,128)(2,1)S(1)} %bitcast.429, f32[1024]{0:T(1024)S(1)} %bitcast.517, bf16[256,1024]{1,0:T(8,128)(2,1)} %copy-done.77, bf16[256,1024]{1,0:T(8,128)(2,1)} %copy-done.74, bf16[256,1024]{1,0:T(8,128)(2,1)} %copy-done.76, ...), kind=kOutput, calls=%fused_computation.155 | convolution fusion | flops 4323278848 | bytes 14684160 | tf_op jit(solution)/shard_map/dot_general | solution.py:22
  235.0 2.4 fusion.26
  252.8 4.3 collective-permute-done.26
  262.6 2.3 convolution_bitcast_fusion.1
  264.8 6.9 %collective-permute-done.18 = bf16[256,1024]{1,0:T(8,128)(2,1)} collective-permute-done((bf16[256,1024]{1,0:T(8,128)(2,1)S(1)}, bf16[256,1024]{1,0:T(8,128)(2,1)}, u32[]{:S(2)}, u32[]{:S(2)}) %collective-permute-start.18) | collective-permute-done | bytes 524320 | tf_op jit(solution)/shard_map/ppermute | solution.py:233
  271.7 5.6 %collective-permute-done.40 = bf16[4,128,1024]{2,1,0:T(8,128)(2,1)S(1)} collective-permute-done((bf16[4,128,1024]{2,1,0:T(8,128)(2,1)S(1)}, bf16[4,128,1024]{2,1,0:T(8,128)(2,1)S(1)}, u32[]{:S(2)}, u32[]{:S(2)}) %collective-permute-start.40) | collective-permute-done | bytes 1048608 | tf_op jit(solution)/shard_map/ppermute | solution.py:233
  284.2 3.0 convolution_convert_fusion.g0_ref.g1_ref.g2_ref.g3_ref
  287.8 15.7 %self_back.1 = (bf16[1024,256]{1,0:T(8,128)(2,1)}, bf16[1024,256]{1,0:T(8,128)(2,1)}, bf16[1024,256]{1,0:T(8,128)(2,1)}) custom-call(s32[6]{0:T(128)} %stack.233.info, bf16[1024,512]{1,0:T(8,128)(2,1)} %get-tuple-element.61.q_ref, bf16[1024,512]{1,0:T(8,128)(2,1)} %slice.517.k_ref, bf16[1024,512]{1,0:T(8,128)(2,1)} %get-tuple-element.60.v_ref, ...), custom_call_target="tpu_custom_call" | custom-call | flops 5368709120 | bytes 3670016 | tf_op jit(solution)/shard_map/self_back/pallas_call | solution.py:207
  312.0 5.2 %fusion.38 = f32[1024,768]{0,1:T(8,128)} fusion(bf16[1024,768]{1,0:T(8,128)(2,1)S(1)} %constant_dynamic-update-slice_fusion, bf16[1,1024,1024]{2,1,0:T(8,128)(2,1)} %param.16), kind=kOutput, calls=%fused_computation.69 | convolution fusion | flops 1610612736 | bytes 6815744 | tf_op jit(solution)/shard_map/dot_general | solution.py:22
  317.5 3.3 fusion.18
  320.8 5.6 %reshape_reshape.21 = f32[4,2,128,768]{2,1,0,3:T(2,128)} reshape(f32[1024,768]{0,1:T(8,128)} %fusion.38) | data formatting | bytes 6291456 | tf_op jit(solution)/shard_map/reshape;reshape | solution.py:250
  328.0 3.2 constant_dynamic-slice_fusion.10
  333.0 2.6 constant_dynamic-slice_fusion.9
  335.5 3.4 copy.117
  340.6 3.1 collective-permute-done.61
  343.7 3.0 collective-permute-start.62
  348.4 3.2 copy.84
  357.5 9.3 %collective-permute-done.42 = bf16[1,128,1024]{1,2,0:T(8,128)(2,1)S(1)} collective-permute-done((bf16[1,128,1024]{1,2,0:T(8,128)(2,1)S(1)}, bf16[1,128,1024]{1,2,0:T(8,128)(2,1)S(1)}, u32[]{:S(2)}, u32[]{:S(2)}) %collective-permute-start.42) | collective-permute-done | bytes 262176 | tf_op jit(solution)/shard_map/ppermute | solution.py:233
  367.9 2.9 bitcast_add_fusion.1
  376.3 2.3 fusion.51
  391.0 2.7 reshape.464
  394.8 15.4 %collective-permute-done.32 = bf16[2,128,1024]{2,1,0:T(8,128)(2,1)} collective-permute-done((bf16[2,128,1024]{2,1,0:T(8,128)(2,1)}, bf16[2,128,1024]{2,1,0:T(8,128)(2,1)}, u32[]{:S(2)}, u32[]{:S(2)}) %collective-permute-start.32) | collective-permute-done | bytes 524320 | tf_op jit(solution)/shard_map/ppermute | solution.py:233
  412.7 2.7 fusion.53
  416.5 10.5 %collective-permute-done.33 = bf16[1,128,1024]{2,1,0:T(8,128)(2,1)S(1)} collective-permute-done((bf16[1,128,1024]{2,1,0:T(8,128)(2,1)S(1)}, bf16[1,128,1024]{2,1,0:T(8,128)(2,1)S(1)}, u32[]{:S(2)}, u32[]{:S(2)}) %collective-permute-start.33) | collective-permute-done | bytes 262176 | tf_op jit(solution)/shard_map/ppermute | solution.py:233
  429.9 5.5 %collective-permute-done.35 = bf16[128,1024]{1,0:T(8,128)(2,1)S(1)} collective-permute-done((bf16[128,1024]{1,0:T(8,128)(2,1)S(1)}, bf16[128,1024]{1,0:T(8,128)(2,1)S(1)}, u32[]{:S(2)}, u32[]{:S(2)}) %collective-permute-start.35) | collective-permute-done | bytes 262176 | tf_op jit(solution)/shard_map/ppermute | solution.py:233
  444.7 3.1 copy.109
  448.7 13.7 %collective-permute-done.54 = bf16[1,128,2048]{2,1,0:T(8,128)(2,1)} collective-permute-done((bf16[1,128,2048]{2,1,0:T(8,128)(2,1)}, bf16[1,128,2048]{2,1,0:T(8,128)(2,1)}, u32[]{:S(2)}, u32[]{:S(2)}) %collective-permute-start.54) | collective-permute-done | bytes 524320 | tf_op jit(solution)/shard_map/ppermute | solution.py:233
  466.2 11.6 %collective-permute-done.56 = bf16[128,2048]{1,0:T(8,128)(2,1)} collective-permute-done((bf16[128,2048]{1,0:T(8,128)(2,1)S(1)}, bf16[128,2048]{1,0:T(8,128)(2,1)}, u32[]{:S(2)}, u32[]{:S(2)}) %collective-permute-start.56) | collective-permute-done | bytes 524320 | tf_op jit(solution)/shard_map/ppermute | solution.py:233
  479.8 2.5 maximum_convert_fusion
  484.3 2.7 copy.108
  487.0 3.2 reshape.468
  (477 shorter events, 138.2 us)
Async XLA Ops:
  0.6 94.4 %copy-start = (bf16[1024,1024]{1,0:T(8,128)(2,1)S(1)}, bf16[1024,1024]{1,0:T(8,128)(2,1)}, u32[]{:S(2)}) copy-start(bf16[1024,1024]{1,0:T(8,128)(2,1)} %param.25) | copy-start | bytes 6291460
  0.7 69.0 %collective-permute-start.3 = (bf16[256,1024]{1,0:T(8,128)(2,1)}, bf16[256,1024]{1,0:T(8,128)(2,1)}, u32[]{:S(2)}, u32[]{:S(2)}) collective-permute-start(bf16[256,1024]{1,0:T(8,128)(2,1)} %bitcast.527), channel_id=1, source_target_pairs={{0,2},{1,3},{2,0},{3,1},{4,6},{5,7},{6,4},{7,5},{8,10},{9,11},{10,... | collective-permute-start | bytes 1572872 | tf_op jit(solution)/shard_map/ppermute | solution.py:233
  3.7 69.6 %collective-permute-start.2 = (bf16[256,1024]{1,0:T(8,128)(2,1)}, bf16[256,1024]{1,0:T(8,128)(2,1)}, u32[]{:S(2)}, u32[]{:S(2)}) collective-permute-start(bf16[256,1024]{1,0:T(8,128)(2,1)} %bitcast.528), channel_id=1, source_target_pairs={{0,1},{1,0},{2,3},{3,2},{4,5},{5,4},{6,7},{7,6},{8,9},{9,8},{10,11... | collective-permute-start | bytes 1572872 | tf_op jit(solution)/shard_map/ppermute | solution.py:233
  39.1 11.7 %collective-permute-start = (bf16[256,512]{1,0:T(8,128)(2,1)S(1)}, bf16[256,512]{1,0:T(8,128)(2,1)S(1)}, u32[]{:S(2)}, u32[]{:S(2)}) collective-permute-start(bf16[256,512]{1,0:T(8,128)(2,1)S(1)} %get-tuple-element.126), channel_id=1, source_target_pairs={{0,1},{1,0},{2,3},{3,2},{4,5},{5,4},{6,7},{7,6},{8,9},{9,8},{10,11... | collective-permute-start | bytes 786440 | tf_op jit(solution)/shard_map/ppermute | solution.py:233
  55.0 15.2 %collective-permute-start.1 = (bf16[256,1024]{1,0:T(8,128)(2,1)}, bf16[256,1024]{1,0:T(8,128)(2,1)}, u32[]{:S(2)}, u32[]{:S(2)}) collective-permute-start(bf16[256,1024]{1,0:T(8,128)(2,1)} %fusion.69), channel_id=1, source_target_pairs={{0,1},{1,0},{2,3},{3,2},{4,5},{5,4},{6,7},{7,6},{8,9},{9,8},{10,11... | collective-permute-start | bytes 1572872 | tf_op jit(solution)/shard_map/ppermute | solution.py:233
  69.7 3.6 collective-permute-start.4
  90.8 3.3 collective-permute-start.5
  94.1 31.0 %collective-permute-start.9 = (bf16[256,1024]{1,0:T(8,128)(2,1)}, bf16[256,1024]{1,0:T(8,128)(2,1)}, u32[]{:S(2)}, u32[]{:S(2)}) collective-permute-start(bf16[256,1024]{1,0:T(8,128)(2,1)} %fusion.69), channel_id=1, source_target_pairs={{0,2},{1,3},{2,0},{3,1},{4,6},{5,7},{6,4},{7,5},{8,10},{9,11},{10,... | collective-permute-start | bytes 1572872 | tf_op jit(solution)/shard_map/ppermute | solution.py:233
  123.0 15.1 %collective-permute-start.12 = (bf16[256,1024]{1,0:T(8,128)(2,1)}, bf16[256,1024]{1,0:T(8,128)(2,1)}, u32[]{:S(2)}, u32[]{:S(2)}) collective-permute-start(bf16[256,1024]{1,0:T(8,128)(2,1)} %get-tuple-element.55), channel_id=1, source_target_pairs={{0,2},{1,3},{2,0},{3,1},{4,6},{5,7},{6,4},{7,5},{8,10},{9,11},{10,... | collective-permute-start | bytes 1572872 | tf_op jit(solution)/shard_map/ppermute | solution.py:233
  125.1 24.3 %collective-permute-start.29 = (bf16[256,1024]{1,0:T(8,128)(2,1)}, bf16[256,1024]{1,0:T(8,128)(2,1)}, u32[]{:S(2)}, u32[]{:S(2)}) collective-permute-start(bf16[256,1024]{1,0:T(8,128)(2,1)} %copy-done.48), channel_id=1, source_target_pairs={{0,2},{1,3},{2,0},{3,1},{4,6},{5,7},{6,4},{7,5},{8,10},{9,11},{10,... | collective-permute-start | bytes 1572872 | tf_op jit(solution)/shard_map/ppermute | solution.py:233
  125.1 24.2 %collective-permute-start.10 = (bf16[256,1024]{1,0:T(8,128)(2,1)}, bf16[256,1024]{1,0:T(8,128)(2,1)}, u32[]{:S(2)}, u32[]{:S(2)}) collective-permute-start(bf16[256,1024]{1,0:T(8,128)(2,1)} %collective-permute-done.9), channel_id=1, source_target_pairs={{0,1},{1,0},{2,3},{3,2},{4,5},{5,4},{6,7},{7,6},{8,9},{9,8},{10,11... | collective-permute-start | bytes 1572872 | tf_op jit(solution)/shard_map/ppermute | solution.py:233
  129.5 23.7 %collective-permute-start.11 = (bf16[256,1024]{1,0:T(8,128)(2,1)}, bf16[256,1024]{1,0:T(8,128)(2,1)}, u32[]{:S(2)}, u32[]{:S(2)}) collective-permute-start(bf16[256,1024]{1,0:T(8,128)(2,1)} %get-tuple-element.55), channel_id=1, source_target_pairs={{0,1},{1,0},{2,3},{3,2},{4,5},{5,4},{6,7},{7,6},{8,9},{9,8},{10,11... | collective-permute-start | bytes 1572872 | tf_op jit(solution)/shard_map/ppermute | solution.py:233
  130.0 30.0 %collective-permute-start.47 = (bf16[256,1024]{1,0:T(8,128)(2,1)}, bf16[256,1024]{1,0:T(8,128)(2,1)}, u32[]{:S(2)}, u32[]{:S(2)}) collective-permute-start(bf16[256,1024]{1,0:T(8,128)(2,1)} %copy-done.43), channel_id=1, source_target_pairs={{0,2},{1,3},{2,0},{3,1},{4,6},{5,7},{6,4},{7,5},{8,10},{9,11},{10,... | collective-permute-start | bytes 1572872 | tf_op jit(solution)/shard_map/ppermute | solution.py:233
  138.1 23.6 %collective-permute-start.13 = (bf16[256,1024]{1,0:T(8,128)(2,1)}, bf16[256,1024]{1,0:T(8,128)(2,1)}, u32[]{:S(2)}, u32[]{:S(2)}) collective-permute-start(bf16[256,1024]{1,0:T(8,128)(2,1)} %collective-permute-done.12), channel_id=1, source_target_pairs={{0,1},{1,0},{2,3},{3,2},{4,5},{5,4},{6,7},{7,6},{8,9},{9,8},{10,11... | collective-permute-start | bytes 1572872 | tf_op jit(solution)/shard_map/ppermute | solution.py:233
  149.4 167.8 %collective-permute-start.28 = (bf16[256,1024]{1,0:T(8,128)(2,1)}, bf16[256,1024]{1,0:T(8,128)(2,1)}, u32[]{:S(2)}, u32[]{:S(2)}) collective-permute-start(bf16[256,1024]{1,0:T(8,128)(2,1)} %copy-done.48), channel_id=1, source_target_pairs={{0,1},{1,0},{2,3},{3,2},{4,5},{5,4},{6,7},{7,6},{8,9},{9,8},{10,11... | collective-permute-start | bytes 1572872 | tf_op jit(solution)/shard_map/ppermute | solution.py:233
  149.4 168.1 %collective-permute-start.30 = (bf16[256,1024]{1,0:T(8,128)(2,1)}, bf16[256,1024]{1,0:T(8,128)(2,1)}, u32[]{:S(2)}, u32[]{:S(2)}) collective-permute-start(bf16[256,1024]{1,0:T(8,128)(2,1)} %collective-permute-done.29), channel_id=1, source_target_pairs={{0,1},{1,0},{2,3},{3,2},{4,5},{5,4},{6,7},{7,6},{8,9},{9,8},{10,11... | collective-permute-start | bytes 1572872 | tf_op jit(solution)/shard_map/ppermute | solution.py:233
  153.2 43.9 %collective-permute-start.46 = (bf16[256,1024]{1,0:T(8,128)(2,1)S(1)}, bf16[256,1024]{1,0:T(8,128)(2,1)S(1)}, u32[]{:S(2)}, u32[]{:S(2)}) collective-permute-start(bf16[256,1024]{1,0:T(8,128)(2,1)S(1)} %copy-done.44), channel_id=1, source_target_pairs={{0,1},{1,0},{2,3},{3,2},{4,5},{5,4},{6,7},{7,6},{8,9},{9,8},{10,11... | collective-permute-start | bytes 1572872 | tf_op jit(solution)/shard_map/ppermute | solution.py:233
  160.0 37.5 %collective-permute-start.50 = (bf16[256,1024]{1,0:T(8,128)(2,1)S(1)}, bf16[256,1024]{1,0:T(8,128)(2,1)S(1)}, u32[]{:S(2)}, u32[]{:S(2)}) collective-permute-start(bf16[256,1024]{1,0:T(8,128)(2,1)S(1)} %copy-done.41), channel_id=1, source_target_pairs={{0,2},{1,3},{2,0},{3,1},{4,6},{5,7},{6,4},{7,5},{8,10},{9,11},{10,... | collective-permute-start | bytes 1572872 | tf_op jit(solution)/shard_map/ppermute | solution.py:233
  161.7 36.1 %collective-permute-start.48 = (bf16[256,1024]{1,0:T(8,128)(2,1)}, bf16[256,1024]{1,0:T(8,128)(2,1)S(1)}, u32[]{:S(2)}, u32[]{:S(2)}) collective-permute-start(bf16[256,1024]{1,0:T(8,128)(2,1)} %collective-permute-done.47), channel_id=1, source_target_pairs={{0,1},{1,0},{2,3},{3,2},{4,5},{5,4},{6,7},{7,6},{8,9},{9,8},{10,11... | collective-permute-start | bytes 1572872 | tf_op jit(solution)/shard_map/ppermute | solution.py:233
  197.2 14.7 %collective-permute-start.38 = (bf16[256,1024]{1,0:T(8,128)(2,1)}, bf16[256,1024]{1,0:T(8,128)(2,1)}, u32[]{:S(2)}, u32[]{:S(2)}) collective-permute-start(bf16[256,1024]{1,0:T(8,128)(2,1)} %maximum_select_fusion.1), channel_id=1, source_target_pairs={{0,2},{1,3},{2,0},{3,1},{4,6},{5,7},{6,4},{7,5},{8,10},{9,11},{10,... | collective-permute-start | bytes 1572872 | tf_op jit(solution)/shard_map/ppermute | solution.py:233
  197.5 14.4 %collective-permute-start.49 = (bf16[256,1024]{1,0:T(8,128)(2,1)S(1)}, bf16[256,1024]{1,0:T(8,128)(2,1)S(1)}, u32[]{:S(2)}, u32[]{:S(2)}) collective-permute-start(bf16[256,1024]{1,0:T(8,128)(2,1)S(1)} %copy-done.41), channel_id=1, source_target_pairs={{0,1},{1,0},{2,3},{3,2},{4,5},{5,4},{6,7},{7,6},{8,9},{9,8},{10,11... | collective-permute-start | bytes 1572872 | tf_op jit(solution)/shard_map/ppermute | solution.py:233
  197.8 14.4 %collective-permute-start.51 = (bf16[256,1024]{1,0:T(8,128)(2,1)S(1)}, bf16[256,1024]{1,0:T(8,128)(2,1)S(1)}, u32[]{:S(2)}, u32[]{:S(2)}) collective-permute-start(bf16[256,1024]{1,0:T(8,128)(2,1)S(1)} %collective-permute-done.50), channel_id=1, source_target_pairs={{0,1},{1,0},{2,3},{3,2},{4,5},{5,4},{6,7},{7,6},{8,9},{9,8},{10,11... | collective-permute-start | bytes 1572872 | tf_op jit(solution)/shard_map/ppermute | solution.py:233
  211.9 21.3 %collective-permute-start.37 = (bf16[256,1024]{1,0:T(8,128)(2,1)}, bf16[256,1024]{1,0:T(8,128)(2,1)}, u32[]{:S(2)}, u32[]{:S(2)}) collective-permute-start(bf16[256,1024]{1,0:T(8,128)(2,1)} %maximum_select_fusion.1), channel_id=1, source_target_pairs={{0,1},{1,0},{2,3},{3,2},{4,5},{5,4},{6,7},{7,6},{8,9},{9,8},{10,11... | collective-permute-start | bytes 1572872 | tf_op jit(solution)/shard_map/ppermute | solution.py:233
  211.9 20.9 %collective-permute-start.7 = (bf16[256,1024]{1,0:T(8,128)(2,1)}, bf16[256,1024]{1,0:T(8,128)(2,1)}, u32[]{:S(2)}, u32[]{:S(2)}) collective-permute-start(bf16[256,1024]{1,0:T(8,128)(2,1)} %get-tuple-element.78), channel_id=1, source_target_pairs={{0,2},{1,3},{2,0},{3,1},{4,6},{5,7},{6,4},{7,5},{8,10},{9,11},{10,... | collective-permute-start | bytes 1572872 | tf_op jit(solution)/shard_map/ppermute | solution.py:233
  212.3 21.2 %collective-permute-start.39 = (bf16[256,1024]{1,0:T(8,128)(2,1)}, bf16[256,1024]{1,0:T(8,128)(2,1)}, u32[]{:S(2)}, u32[]{:S(2)}) collective-permute-start(bf16[256,1024]{1,0:T(8,128)(2,1)} %collective-permute-done.38), channel_id=1, source_target_pairs={{0,1},{1,0},{2,3},{3,2},{4,5},{5,4},{6,7},{7,6},{8,9},{9,8},{10,11... | collective-permute-start | bytes 1572872 | tf_op jit(solution)/shard_map/ppermute | solution.py:233
  232.8 6.3 %collective-permute-start.6 = (bf16[256,1024]{1,0:T(8,128)(2,1)}, bf16[256,1024]{1,0:T(8,128)(2,1)S(1)}, u32[]{:S(2)}, u32[]{:S(2)}) collective-permute-start(bf16[256,1024]{1,0:T(8,128)(2,1)} %get-tuple-element.78), channel_id=1, source_target_pairs={{0,1},{1,0},{2,3},{3,2},{4,5},{5,4},{6,7},{7,6},{8,9},{9,8},{10,11... | collective-permute-start | bytes 1572872 | tf_op jit(solution)/shard_map/ppermute | solution.py:233
  233.2 6.3 %collective-permute-start.8 = (bf16[256,1024]{1,0:T(8,128)(2,1)}, bf16[256,1024]{1,0:T(8,128)(2,1)S(1)}, u32[]{:S(2)}, u32[]{:S(2)}) collective-permute-start(bf16[256,1024]{1,0:T(8,128)(2,1)} %collective-permute-done.7), channel_id=1, source_target_pairs={{0,1},{1,0},{2,3},{3,2},{4,5},{5,4},{6,7},{7,6},{8,9},{9,8},{10,11... | collective-permute-start | bytes 1572872 | tf_op jit(solution)/shard_map/ppermute | solution.py:233
  233.4 9.3 %collective-permute-start.16 = (bf16[256,256]{1,0:T(8,128)(2,1)S(1)}, bf16[256,256]{1,0:T(8,128)(2,1)S(1)}, u32[]{:S(2)}, u32[]{:S(2)}) collective-permute-start(bf16[256,256]{1,0:T(8,128)(2,1)S(1)} %get-tuple-element.120), channel_id=1, source_target_pairs={{0,3},{1,2},{2,1},{3,0},{4,7},{5,6},{6,5},{7,4},{8,11},{9,10},{10,... | collective-permute-start | bytes 393224 | tf_op jit(solution)/shard_map/ppermute | solution.py:233
  239.1 5.6 %collective-permute-start.15 = (bf16[256,256]{1,0:T(8,128)(2,1)S(1)}, bf16[256,256]{1,0:T(8,128)(2,1)S(1)}, u32[]{:S(2)}, u32[]{:S(2)}) collective-permute-start(bf16[256,256]{1,0:T(8,128)(2,1)S(1)} %get-tuple-element.121), channel_id=1, source_target_pairs={{0,2},{1,3},{2,0},{3,1},{4,6},{5,7},{6,4},{7,5},{8,10},{9,11},{10,... | collective-permute-start | bytes 393224 | tf_op jit(solution)/shard_map/ppermute | solution.py:233
  239.5 5.6 %collective-permute-start.14 = (bf16[256,256]{1,0:T(8,128)(2,1)S(1)}, bf16[256,256]{1,0:T(8,128)(2,1)S(1)}, u32[]{:S(2)}, u32[]{:S(2)}) collective-permute-start(bf16[256,256]{1,0:T(8,128)(2,1)S(1)} %get-tuple-element.122), channel_id=1, source_target_pairs={{0,1},{1,0},{2,3},{3,2},{4,5},{5,4},{6,7},{7,6},{8,9},{9,8},{10,11... | collective-permute-start | bytes 393224 | tf_op jit(solution)/shard_map/ppermute | solution.py:233
  242.8 8.5 %collective-permute-start.27 = (bf16[256,512]{1,0:T(8,128)(2,1)S(1)}, bf16[256,512]{1,0:T(8,128)(2,1)S(1)}, u32[]{:S(2)}, u32[]{:S(2)}) collective-permute-start(bf16[256,512]{1,0:T(8,128)(2,1)S(1)} %get-tuple-element.96), channel_id=1, source_target_pairs={{0,3},{1,2},{2,1},{3,0},{4,7},{5,6},{6,5},{7,4},{8,11},{9,10},{10,... | collective-permute-start | bytes 786440 | tf_op jit(solution)/shard_map/ppermute | solution.py:233
  244.7 12.4 %collective-permute-start.26 = (bf16[256,512]{1,0:T(8,128)(2,1)S(1)}, bf16[256,512]{1,0:T(8,128)(2,1)S(1)}, u32[]{:S(2)}, u32[]{:S(2)}) collective-permute-start(bf16[256,512]{1,0:T(8,128)(2,1)S(1)} %get-tuple-element.97), channel_id=1, source_target_pairs={{0,2},{1,3},{2,0},{3,1},{4,6},{5,7},{6,4},{7,5},{8,10},{9,11},{10,... | collective-permute-start | bytes 786440 | tf_op jit(solution)/shard_map/ppermute | solution.py:233
  245.1 13.5 %collective-permute-start.25 = (bf16[256,512]{1,0:T(8,128)(2,1)S(1)}, bf16[256,512]{1,0:T(8,128)(2,1)S(1)}, u32[]{:S(2)}, u32[]{:S(2)}) collective-permute-start(bf16[256,512]{1,0:T(8,128)(2,1)S(1)} %get-tuple-element.98), channel_id=1, source_target_pairs={{0,1},{1,0},{2,3},{3,2},{4,5},{5,4},{6,7},{7,6},{8,9},{9,8},{10,11... | collective-permute-start | bytes 786440 | tf_op jit(solution)/shard_map/ppermute | solution.py:233
  251.3 26.0 %collective-permute-start.40 = (bf16[4,128,1024]{2,1,0:T(8,128)(2,1)S(1)}, bf16[4,128,1024]{2,1,0:T(8,128)(2,1)S(1)}, u32[]{:S(2)}, u32[]{:S(2)}) collective-permute-start(bf16[4,128,1024]{2,1,0:T(8,128)(2,1)S(1)} %pad_maximum_fusion.14), channel_id=1, source_target_pairs={{0,4},{4,0},{8,12},{12,8},{16,20},{20,16},{24,28},{28,24},{1,5},{5... | collective-permute-start | bytes 3145736 | tf_op jit(solution)/shard_map/ppermute | solution.py:233
  257.1 110.8 %collective-permute-start.52 = (bf16[4,128,2048]{2,1,0:T(8,128)(2,1)}, bf16[4,128,2048]{2,1,0:T(8,128)(2,1)}, u32[]{:S(2)}, u32[]{:S(2)}) collective-permute-start(bf16[4,128,2048]{2,1,0:T(8,128)(2,1)} %pad_maximum_fusion.8), channel_id=1, source_target_pairs={{0,4},{4,0},{8,12},{12,8},{16,20},{20,16},{24,28},{28,24},{1,5},{5... | collective-permute-start | bytes 6291464 | tf_op jit(solution)/shard_map/ppermute | solution.py:233
  258.6 13.1 %collective-permute-start.18 = (bf16[256,1024]{1,0:T(8,128)(2,1)S(1)}, bf16[256,1024]{1,0:T(8,128)(2,1)}, u32[]{:S(2)}, u32[]{:S(2)}) collective-permute-start(bf16[256,1024]{1,0:T(8,128)(2,1)S(1)} %get-tuple-element.58), channel_id=1, source_target_pairs={{0,2},{1,3},{2,0},{3,1},{4,6},{5,7},{6,4},{7,5},{8,10},{9,11},{10,... | collective-permute-start | bytes 1572872 | tf_op jit(solution)/shard_map/ppermute | solution.py:233
  271.7 9.3 %collective-permute-start.17 = (bf16[256,1024]{1,0:T(8,128)(2,1)S(1)}, bf16[256,1024]{1,0:T(8,128)(2,1)}, u32[]{:S(2)}, u32[]{:S(2)}) collective-permute-start(bf16[256,1024]{1,0:T(8,128)(2,1)S(1)} %get-tuple-element.58), channel_id=1, source_target_pairs={{0,1},{1,0},{2,3},{3,2},{4,5},{5,4},{6,7},{7,6},{8,9},{9,8},{10,11... | collective-permute-start | bytes 1572872 | tf_op jit(solution)/shard_map/ppermute | solution.py:233
  277.3 5.3 %collective-permute-start.19 = (bf16[256,1024]{1,0:T(8,128)(2,1)}, bf16[256,1024]{1,0:T(8,128)(2,1)}, u32[]{:S(2)}, u32[]{:S(2)}) collective-permute-start(bf16[256,1024]{1,0:T(8,128)(2,1)} %collective-permute-done.18), channel_id=1, source_target_pairs={{0,1},{1,0},{2,3},{3,2},{4,5},{5,4},{6,7},{7,6},{8,9},{9,8},{10,11... | collective-permute-start | bytes 1572872 | tf_op jit(solution)/shard_map/ppermute | solution.py:233
  281.0 71.5 %collective-permute-start.41 = (bf16[2,128,1024]{1,2,0:T(8,128)(2,1)}, bf16[2,128,1024]{1,2,0:T(8,128)(2,1)}, u32[]{:S(2)}, u32[]{:S(2)}) collective-permute-start(bf16[2,128,1024]{1,2,0:T(8,128)(2,1)} %pad_maximum_fusion.20), channel_id=1, source_target_pairs={{0,8},{4,12},{8,0},{12,4},{16,24},{20,28},{24,16},{28,20},{1,9},{5... | collective-permute-start | bytes 1572872 | tf_op jit(solution)/shard_map/ppermute | solution.py:233
  311.4 63.4 %collective-permute-start.20 = (bf16[512,1024]{1,0:T(8,128)(2,1)}, bf16[512,1024]{1,0:T(8,128)(2,1)}, u32[]{:S(2)}, u32[]{:S(2)}) collective-permute-start(bf16[512,1024]{1,0:T(8,128)(2,1)} %pad_maximum_fusion.10), channel_id=1, source_target_pairs={{0,1},{1,0},{2,3},{3,2},{4,5},{5,4},{6,7},{7,6},{8,9},{9,8},{10,11... | collective-permute-start | bytes 3145736 | tf_op jit(solution)/shard_map/ppermute | solution.py:233
  317.2 9.2 %collective-permute-start.58 = (f32[17,1024]{1,0:T(8,128)S(1)}, f32[17,1024]{1,0:T(8,128)S(1)}, u32[]{:S(2)}, u32[]{:S(2)}) collective-permute-start(f32[17,1024]{1,0:T(8,128)S(1)} %concatenate.150), channel_id=1, source_target_pairs={{0,1},{1,0},{2,3},{3,2},{4,5},{5,4},{6,7},{7,6},{8,9},{9,8},{10,11... | collective-permute-start | bytes 208904 | tf_op jit(solution)/shard_map/ppermute | solution.py:233
  326.4 5.0 %collective-permute-start.59 = (f32[17,1024]{1,0:T(8,128)S(1)}, f32[17,1024]{1,0:T(8,128)S(1)}, u32[]{:S(2)}, u32[]{:S(2)}) collective-permute-start(f32[17,1024]{1,0:T(8,128)S(1)} %add.665), channel_id=1, source_target_pairs={{0,2},{1,3},{2,0},{3,1},{4,6},{5,7},{6,4},{7,5},{8,10},{9,11},{10,... | collective-permute-start | bytes 208904 | tf_op jit(solution)/shard_map/ppermute | solution.py:233
  331.4 7.6 %collective-permute-start.60 = (f32[17,1024]{1,0:T(8,128)S(1)}, f32[17,1024]{1,0:T(8,128)S(1)}, u32[]{:S(2)}, u32[]{:S(2)}) collective-permute-start(f32[17,1024]{1,0:T(8,128)S(1)} %add.666), channel_id=1, source_target_pairs={{0,4},{4,0},{8,12},{12,8},{16,20},{20,16},{24,28},{28,24},{1,5},{5... | collective-permute-start | bytes 208904 | tf_op jit(solution)/shard_map/ppermute | solution.py:233
  339.0 4.7 collective-permute-start.61
  343.7 7.9 %collective-permute-start.62 = (f32[17,1024]{1,0:T(8,128)S(1)}, f32[17,1024]{1,0:T(8,128)}, u32[]{:S(2)}, u32[]{:S(2)}) collective-permute-start(f32[17,1024]{1,0:T(8,128)S(1)} %add.668), channel_id=1, source_target_pairs={{0,16},{4,20},{8,24},{12,28},{16,0},{20,4},{24,8},{28,12},{1,17},{... | collective-permute-start | bytes 208904 | tf_op jit(solution)/shard_map/ppermute | solution.py:233
  347.9 31.1 %collective-permute-start.31 = (bf16[4,128,1024]{2,1,0:T(8,128)(2,1)}, bf16[4,128,1024]{2,1,0:T(8,128)(2,1)}, u32[]{:S(2)}, u32[]{:S(2)}) collective-permute-start(bf16[4,128,1024]{2,1,0:T(8,128)(2,1)} %pad_maximum_fusion.12), channel_id=1, source_target_pairs={{0,4},{4,0},{8,12},{12,8},{16,20},{20,16},{24,28},{28,24},{1,5},{5... | collective-permute-start | bytes 3145736 | tf_op jit(solution)/shard_map/ppermute | solution.py:233
  354.9 11.9 %collective-permute-start.42 = (bf16[1,128,1024]{1,2,0:T(8,128)(2,1)S(1)}, bf16[1,128,1024]{1,2,0:T(8,128)(2,1)S(1)}, u32[]{:S(2)}, u32[]{:S(2)}) collective-permute-start(bf16[1,128,1024]{1,2,0:T(8,128)(2,1)S(1)} %pad_maximum_fusion.34), channel_id=1, source_target_pairs={{0,16},{4,20},{8,24},{12,28},{16,0},{20,4},{24,8},{28,12},{1,17},{... | collective-permute-start | bytes 786440 | tf_op jit(solution)/shard_map/ppermute | solution.py:233
  366.9 7.9 %collective-permute-start.44 = (bf16[128,1024]{0,1:T(8,128)(2,1)S(1)}, bf16[128,1024]{0,1:T(8,128)(2,1)S(1)}, u32[]{:S(2)}, u32[]{:S(2)}) collective-permute-start(bf16[128,1024]{0,1:T(8,128)(2,1)S(1)} %get-tuple-element.144), channel_id=1, source_target_pairs={{0,2},{1,3},{2,0},{3,1},{4,6},{5,7},{6,4},{7,5},{8,10},{9,11},{10,... | collective-permute-start | bytes 786440 | tf_op jit(solution)/shard_map/ppermute | solution.py:233
  367.9 16.1 %collective-permute-start.43 = (bf16[128,1024]{0,1:T(8,128)(2,1)S(1)}, bf16[128,1024]{0,1:T(8,128)(2,1)S(1)}, u32[]{:S(2)}, u32[]{:S(2)}) collective-permute-start(bf16[128,1024]{0,1:T(8,128)(2,1)S(1)} %get-tuple-element.144), channel_id=1, source_target_pairs={{0,1},{1,0},{2,3},{3,2},{4,5},{5,4},{6,7},{7,6},{8,9},{9,8},{10,11... | collective-permute-start | bytes 786440 | tf_op jit(solution)/shard_map/ppermute | solution.py:233
  373.1 55.2 %collective-permute-start.53 = (bf16[2,128,2048]{2,1,0:T(8,128)(2,1)}, bf16[2,128,2048]{2,1,0:T(8,128)(2,1)}, u32[]{:S(2)}, u32[]{:S(2)}) collective-permute-start(bf16[2,128,2048]{2,1,0:T(8,128)(2,1)} %pad_maximum_fusion.16), channel_id=1, source_target_pairs={{0,8},{4,12},{8,0},{12,4},{16,24},{20,28},{24,16},{28,20},{1,9},{5... | collective-permute-start | bytes 3145736 | tf_op jit(solution)/shard_map/ppermute | solution.py:233
  374.8 9.2 %collective-permute-start.45 = (bf16[128,1024]{0,1:T(8,128)(2,1)S(1)}, bf16[128,1024]{0,1:T(8,128)(2,1)S(1)}, u32[]{:S(2)}, u32[]{:S(2)}) collective-permute-start(bf16[128,1024]{0,1:T(8,128)(2,1)S(1)} %collective-permute-done.44), channel_id=1, source_target_pairs={{0,1},{1,0},{2,3},{3,2},{4,5},{5,4},{6,7},{7,6},{8,9},{9,8},{10,11... | collective-permute-start | bytes 786440 | tf_op jit(solution)/shard_map/ppermute | solution.py:233
  378.6 34.1 %collective-permute-start.21 = (bf16[256,1024]{1,0:T(8,128)(2,1)}, bf16[256,1024]{1,0:T(8,128)(2,1)}, u32[]{:S(2)}, u32[]{:S(2)}) collective-permute-start(bf16[256,1024]{1,0:T(8,128)(2,1)} %fusion.51), channel_id=1, source_target_pairs={{0,2},{1,3},{2,0},{3,1},{4,6},{5,7},{6,4},{7,5},{8,10},{9,11},{10,... | collective-permute-start | bytes 1572872 | tf_op jit(solution)/shard_map/ppermute | solution.py:233
  382.7 27.6 %collective-permute-start.32 = (bf16[2,128,1024]{2,1,0:T(8,128)(2,1)}, bf16[2,128,1024]{2,1,0:T(8,128)(2,1)}, u32[]{:S(2)}, u32[]{:S(2)}) collective-permute-start(bf16[2,128,1024]{2,1,0:T(8,128)(2,1)} %pad_maximum_fusion.19), channel_id=1, source_target_pairs={{0,8},{4,12},{8,0},{12,4},{16,24},{20,28},{24,16},{28,20},{1,9},{5... | collective-permute-start | bytes 1572872 | tf_op jit(solution)/shard_map/ppermute | solution.py:233
  412.6 14.4 %collective-permute-start.33 = (bf16[1,128,1024]{2,1,0:T(8,128)(2,1)S(1)}, bf16[1,128,1024]{2,1,0:T(8,128)(2,1)S(1)}, u32[]{:S(2)}, u32[]{:S(2)}) collective-permute-start(bf16[1,128,1024]{2,1,0:T(8,128)(2,1)S(1)} %pad_maximum_fusion.32), channel_id=1, source_target_pairs={{0,16},{4,20},{8,24},{12,28},{16,0},{20,4},{24,8},{28,12},{1,17},{... | collective-permute-start | bytes 786440 | tf_op jit(solution)/shard_map/ppermute | solution.py:233
  415.4 22.8 %collective-permute-start.23 = (bf16[256,1024]{1,0:T(8,128)(2,1)}, bf16[256,1024]{1,0:T(8,128)(2,1)}, u32[]{:S(2)}, u32[]{:S(2)}) collective-permute-start(bf16[256,1024]{1,0:T(8,128)(2,1)} %fusion.53), channel_id=1, source_target_pairs={{0,2},{1,3},{2,0},{3,1},{4,6},{5,7},{6,4},{7,5},{8,10},{9,11},{10,... | collective-permute-start | bytes 1572872 | tf_op jit(solution)/shard_map/ppermute | solution.py:233
  416.5 61.2 %collective-permute-start.22 = (bf16[256,1024]{1,0:T(8,128)(2,1)}, bf16[256,1024]{1,0:T(8,128)(2,1)}, u32[]{:S(2)}, u32[]{:S(2)}) collective-permute-start(bf16[256,1024]{1,0:T(8,128)(2,1)} %fusion.53), channel_id=1, source_target_pairs={{0,1},{1,0},{2,3},{3,2},{4,5},{5,4},{6,7},{7,6},{8,9},{9,8},{10,11... | collective-permute-start | bytes 1572872 | tf_op jit(solution)/shard_map/ppermute | solution.py:233
  427.1 8.3 %collective-permute-start.35 = (bf16[128,1024]{1,0:T(8,128)(2,1)S(1)}, bf16[128,1024]{1,0:T(8,128)(2,1)S(1)}, u32[]{:S(2)}, u32[]{:S(2)}) collective-permute-start(bf16[128,1024]{1,0:T(8,128)(2,1)S(1)} %get-tuple-element.148), channel_id=1, source_target_pairs={{0,2},{1,3},{2,0},{3,1},{4,6},{5,7},{6,4},{7,5},{8,10},{9,11},{10,... | collective-permute-start | bytes 786440 | tf_op jit(solution)/shard_map/ppermute | solution.py:233
  428.3 10.1 %collective-permute-start.34 = (bf16[128,1024]{1,0:T(8,128)(2,1)S(1)}, bf16[128,1024]{1,0:T(8,128)(2,1)S(1)}, u32[]{:S(2)}, u32[]{:S(2)}) collective-permute-start(bf16[128,1024]{1,0:T(8,128)(2,1)S(1)} %get-tuple-element.148), channel_id=1, source_target_pairs={{0,1},{1,0},{2,3},{3,2},{4,5},{5,4},{6,7},{7,6},{8,9},{9,8},{10,11... | collective-permute-start | bytes 786440 | tf_op jit(solution)/shard_map/ppermute | solution.py:233
  435.4 3.0 collective-permute-start.36
  436.3 26.1 %collective-permute-start.54 = (bf16[1,128,2048]{2,1,0:T(8,128)(2,1)}, bf16[1,128,2048]{2,1,0:T(8,128)(2,1)}, u32[]{:S(2)}, u32[]{:S(2)}) collective-permute-start(bf16[1,128,2048]{2,1,0:T(8,128)(2,1)} %pad_maximum_fusion.21), channel_id=1, source_target_pairs={{0,16},{4,20},{8,24},{12,28},{16,0},{20,4},{24,8},{28,12},{1,17},{... | collective-permute-start | bytes 1572872 | tf_op jit(solution)/shard_map/ppermute | solution.py:233
  438.2 39.6 %collective-permute-start.24 = (bf16[256,1024]{1,0:T(8,128)(2,1)}, bf16[256,1024]{1,0:T(8,128)(2,1)}, u32[]{:S(2)}, u32[]{:S(2)}) collective-permute-start(bf16[256,1024]{1,0:T(8,128)(2,1)} %collective-permute-done.23), channel_id=1, source_target_pairs={{0,1},{1,0},{2,3},{3,2},{4,5},{5,4},{6,7},{7,6},{8,9},{9,8},{10,11... | collective-permute-start | bytes 1572872 | tf_op jit(solution)/shard_map/ppermute | solution.py:233
  463.7 14.1 %collective-permute-start.56 = (bf16[128,2048]{1,0:T(8,128)(2,1)S(1)}, bf16[128,2048]{1,0:T(8,128)(2,1)}, u32[]{:S(2)}, u32[]{:S(2)}) collective-permute-start(bf16[128,2048]{1,0:T(8,128)(2,1)S(1)} %get-tuple-element.110), channel_id=1, source_target_pairs={{0,2},{1,3},{2,0},{3,1},{4,6},{5,7},{6,4},{7,5},{8,10},{9,11},{10,... | collective-permute-start | bytes 1572872 | tf_op jit(solution)/shard_map/ppermute | solution.py:233
  466.2 16.1 %collective-permute-start.55 = (bf16[128,2048]{1,0:T(8,128)(2,1)S(1)}, bf16[128,2048]{1,0:T(8,128)(2,1)S(1)}, u32[]{:S(2)}, u32[]{:S(2)}) collective-permute-start(bf16[128,2048]{1,0:T(8,128)(2,1)S(1)} %get-tuple-element.110), channel_id=1, source_target_pairs={{0,1},{1,0},{2,3},{3,2},{4,5},{5,4},{6,7},{7,6},{8,9},{9,8},{10,11... | collective-permute-start | bytes 1572872 | tf_op jit(solution)/shard_map/ppermute | solution.py:233
  477.8 4.5 collective-permute-start.57
  (82 other events, 450.8 us)

commit v2 on v1

--- a/solution.py
+++ b/solution.py
@@ -228,44 +228,297 @@
     )(info, q, k, v, g, g, g, g, bias)
 
 
+def pick_kernel(info, in_ref, out_ref):
+    out_ref[...] = in_ref[...]
+
+
+def pick_columns(matrix, size, count, stride, offset):
+    rows = matrix.shape[0]
+    return pl.pallas_call(
+        pick_kernel,
+        out_shape=jax.ShapeDtypeStruct((rows, size * count), matrix.dtype),
+        grid_spec=pltpu.PrefetchScalarGridSpec(
+            num_scalar_prefetch=1,
+            grid=(count,),
+            in_specs=[pl.BlockSpec((rows, size), lambda n, s: (0, n * stride + s[0]))],
+            out_specs=pl.BlockSpec((rows, size), lambda n, s: (0, n)),
+        ),
+        cost_estimate=pl.CostEstimate(flops=0, bytes_accessed=4 * rows * size * count, transcendentals=0),
+        name="pick_columns",
+    )(offset.astype(jnp.int32).reshape(1), matrix)
+
+
 def swap(part, axis, distance):
     count = lax.axis_size(axis)
     return lax.ppermute(part, axis, [(i, i ^ distance) for i in range(count)])
 
 
-def gather_rel(part):
-    core = swap(part, "mem", 1)
-    across = swap(part, "mem", 2)
-    return [part, core, across, swap(across, "mem", 1)]
-
-
-def scatter_dp(parts):
-    count = lax.axis_size("dp")
-    me = lax.axis_index("dp")
-    kept = [a.reshape(count, a.shape[0] // count, a.shape[1]) for a in parts]
-    widths = [a.shape[1] for a in parts]
-    distance = 1
-    while count > 1:
+ORDER = (0, 2, 1, 3)
+
+
+def gather_rows(part):
+    pair = jnp.concatenate([part, swap(part, "mem", 2)], axis=0)
+    return jnp.concatenate([pair, swap(pair, "mem", 1)], axis=0)
+
+
+def bits_of(count, first):
+    every = [1 << i for i in range(count.bit_length() - 1)]
+    return [first] + [d for d in every if d != first]
+
+
+class Halving:
+    def __init__(self, parts, first):
+        count = lax.axis_size("dp")
+        self.dims = [count]
+        self.kept = [a.reshape(count, a.shape[0] // count, a.shape[1]) for a in parts]
+        self.left = bits_of(count, first)
+        self.done_bits = []
+        self.count = count
+
+    def send(self):
+        me = lax.axis_index("dp")
+        distance = self.left[0]
+        below = sum(1 for d in self.left if d < distance)
+        low_size = 1 << below
         bit = (me // distance) % 2
-        halves = [a.reshape(count // 2, 2, a.shape[1], a.shape[2]) for a in kept]
-        mine = [lax.dynamic_index_in_dim(a, bit, 1, False) for a in halves]
-        theirs = [lax.dynamic_index_in_dim(a, 1 - bit, 1, False).astype(low) for a in halves]
-        got = swap(jnp.concatenate(theirs, axis=2), "dp", distance)
-        start, kept = 0, []
-        for a, w in zip(mine, widths):
-            kept.append(a + got[:, :, start : start + w].astype(jnp.float32))
-            start += w
-        count, distance = count // 2, distance * 2
-    return [a[0] for a in kept]
-
-
-def sum_all(vector):
-    for axis in ("mem", "dp"):
-        distance = 1
-        while distance < lax.axis_size(axis):
-            vector = vector + swap(vector, axis, distance)
-            distance *= 2
-    return vector
+        self.mine, theirs = [], []
+        for a in self.kept:
+            n, r, w = a.shape
+            split = a.reshape(n // (2 * low_size), 2, low_size, r, w)
+            self.mine.append(lax.dynamic_index_in_dim(split, bit, 1, False).reshape(n // 2, r, w))
+            theirs.append(lax.dynamic_index_in_dim(split, 1 - bit, 1, False).reshape(n // 2, r, w))
+        return jnp.concatenate([t.astype(low) for t in theirs], axis=2)
+
+    def move(self, sent):
+        return swap(sent, "dp", self.left.pop(0))
+
+    def add(self, got):
+        start, self.kept = 0, []
+        for a in self.mine:
+            self.kept.append(a + got[:, :, start : start + a.shape[2]].astype(jnp.float32))
+            start += a.shape[2]
+
+    def step(self):
+        self.add(self.move(self.send()))
+
+    def finish(self):
+        while self.left:
+            self.step()
+        return [a[0] for a in self.kept]
+
+
+def tie(*values):
+    return lax.optimization_barrier(values)
+
+
+def finale_kernel(a_ref, b_ref, f_ref, g_ref, h_ref, v_ref,
+                  oa_ref, ob_ref, of_ref, og_ref, ov_ref,
+                  ay, by, az, bz, gc, gs, gx, vs, vc, vx, vy, vz, send, recv):
+    dp, mem = lax.axis_index("dp"), lax.axis_index("mem")
+    y, row = dp % 2, dp // 2
+    chip, core = mem // 2, mem % 2
+    groups = b_ref.shape[0]
+    far = a_ref.shape[0]
+
+    def quarter_of(m):
+        return 2 * (m % 2) + m // 2
+
+    def block_of(m):
+        return (m // 2) + (m % 2) * (3 - 2 * (m // 2))
+
+    barrier = pltpu.get_barrier_semaphore()
+    peers = [{"mem": mem ^ 1}, {"mem": mem ^ 2}, {"dp": dp ^ 1}]
+    peers += [{"dp": (row ^ j) * 2 + y} for j in range(1, groups)]
+    for peer in peers:
+        pl.semaphore_signal(barrier, inc=1, device_id=peer, device_id_type=pl.DeviceIdType.MESH)
+    pl.semaphore_wait(barrier, len(peers))
+
+    count = [0]
+    sent = []
+
+    def start(src, dst, peer):
+        n = count[0]
+        count[0] += 1
+        copy = pltpu.make_async_remote_copy(
+            src_ref=src, dst_ref=dst, send_sem=send.at[n], recv_sem=recv.at[n],
+            device_id=peer, device_id_type=pl.DeviceIdType.MESH,
+        )
+        copy.start()
+        sent.append(copy)
+        return copy
+
+    core_peer, chip_peer, y_peer = peers[:3]
+    f32 = jnp.float32
+
+    copy_ay = start(a_ref.at[:, 1 - y], ay, y_peer)
+    copy_by = start(b_ref.at[:, 1 - y], by, y_peer)
+    mine_q = quarter_of(mem)
+    of_ref[mine_q] = f_ref[...]
+    copy_fx = start(f_ref, of_ref.at[mine_q], chip_peer)
+    copy_fc = start(f_ref, of_ref.at[mine_q], core_peer)
+    copy_g1 = start(g_ref.at[block_of(mem ^ 1)], gc.at[0], core_peer)
+    copy_g3 = start(g_ref.at[block_of(mem ^ 3)], gc.at[1], core_peer)
+    copy_vc = start(v_ref, vc, core_peer)
+
+    copy_g3.wait_recv()
+    gs[...] = (g_ref[block_of(mem ^ 2)].astype(f32) + gc[1].astype(f32)).astype(low)
+    copy_gx = start(gs, gx, chip_peer)
+    copy_vc.wait_recv()
+    vs[0] = v_ref[...] + vc[...]
+    copy_vx = start(vs.at[0], vx, chip_peer)
+    copy_g1.wait_recv()
+
+    copy_vx.wait_recv()
+    vs[1] = vs[0] + vx[...]
+    copy_vy = start(vs.at[1], vy, y_peer)
+
+    copy_ay.wait_recv()
+    own_far = row // 2
+    for t in range(far):
+        ay[t] = (ay[t].astype(f32) + a_ref[t, y].astype(f32)).astype(low)
+    az[own_far] = ay[own_far]
+    copies_az = [
+        start(ay.at[own_far ^ j], az.at[own_far], {"dp": ((own_far ^ j) * 2 + row % 2) * 2 + y})
+        for j in range(1, far)
+    ]
+    copy_vy.wait_recv()
+    vs[2] = vs[1] + vy[...]
+    vz[row] = vs[2]
+    copies_vz = [start(vs.at[2], vz.at[row], {"dp": (row ^ j) * 2 + y}) for j in range(1, groups)]
+    copy_gx.wait_recv()
+    block = block_of(mem)
+    total = h_ref[...] + g_ref[block].astype(f32) + gc[0].astype(f32) + gx[...].astype(f32)
+    og_ref[block] = total.astype(low)
+    copy_gax = start(og_ref.at[block], og_ref.at[block], chip_peer)
+    copy_gac = start(og_ref.at[block], og_ref.at[block], core_peer)
+    copy_by.wait_recv()
+    for t in range(groups):
+        by[t] = (by[t].astype(f32) + b_ref[t, y].astype(f32)).astype(low)
+    bz[row] = by[row]
+    copies_bz = [start(by.at[row ^ j], bz.at[row], {"dp": (row ^ j) * 2 + y}) for j in range(1, groups)]
+
+    other_q = quarter_of(mem ^ 2)
+    copy_fx.wait_recv()
+    copy_fr = start(of_ref.at[other_q], of_ref.at[other_q], core_peer)
+    for copy in copies_az:
+        copy.wait_recv()
+    total = az[0].astype(f32)
+    for t in range(1, far):
+        total = total + az[t].astype(f32)
+    oa_ref[mine_q] = total.astype(low)
+    copy_aax = start(oa_ref.at[mine_q], oa_ref.at[mine_q], chip_peer)
+    copy_aac = start(oa_ref.at[mine_q], oa_ref.at[mine_q], core_peer)
+    copy_gax.wait_recv()
+    other = block_of(mem ^ 2)
+    copy_gr = start(og_ref.at[other], og_ref.at[other], core_peer)
+    for copy in copies_vz:
+        copy.wait_recv()
+    total = vz[0]
+    for t in range(1, groups):
+        total = total + vz[t]
+    ov_ref[...] = total
+    for copy in copies_bz:
+        copy.wait_recv()
+    total = bz[0].astype(f32)
+    for t in range(1, groups):
+        total = total + bz[t].astype(f32)
+    ob_ref[mine_q] = total.astype(low)
+    copy_bax = start(ob_ref.at[mine_q], ob_ref.at[mine_q], chip_peer)
+    copy_bac = start(ob_ref.at[mine_q], ob_ref.at[mine_q], core_peer)
+    copy_aax.wait_recv()
+    copy_ar = start(oa_ref.at[other_q], oa_ref.at[other_q], core_peer)
+    copy_bax.wait_recv()
+    copy_br = start(ob_ref.at[other_q], ob_ref.at[other_q], core_peer)
+    for copy in (copy_fc, copy_gac, copy_aac, copy_bac, copy_fr, copy_gr, copy_ar, copy_br):
+        copy.wait_recv()
+    for copy in sent:
+        copy.wait_send()
+
+
+def finale(a, b, f, g, h, v):
+    far, groups = a.shape[0], b.shape[0]
+    r, wa, wb, wf = a.shape[2], a.shape[3], b.shape[3], f.shape[1]
+    copies = 17 + (far - 1) + 2 * (groups - 1) + 4
+    vmem = pl.BlockSpec(memory_space=pltpu.VMEM)
+    f32 = jnp.float32
+    return pl.pallas_call(
+        finale_kernel,
+        out_shape=[
+            jax.ShapeDtypeStruct((4, r, wa), low),
+            jax.ShapeDtypeStruct((4, r, wb), low),
+            jax.ShapeDtypeStruct((4, r, wf), low),
+            jax.ShapeDtypeStruct(g.shape, low),
+            jax.ShapeDtypeStruct(v.shape, f32),
+        ],
+        in_specs=[vmem] * 6,
+        out_specs=[vmem] * 5,
+        scratch_shapes=[
+            pltpu.VMEM((far, r, wa), low),
+            pltpu.VMEM((groups, r, wb), low),
+            pltpu.VMEM((far, r, wa), low),
+            pltpu.VMEM((groups, r, wb), low),
+            pltpu.VMEM((2,) + g.shape[1:], low),
+            pltpu.VMEM(g.shape[1:], low),
+            pltpu.VMEM(g.shape[1:], low),
+            pltpu.VMEM((3,) + v.shape, f32),
+            pltpu.VMEM(v.shape, f32),
+            pltpu.VMEM(v.shape, f32),
+            pltpu.VMEM(v.shape, f32),
+            pltpu.VMEM((groups,) + v.shape, f32),
+            pltpu.SemaphoreType.DMA((copies,)),
+            pltpu.SemaphoreType.DMA((copies,)),
+        ],
+        compiler_params=pltpu.CompilerParams(
+            collective_id=0, has_side_effects=True, vmem_limit_bytes=VMEM_LIMIT
+        ),
+        cost_estimate=pl.CostEstimate(flops=10**6, bytes_accessed=10**8, transcendentals=0),
+        name="finale",
+    )(a, b, f, g, h, v)
+
+
+def unpack_kernel(a_ref, b_ref, f_ref, g_ref, qkv_ref, so_ref, cq_ref, ckv_ref, co_ref, fi_ref, fo_ref, gd_ref, *, quarter, piece):
+    f32 = jnp.float32
+
+    def spread(source, start, count, size, target):
+        for p in range(4):
+            for n in range(count):
+                target[:, (n * 4 + p) * size : (n * 4 + p + 1) * size] = source[
+                    p, :, start + n * size : start + (n + 1) * size
+                ].astype(f32)
+
+    spread(b_ref, 0, 3, quarter, qkv_ref)
+    spread(a_ref, 0, 1, quarter, co_ref)
+    spread(a_ref, quarter, 1, quarter, cq_ref)
+    spread(a_ref, 2 * quarter, 2, quarter, ckv_ref)
+    spread(a_ref, 4 * quarter, 1, quarter, so_ref)
+    spread(f_ref, 0, quarter * 4 // piece, piece, fi_ref)
+    for p in range(4):
+        fo_ref[p] = f_ref[p, :, 4 * quarter :].astype(f32)
+        gd_ref[p] = g_ref[p].astype(f32)
+
+
+def unpack(a, b, f, g, width, hidden, piece):
+    r = a.shape[1]
+    steps = 4 if r % 64 == 0 else 1
+    h, gh = r // steps, g.shape[1] // steps
+    f32 = jnp.float32
+
+    def slots(x, n):
+        return pl.BlockSpec((4, n, x.shape[2]), lambda i: (0, i, 0))
+
+    wide = [3 * width, width, width, 2 * width, width, hidden]
+    return pl.pallas_call(
+        functools.partial(unpack_kernel, quarter=width // 4, piece=piece),
+        out_shape=[jax.ShapeDtypeStruct((r, w), f32) for w in wide]
+        + [jax.ShapeDtypeStruct((4, r, width), f32), jax.ShapeDtypeStruct(g.shape, f32)],
+        grid=(steps,),
+        in_specs=[slots(a, h), slots(b, h), slots(f, h), slots(g, gh)],
+        out_specs=[pl.BlockSpec((h, w), lambda i: (i, 0)) for w in wide]
+        + [pl.BlockSpec((4, h, width), lambda i: (0, i, 0)), slots(g, gh)],
+        compiler_params=pltpu.CompilerParams(vmem_limit_bytes=VMEM_LIMIT),
+        cost_estimate=pl.CostEstimate(flops=10**6, bytes_accessed=2 * 10**7, transcendentals=0),
+        name="unpack",
+    )(a, b, f, g)
 
 
 def per_device(
@@ -301,43 +554,43 @@
     def block_of(m):
         return jnp.where(m // 2 == 0, 3 * (m % 2), 1 + m % 2)
 
-    def columns_half(w, count):
-        piece = w.reshape(w.shape[0], count, 2, half)
-        return lax.dynamic_index_in_dim(piece, core, 2, False).reshape(w.shape[0], count * half)
-
-    def columns_quarter(w, count):
-        piece = w.reshape(w.shape[0], count, 4, quarter)
-        return lax.dynamic_index_in_dim(piece, quart, 2, False).reshape(w.shape[0], count * quarter)
+    def cut(a, start, size, axis=1):
+        return lax.dynamic_slice_in_dim(a, start, size, axis)
 
     def own_rows(a):
-        return lax.dynamic_slice_in_dim(a, block_of(me) * block, block, 0)
-
-    def by_block(slots):
-        stacked = jnp.stack(slots)
-        order = [0, 2, 3, 1]
-        return jnp.concatenate(
-            [lax.dynamic_index_in_dim(stacked, me ^ order[n], 0, False) for n in range(4)], axis=0
-        )
+        return cut(a, block_of(me) * block, block, 0)
+
+    def by_block(gathered):
+        size = gathered.shape[0] // 4
+        where = [0, 2, 3, 1]
+        pieces = []
+        for n in range(4):
+            offset = me ^ where[n]
+            slot = (offset % 2) * 2 + offset // 2
+            pieces.append(cut(gathered, slot * size, size, 0))
+        return jnp.concatenate(pieces, axis=0)
 
     def by_quarter(slots):
         stacked = jnp.stack(slots)
-        order = [0, 2, 1, 3]
-        return [lax.dynamic_index_in_dim(stacked, me ^ order[n], 0, False) for n in range(4)]
-
-    mem_full = jnp.concatenate(gather_rel(mem_rows), axis=0)
-
-    qkv8 = product(x_full, columns_half(self_qkv, 3))
-    bias_q8 = lax.dynamic_slice_in_dim(proj_bias[0], core * half, half)
-    bias_v8 = lax.dynamic_slice_in_dim(proj_bias[1], core * half, half)
-    q8 = ((qkv8[:, :half] + bias_q8) * 0.125).astype(low)
-    k8 = qkv8[:, half : 2 * half].astype(low)
-    v8 = (qkv8[:, 2 * half :] + bias_v8).astype(low)
+        where = [0, 2, 1, 3]
+        out = []
+        for n in range(4):
+            offset = me ^ where[n]
+            out.append(lax.dynamic_index_in_dim(stacked, (offset % 2) * 2 + offset // 2, 0, False))
+        return out
+
+    mem_full = gather_rows(mem_rows)
+
+    side = core * half
+    q8 = ((product(x_full, cut(self_qkv, side, half)) + cut(proj_bias[0], side, half, 0)) * 0.125).astype(low)
+    k8 = product(x_full, cut(self_qkv, width + side, half)).astype(low)
+    v8 = (product(x_full, cut(self_qkv, 2 * width + side, half)) + cut(proj_bias[1], side, half, 0)).astype(low)
     info_f = jnp.stack([chip, dec_len[0]]).astype(jnp.int32)
     att8 = self_forward(info_f, q8, k8, v8)
 
     def heads_to_rows(a8):
-        mine = lax.dynamic_slice_in_dim(a8, core * block, block, 0)
-        other = swap(lax.dynamic_slice_in_dim(a8, (1 - core) * block, block, 0), "mem", 1)
+        mine = cut(a8, core * block, block, 0)
+        other = swap(cut(a8, (1 - core) * block, block, 0), "mem", 1)
         return jnp.where(
             core == 0, jnp.concatenate([mine, other], axis=1), jnp.concatenate([other, mine], axis=1)
         )
@@ -348,22 +601,17 @@
         x_own + product(attended, self_out) + proj_bias[2], norm_gain[0], norm_shift[0]
     )
     first_low = first.astype(low)
-    first_slots = gather_rel(first_low)
-    first_chip = jnp.concatenate(
-        [
-            jnp.where(core == 0, first_slots[0], first_slots[1]),
-            jnp.where(core == 0, first_slots[1], first_slots[0]),
-        ],
-        axis=0,
-    )
-
-    bias_cq8 = lax.dynamic_slice_in_dim(proj_bias[3], core * half, half)
-    cq8 = ((product(first_chip, columns_half(cross_q, 1)) + bias_cq8) * 0.125).astype(low)
-    kv8 = product(mem_full, columns_half(cross_kv, 2))
-    bias_cv8 = lax.dynamic_slice_in_dim(proj_bias[4], core * half, half)
-    kc8 = kv8[:, :half].astype(low)
-    vc8 = (kv8[:, half:] + bias_cv8).astype(low)
-    slot_pos = jnp.stack([(me ^ k) * mem_block for k in range(4)])
+    first_other = swap(first_low, "mem", 1)
+    first_chip = jnp.where(
+        core == 0,
+        jnp.concatenate([first_low, first_other], axis=0),
+        jnp.concatenate([first_other, first_low], axis=0),
+    )
+
+    cq8 = ((product(first_chip, cut(cross_q, side, half)) + cut(proj_bias[3], side, half, 0)) * 0.125).astype(low)
+    kc8 = product(mem_full, cut(cross_kv, side, half)).astype(low)
+    vc8 = (product(mem_full, cut(cross_kv, width + side, half)) + cut(proj_bias[4], side, half, 0)).astype(low)
+    slot_pos = jnp.stack([(me ^ k) * mem_block for k in ORDER])
     mem_pos = (slot_pos[:, None] + jnp.arange(mem_block, dtype=jnp.int32)[None, :]).reshape(-1)
     mem_bias = jnp.where(mem_pos < mem_len[0], 0.0, neg_fill).astype(jnp.float32)
     crossed = heads_to_rows(cross_forward(cq8, kc8, vc8, mem_bias[None, :]))
@@ -387,94 +635,101 @@
     )
     dco = dh2.astype(low)
 
-    second_full = jnp.concatenate(gather_rel(second_low), axis=0)
-    dz_full = jnp.concatenate(gather_rel(dz), axis=0)
-    dco_full = jnp.concatenate(gather_rel(dco), axis=0)
+    second_full = gather_rows(second_low)
+    dz_full = gather_rows(dz)
+    dco_full = gather_rows(dco)
     piece = hidden // groups // 4
-    w_in_q = lax.dynamic_index_in_dim(ffn_in.reshape(width, groups, 4, piece), quart, 2, False).reshape(
-        width, hidden // 4
-    )
-    w_out_q = lax.dynamic_index_in_dim(ffn_out.reshape(groups, 4, piece, width), quart, 1, False).reshape(
-        hidden // 4, width
-    )
+    if piece % 128 == 0:
+        w_in_q = pick_columns(ffn_in, piece, groups, 4, quart)
+    else:
+        w_in_q = lax.dynamic_index_in_dim(ffn_in.reshape(width, groups, 4, piece), quart, 2, False)
+        w_in_q = w_in_q.reshape(width, hidden // 4)
+    w_out_q = lax.dynamic_index_in_dim(ffn_out.reshape(groups, 4, piece, width), quart, 1, False)
+    w_out_q = w_out_q.reshape(hidden // 4, width)
     b_in_q = lax.dynamic_index_in_dim(ffn_bias.reshape(groups, 4, piece), quart, 1, False).reshape(-1)
     act_q, slope_q = gelu_parts(product(second_full, w_in_q) + b_in_q)
     act_q = act_q.astype(low)
     du_q = (product_nt(dz_full, w_out_q) * slope_q).astype(low)
-    g_in, g_out = scatter_dp([product_tn(second_full, du_q), product_tn(act_q, dz_full)])
-
-    first_full = jnp.concatenate(first_slots, axis=0)
-    bias_cq4 = lax.dynamic_slice_in_dim(proj_bias[3], quart * quarter, quarter)
-    cq4 = ((product(first_full, columns_quarter(cross_q, 1)) + bias_cq4) * 0.125).astype(low)
-    cross_out_q = lax.dynamic_slice_in_dim(cross_out, quart * quarter, quarter, 0)
-    dx4 = product_nt(dco_full, cross_out_q).astype(low)
+    sum_in = Halving([product_tn(second_full, du_q)], 1)
+    sum_out = Halving([product_tn(act_q, dz_full)], min(2, groups // 2))
+    send_in, send_out = sum_in.send(), sum_out.send()
+
+    first_full = gather_rows(first_low)
+    wide = quart * quarter
+    cq4 = ((product(first_full, cut(cross_q, wide, quarter)) + cut(proj_bias[3], wide, quarter, 0)) * 0.125).astype(low)
+    dx4 = product_nt(dco_full, cut(cross_out, wide, quarter, 0)).astype(low)
     pair_base = chip * (quarter // 128)
     info_c = jnp.stack([pair_base]).astype(jnp.int32)
     bias_col = jnp.broadcast_to(mem_bias[:, None], (mem_bias.shape[0], 128))
+    dx4, send_in, send_out = tie(dx4, send_in, send_out)
+    got_in, got_out = sum_in.move(send_in), sum_out.move(send_out)
     dq4, dkc4, dvc4 = attention_back(info_c, cq4, kc8, vc8, dx4, bias_col, False)
+    dq4, dkc4, dvc4, got_in, got_out = tie(dq4, dkc4, dvc4, got_in, got_out)
+    sum_in.add(got_in)
+    sum_out.add(got_out)
     dkv4 = jnp.concatenate([dkc4, dvc4], axis=1)
 
-    def to_rows(a, size):
-        slots = [a[k * size : (k + 1) * size] for k in range(4)]
-        return by_quarter([slots[0]] + [swap(slots[k], "mem", k) for k in (1, 2, 3)])
-
-    dq_own = jnp.concatenate(to_rows(dq4, block), axis=1)
-    dkv_parts = to_rows(dkv4, mem_block)
+    def to_rows(a):
+        b0, b2, b1, b3 = jnp.split(a, 4, axis=0)
+        over = swap(jnp.concatenate([b2, b3], axis=0), "mem", 2)
+        size = b0.shape[0]
+        mine = jnp.concatenate([b0, over[:size]], axis=0)
+        other = swap(jnp.concatenate([b1, over[size:]], axis=0), "mem", 1)
+        return by_quarter([mine[:size], mine[size:], other[:size], other[size:]])
+
+    dq_own = jnp.concatenate(to_rows(dq4), axis=1)
+    dkv_parts = to_rows(dkv4)
     dkv_own = jnp.concatenate(
         [a[:, :quarter] for a in dkv_parts] + [a[:, quarter:] for a in dkv_parts], axis=1
     )
     grad_memory = product_nt(dkv_own, cross_kv)[None]
-    crossed_full = jnp.concatenate(gather_rel(crossed), axis=0)
-    dco_q = lax.dynamic_slice_in_dim(dco_full, quart * quarter, quarter, 1)
-    g_co, g_cq, g_ckv = scatter_dp(
-        [product_tn(crossed_full, dco_q), product_tn(first_full, dq4), product_tn(mem_full, dkv4)]
-    )
+    crossed_full = gather_rows(crossed)
+    attended_full = gather_rows(attended)
+    send_in, send_out = sum_in.send(), sum_out.send()
+    got_in, got_out = sum_in.move(send_in), sum_out.move(send_out)
 
     dh1, gain_one, shift_one = norm_back(
         dh2 + product_nt(dq_own, cross_q), first_norm, first_inv, norm_gain[0]
     )
     do = dh1.astype(low)
-    do_full = jnp.concatenate(gather_rel(do), axis=0)
-
-    self_out_q = lax.dynamic_slice_in_dim(self_out, quart * quarter, quarter, 0)
-    da4 = product_nt(do_full, self_out_q).astype(low)
-    order = [0, 2, 3, 1]
-    info_s = jnp.stack([pair_base, dec_len[0]] + [me ^ order[n] for n in range(4)]).astype(jnp.int32)
+    do_full = gather_rows(do)
+    sum_cross = Halving(
+        [
+            product_tn(crossed_full, cut(dco_full, wide, quarter)),
+            product_tn(first_full, dq4),
+            product_tn(mem_full, dkv4),
+            product_tn(attended_full, cut(do_full, wide, quarter)),
+        ],
+        min(2, groups // 2),
+    )
+    send_cross = sum_cross.send()
+
+    da4 = product_nt(do_full, cut(self_out, wide, quarter, 0)).astype(low)
+    where = [0, 2, 3, 1]
+    slots = [((me ^ n) % 2) * 2 + (me ^ n) // 2 for n in where]
+    info_s = jnp.stack([pair_base, dec_len[0]] + slots).astype(jnp.int32)
+    da4, got_in, got_out, send_cross = tie(da4, got_in, got_out, send_cross)
+    sum_in.add(got_in)
+    sum_out.add(got_out)
+    send_in, send_out = sum_in.send(), sum_out.send()
+    da4, send_in, send_out = tie(da4, send_in, send_out)
+    got_in, got_out, got_cross = sum_in.move(send_in), sum_out.move(send_out), sum_cross.move(send_cross)
     sq4, sk4, sv4 = attention_back(info_s, q8, k8, v8, da4, bias_col[:8], True)
+    sq4, sk4, sv4, got_in, got_out, got_cross = tie(sq4, sk4, sv4, got_in, got_out, got_cross)
+    sum_in.add(got_in)
+    sum_out.add(got_out)
+    sum_cross.add(got_cross)
+    (g_in,), (g_out,) = sum_in.finish(), sum_out.finish()
+
     dqkv4 = jnp.concatenate([sq4, sk4, sv4], axis=1)
-    qkv_q = columns_quarter(self_qkv, 3)
-    partial = product_nt(dqkv4, qkv_q).reshape(4, block, width)
-
-    def rows_for(m):
-        return lax.dynamic_index_in_dim(partial, block_of(m), 0, False)
-
-    sent = jnp.concatenate([rows_for(me ^ 1).astype(low), rows_for(me ^ 3).astype(low)], axis=0)
-    got = swap(sent, "mem", 1).astype(jnp.float32)
-    across = swap((rows_for(me ^ 2) + got[block:]).astype(low), "mem", 2).astype(jnp.float32)
-    grad_own = (dh1 + rows_for(me) + got[:block] + across).astype(low)
-    grad_dec = by_block(gather_rel(grad_own)).astype(jnp.float32)[None]
-    layer_out = by_block(gather_rel(third.astype(low)))[None]
-
-    attended_full = jnp.concatenate(gather_rel(attended), axis=0)
-    do_q = lax.dynamic_slice_in_dim(do_full, quart * quarter, quarter, 1)
-    g_qkv, g_so = scatter_dp([product_tn(x_full, dqkv4), product_tn(attended_full, do_q)])
-
-    def gather_parts(parts):
-        packed = jnp.concatenate([a.astype(low) for a in parts], axis=1)
-        slots = by_quarter(gather_rel(packed))
-        out, start = [], 0
-        for a in parts:
-            out.append([s[:, start : start + a.shape[1]].astype(jnp.float32) for s in slots])
-            start += a.shape[1]
-        return out
-
-    in_parts, out_parts = gather_parts([g_in, g_out])
-    co_parts, cq_parts, ckv_parts = gather_parts([g_co, g_cq, g_ckv])
-    qkv_parts, so_parts = gather_parts([g_qkv, g_so])
-
-    def interleave(parts, count):
-        r = parts[0].shape[0]
-        return jnp.stack([p.reshape(r, count, -1) for p in parts], axis=2).reshape(r, -1)
+    per = width // groups
+    qkv_grad = product_tn(x_full, dqkv4).astype(low).reshape(groups // 2, 2, per, 3 * quarter)
+    qkv_q = jnp.concatenate([cut(self_qkv, n * width + wide, quarter) for n in range(3)], axis=1)
+    partial = product_nt(dqkv4, qkv_q).astype(low).reshape(4, block, width)
+    cross_grad = jnp.concatenate([part.astype(low) for part in sum_cross.kept], axis=2)
+    cross_grad = cross_grad.reshape(groups // 4, 2, per, cross_grad.shape[2])
+    ffn_grad = jnp.concatenate([g_in.astype(low), g_out.astype(low)], axis=1)
+    layer_out = by_block(gather_rows(third.astype(low)))[None]
 
     place = jnp.zeros((2, width), jnp.float32)
     own_sums = jnp.stack([column_sum(sq4), column_sum(sv4)])
@@ -501,20 +756,24 @@
         ],
         axis=0,
     )
-    packed = sum_all(packed)
+    packed = jnp.pad(packed, ((0, -packed.shape[0] % 8), (0, 0)))
+    cross_w, qkv_w, ffn_w, grad_rows, packed = finale(cross_grad, qkv_grad, ffn_grad, partial, dh1, packed)
+    w_qkv, w_so, w_cq, w_ckv, w_co, w_fi, w_fo, grad_dec = unpack(
+        cross_w, qkv_w, ffn_w, grad_rows, width, hidden, piece
+    )
     return (
         layer_out,
-        grad_dec,
+        grad_dec.reshape(1, rows, width),
         grad_memory,
-        interleave(qkv_parts, 3),
-        interleave(so_parts, 1),
-        interleave(cq_parts, 1),
-        interleave(ckv_parts, 2),
-        interleave(co_parts, 1),
-        interleave(in_parts, groups),
-        jnp.concatenate(out_parts, axis=0),
+        w_qkv,
+        w_so,
+        w_cq,
+        w_ckv,
+        w_co,
+        w_fi,
+        w_fo.reshape(-1, width),
         packed[:7],
-        packed[13:].reshape(hidden),
+        packed[13 : 13 + hidden // width].reshape(hidden),
         packed[7:10],
         packed[10:13],
     )

time: 502 us -> 414 us (0.82)
  Pallas kernels: 57.1 us -> 148 us
  local copies, waits for them, and re-layouts: 120 us -> 39.3 us
  waiting for transfers between devices: 121 us -> 57.4 us
  other arithmetic: 66.8 us -> 37.4 us
  starting transfers between devices: 40.7 us -> 24.7 us
  matrix products: 82.4 us -> 95.5 us
    pallas_call x0 -> x3, Pallas kernels: none -> 91.1 us  [the longest x1 77.9 us: finale(): pl.pallas_call(finale_kernel, out_shape=[jax.ShapeDtypeStruct((4, r, wa),...]
    ppermute x63 -> x32, waiting for transfers between devices: 121 us -> 57.4 us  [swap(): return lax.ppermute(part, axis, [(i, i ^ distance) for i in range(count)])]
    unnamed x193 -> x132, local copies, waits for them, and re-layouts: 51.1 us -> 10.6 us
    ppermute x63 -> x32, starting transfers between devices: 40.7 us -> 24.7 us  [swap(): return lax.ppermute(part, axis, [(i, i ^ distance) for i in range(count)])]
    dynamic_slice x23 -> x13, local copies, waits for them, and re-layouts: 23.3 us -> 8.58 us  [the longest x8 4.91 us: cut(): return lax.dynamic_slice_in_dim(a, start, size, axis)]
    dot_general x9 -> x12, matrix products: 29 us -> 42.2 us  [product(): return jnp.dot(left_rows, right_rows, preferred_element_type=jnp.float32)]
    reshape x6 -> x0, local copies, waits for them, and re-layouts: 11.4 us -> none  [interleave(): jnp.stack([p.reshape(r, count, -1) for p in parts], axis=2).reshape(r, -1)]
    convert_element_type x11 -> x4, other arithmetic: 15.7 us -> 4.64 us  [the longest x2 3.07 us: per_device(): ffn_grad = jnp.concatenate([g_in.astype(low), g_out.astype(low)], axis=1)]
  transfers between devices with their start and end apart: 63 -> 32, of which waited for: 18 -> 11; matrix products, arithmetic and copies ran while one was open for 50% -> 30% of each run, Pallas kernels for 10% -> 13%
where the time goes in v2:
time: 414 us; the launch traced here: 407 us
  Pallas kernels  148 us (36%)
  matrix products  95.5 us (23%)
  waiting for transfers between devices  57.4 us (14%)
  local copies, waits for them, and re-layouts  39.3 us (9%)
  other arithmetic  37.4 us (9%)
  starting transfers between devices  24.7 us (6%)
    pallas_call x1, Pallas kernels, finale(): pl.pallas_call(finale_kernel, out_shape=[jax.ShapeDtypeStruct((4, r, wa),...  77.9 us
    ppermute x32, waiting for transfers between devices, swap(): return lax.ppermute(part, axis, [(i, i ^ distance) for i in range(count)])  57.4 us
    dot_general x12, matrix products, product(): return jnp.dot(left_rows, right_rows, preferred_element_type=jnp.float32)  42.2 us
    pallas_call x2, Pallas kernels, attention_back(): pl.pallas_call(functools.partial(back_kernel, causal=causal), out_shape=[...  37.2 us
    dot_general x7, matrix products, product_tn(): lax.dot_general(left_rows, right_rows, (((0,), (0,)), ((), ())), preferre...  28.6 us
    ppermute x32, starting transfers between devices, swap(): return lax.ppermute(part, axis, [(i, i ^ distance) for i in range(count)])  24.7 us
    dot_general x7, matrix products, product_nt(): lax.dot_general(left_rows, right_rows, (((1,), (1,)), ((), ())), preferre...  24.7 us
    concatenate x9, other arithmetic, gather_rows(): pair = jnp.concatenate([part, swap(part, 'mem', 2)], axis=0)  11.8 us
  transfers between devices with their start and end apart: 32, of which 11 were waited for; matrix products, arithmetic and copies ran while one was open for 30% of the time, Pallas kernels for 13%

profile of v2, /device:TPU:0, one launch (start us, length us, event | category | flops | bytes accessed | tf_op | source)
XLA Modules:
  0.0 406.7 jit_solution(1560426388239256899)
XLA Ops:
  3.0 4.2 %fusion.53.k_ref = bf16[1024,512]{1,0:T(8,128)(2,1)} fusion(bf16[1,1024,1024]{2,1,0:T(8,128)(2,1)} %param.16, bf16[1024,3072]{1,0:T(8,128)(2,1)} %param.21, s32[]{:T(128)S(6)} %select_n.303), kind=kOutput, calls=%fused_computation.69 | convolution fusion | flops 1074266112 | bytes 4194308 | tf_op jit(solution)/shard_map/dot_general | solution.py:18
  7.2 3.4 fusion.56.q_ref
  10.7 4.1 %fusion.59.v_ref = bf16[1024,512]{1,0:T(8,128)(2,1)} fusion(bf16[1,1024,1024]{2,1,0:T(8,128)(2,1)} %param.16, f32[512]{0:T(512)S(1)} %bitcast.299, bf16[1024,3072]{1,0:T(8,128)(2,1)} %param.21, s32[]{:T(128)S(6)} %select_n.304), kind=kOutput, calls=%fused_computation.71 | convolution fusion | flops 1074790400 | bytes 4196356 | tf_op jit(solution)/shard_map/dot_general | solution.py:18
  14.8 9.7 %self_forward.1 = bf16[512,512]{1,0:T(8,128)(2,1)} custom-call(s32[2]{0:T(128)} %pad_add_fusion.info, bf16[1024,512]{1,0:T(8,128)(2,1)} %fusion.56.q_ref, bf16[1024,512]{1,0:T(8,128)(2,1)} %fusion.53.k_ref, bf16[1024,512]{1,0:T(8,128)(2,1)} %fusion.59.v_ref), custom_call_target="tpu_custom_call" | custom-call | flops 3221225472 | bytes 4194304 | tf_op jit(solution)/shard_map/self_forward/pallas_call | solution.py:106
  26.1 2.2 collective-permute-start.2
  29.5 5.7 %pick_columns.1 = bf16[1024,1024]{1,0:T(8,128)(2,1)} custom-call(s32[1]{0:T(128)} %bitcast.31.info, bf16[1024,4096]{1,0:T(8,128)(2,1)} %in_ref.1), custom_call_target="tpu_custom_call" | custom-call | bytes 4194304 | tf_op jit(solution)/shard_map/pick_columns/pallas_call | solution.py:237
  35.9 2.7 fusion.141
  38.9 2.3 collective-permute-done.2
  43.3 2.6 constant_dynamic-slice_fusion.2
  45.9 3.1 constant_dynamic-slice_fusion.8
  49.0 1.7 collective-permute-start.11
  53.4 3.8 convolution_convert_fusion.1.k_ref
  57.2 3.4 add_convert_fusion.v_ref
  60.6 10.3 %cross_forward.1 = bf16[512,512]{1,0:T(8,128)(2,1)} custom-call(bf16[512,512]{1,0:T(8,128)(2,1)} %fusion.69.q_ref, bf16[1024,512]{1,0:T(8,128)(2,1)} %convolution_convert_fusion.1.k_ref, bf16[1024,512]{1,0:T(8,128)(2,1)} %add_convert_fusion.v_ref, f32[1,1024]{1,0:T(1,128)} %bitcast.294), custom_call_target="tpu_custom_call" | custom-call | flops 4294967296 | bytes 2097152 | tf_op jit(solution)/shard_map/cross_forward/pallas_call | solution.py:140
  76.2 1.7 collective-permute-start.7
  78.0 1.9 fusion.142
  80.5 6.1 %convolution_add_fusion = f32[256,4096]{1,0:T(8,128)S(1)} fusion(bf16[256,1024]{1,0:T(8,128)(2,1)S(1)} %fusion.96, bf16[1024,4096]{1,0:T(8,128)(2,1)} %in_ref.1, f32[4096]{0:T(1024)S(1)} %copy-done.46), kind=kOutput, calls=%fused_computation.3 | convolution fusion | flops 2148532224 | bytes 13123584 | tf_op jit(solution)/shard_map/dot_general | solution.py:18
  87.0 2.7 fusion.143
  92.0 6.8 %convert_reduce_fusion = (f32[4096]{0:T(1024)S(1)}, bf16[256,4096]{1,0:T(8,128)(2,1)}) fusion(f32[256,4096]{1,0:T(8,128)S(1)} %convolution_add_fusion, bf16[256,1024]{1,0:T(8,128)(2,1)} %get-tuple-element.107, bf16[4096,1024]{1,0:T(8,128)(2,1)S(1)} %bitcast.260), kind=kOutput, calls=%fused_computation.16 | convolution fusion | flops 2162159616 | bytes 15220736 | tf_op jit(solution)/shard_map/dot_general | solution.py:28
  98.9 1.8 collective-permute-start.15
  101.0 5.4 %multiply_reduce_fusion = (f32[1024]{0:T(1024)}, f32[256]{0:T(256)S(1)}, f32[256]{0:T(256)S(1)}, f32[1024]{0:T(1024)}, f32[256,1024]{1,0:T(8,128)S(1)}) fusion(f32[256,1024]{1,0:T(8,128)S(1)} %get-tuple-element.181, f32[256]{0:T(256)S(1)} %add_rsqrt_fusion.1, f32[256]{0:T(256)S(1)} %broadcast_multiply_fusion.7, f32[1024]{0:T(1024)S(1)} %bitcast.270, ...), kind=kOutput, calls=%fused_computation.125 | convolution fusion | flops 2152461824 | bytes 14180612 | tf_op jit(solution)/shard_map/dot_general | solution.py:28
  107.5 1.5 convert_reduce_fusion.2
  109.1 5.0 %collective-permute-done.15 = bf16[256,1024]{1,0:T(8,128)(2,1)} collective-permute-done((bf16[256,1024]{1,0:T(8,128)(2,1)}, bf16[256,1024]{1,0:T(8,128)(2,1)}, u32[]{:S(2)}, u32[]{:S(2)}) %collective-permute-start.15) | collective-permute-done | bytes 524320 | tf_op jit(solution)/shard_map/ppermute | solution.py:253
  114.0 1.7 collective-permute-start.9
  117.2 2.7 fusion.68.q_ref
  119.9 5.4 %collective-permute-done.5 = bf16[256,1024]{1,0:T(8,128)(2,1)} collective-permute-done((bf16[256,1024]{1,0:T(8,128)(2,1)}, bf16[256,1024]{1,0:T(8,128)(2,1)}, u32[]{:S(2)}, u32[]{:S(2)}) %collective-permute-start.5) | collective-permute-done | bytes 524320 | tf_op jit(solution)/shard_map/ppermute | solution.py:253
  125.3 2.2 pad_maximum_fusion.12
  128.1 2.5 pad_maximum_fusion.13
  130.6 4.1 %collective-permute-done.9 = bf16[256,1024]{1,0:T(8,128)(2,1)S(1)} collective-permute-done((bf16[256,1024]{1,0:T(8,128)(2,1)}, bf16[256,1024]{1,0:T(8,128)(2,1)S(1)}, u32[]{:S(2)}, u32[]{:S(2)}) %collective-permute-start.9) | collective-permute-done | bytes 524320 | tf_op jit(solution)/shard_map/ppermute | solution.py:253
  136.3 5.6 %fusion.98 = f32[1024,1024]{1,0:T(8,128)} fusion(bf16[1024,1024]{1,0:T(8,128)(2,1)S(1)} %copy-done.14, bf16[512,1024]{1,0:T(8,128)(2,1)} %collective-permute-done.14, bf16[256,1024]{1,0:T(8,128)(2,1)S(1)} %copy-done.38, bf16[256,1024]{1,0:T(8,128)(2,1)S(1)} %copy-done.13), kind=kOutput, calls=%fused_computation.160 | convolution fusion | flops 2153775104 | bytes 8388608 | tf_op jit(solution)/shard_map/dot_general | solution.py:18
  142.9 11.3 %fusion.97 = f32[1024,1024]{1,0:T(8,128)} fusion(bf16[512,1024]{1,0:T(8,128)(2,1)} %collective-permute-done.14, bf16[256,1024]{1,0:T(8,128)(2,1)} %copy-done.37, bf16[256,1024]{1,0:T(8,128)(2,1)} %copy-done.12, f32[1024,1024]{1,0:T(8,128)} %fusion.98, bf16[1024,1024]{1,0:T(8,128)(2,1)} %bitcast.246, f32[1024]{0:T(1024)S(1)} %bitcast.291, ...), kind=kOutput, calls=%fused_computation.159 | convolution fusion | flops 4319084544 | bytes 14684160 | tf_op jit(solution)/shard_map/dot_general | solution.py:22
  154.1 5.4 %fusion.13 = f32[1024,1024]{1,0:T(8,128)S(1)} fusion(f32[1024,1024]{1,0:T(8,128)} %fusion.98, f32[1024]{0:T(1024)S(1)} %bitcast.292, bf16[512,1024]{1,0:T(8,128)(2,1)} %copy-done.54, bf16[256,1024]{1,0:T(8,128)(2,1)} %collective-permute-done.15, bf16[256,1024]{1,0:T(8,128)(2,1)} %get-tuple-element.107), kind=kOutput, calls=%fused_computation.22 | convolution fusion | flops 2160066560 | bytes 10489856 | tf_op jit(solution)/shard_map/dot_general | solution.py:22
  159.6 2.8 fusion.72
  163.5 2.9 convolution_convert_fusion.3.g0_ref.g1_ref.g2_ref.g3_ref
  166.4 2.1 collective-permute-start.17
  168.6 1.6 collective-permute-start.18
  171.6 2.3 fusion.14
  174.8 1.7 pad_maximum_fusion.1
  179.2 21.4 %cross_back.1 = (bf16[1024,256]{1,0:T(8,128)(2,1)}, bf16[1024,256]{1,0:T(8,128)(2,1)}, bf16[1024,256]{1,0:T(8,128)(2,1)}) custom-call(s32[1]{0:T(128)} %bitcast.30.info, bf16[1024,256]{1,0:T(8,128)(2,1)} %fusion.68.q_ref, bf16[1024,512]{1,0:T(8,128)(2,1)} %convolution_convert_fusion.1.k_ref, bf16[1024,512]{1,0:T(8,128)(2,1)} %add_convert_fusion.v_ref, ...), custom_call_target="tpu_custom_call" | custom-call | flops 10737418240 | bytes 3670016 | tf_op jit(solution)/shard_map/cross_back/pallas_call | solution.py:207
  201.9 2.2 fusion.99
  206.2 1.6 bitcast_add_fusion.1
  209.2 2.5 fusion.134
  212.8 1.7 bitcast_add_fusion
  216.3 8.7 %collective-permute-done.30 = bf16[512,512]{1,0:T(8,128)(2,1)S(1)} collective-permute-done((bf16[512,512]{1,0:T(8,128)(2,1)S(1)}, bf16[512,512]{1,0:T(8,128)(2,1)S(1)}, u32[]{:S(2)}, u32[]{:S(2)}) %collective-permute-start.30) | collective-permute-done | bytes 524320 | tf_op jit(solution)/shard_map/ppermute | solution.py:253
  226.2 1.6 multiply_reduce_fusion.1
  227.8 1.9 convert_reduce_fusion.5
  231.2 12.0 %collective-permute-done.21 = bf16[256,1024]{1,0:T(8,128)(2,1)S(1)} collective-permute-done((bf16[256,1024]{1,0:T(8,128)(2,1)S(1)}, bf16[256,1024]{1,0:T(8,128)(2,1)S(1)}, u32[]{:S(2)}, u32[]{:S(2)}) %collective-permute-start.21) | collective-permute-done | bytes 524320 | tf_op jit(solution)/shard_map/ppermute | solution.py:253
  243.5 2.3 convolution_bitcast_fusion
  247.0 2.0 fusion.20
  249.0 2.6 convolution_convert_fusion.2.g0_ref.g1_ref.g2_ref.g3_ref
  254.7 2.6 collective-permute-start.27
  258.2 15.8 %self_back.1 = (bf16[1024,256]{1,0:T(8,128)(2,1)}, bf16[1024,256]{1,0:T(8,128)(2,1)}, bf16[1024,256]{1,0:T(8,128)(2,1)}) custom-call(s32[6]{0:T(128)} %stack.124.info, bf16[1024,512]{1,0:T(8,128)(2,1)} %fusion.56.q_ref, bf16[1024,512]{1,0:T(8,128)(2,1)} %fusion.53.k_ref, bf16[1024,512]{1,0:T(8,128)(2,1)} %fusion.59.v_ref, ...), custom_call_target="tpu_custom_call" | custom-call | flops 5368709120 | bytes 3670016 | tf_op jit(solution)/shard_map/self_back/pallas_call | solution.py:207
  274.9 12.4 %collective-permute-done.27 = bf16[1,128,1024]{2,1,0:T(8,128)(2,1)S(1)} collective-permute-done((bf16[1,128,1024]{2,1,0:T(8,128)(2,1)S(1)}, bf16[1,128,1024]{2,1,0:T(8,128)(2,1)S(1)}, u32[]{:S(2)}, u32[]{:S(2)}) %collective-permute-start.27) | collective-permute-done | bytes 262176 | tf_op jit(solution)/shard_map/ppermute | solution.py:253
  287.3 5.1 %collective-permute-done.28 = bf16[1,128,1024]{2,1,0:T(8,128)(2,1)S(1)} collective-permute-done((bf16[1,128,1024]{2,1,0:T(8,128)(2,1)S(1)}, bf16[1,128,1024]{2,1,0:T(8,128)(2,1)S(1)}, u32[]{:S(2)}, u32[]{:S(2)}) %collective-permute-start.28) | collective-permute-done | bytes 262176 | tf_op jit(solution)/shard_map/ppermute | solution.py:253
  292.4 1.8 collective-permute-done.29
  294.2 1.6 constant_dynamic-update-slice_fusion.4
  297.4 3.0 fusion.47
  300.4 2.7 copy.40
  304.2 1.9 fusion.110
  306.1 1.6 concatenate.163
  309.9 1.9 pad_maximum_fusion.28.f_ref
  312.1 3.1 convolution_convert_fusion
  316.4 77.9 %finale.1 = (bf16[4,128,1280]{2,1,0:T(8,128)(2,1)}, bf16[4,128,768]{2,1,0:T(8,128)(2,1)}, bf16[4,128,2048]{2,1,0:T(8,128)(2,1)}, bf16[4,256,1024]{2,1,0:T(8,128)(2,1)}, f32[24,1024]{1,0:T(8,128)}) custom-call(bf16[2,2,128,1280]{3,2,1,0:T(8,128)(2,1)} %bitcast.239, bf16[4,2,128,768]{3,2,1,0:T(8,128)(2,1)} %bitcast.238, ...), custom_call_target="tpu_custom_call" | custom-call | flops 1000000 | bytes 100000000 | tf_op jit(solution)/shard_map/finale/pallas_call | solution.py:444
  398.6 7.6 %unpack.1 = (f32[128,3072]{1,0:T(8,128)}, f32[128,1024]{1,0:T(8,128)}, f32[128,1024]{1,0:T(8,128)}, f32[128,2048]{1,0:T(8,128)}, f32[128,1024]{1,0:T(8,128)}, /*...) custom-call(bf16[4,128,1280]{2,1,0:T(8,128)(2,1)} %get-tuple-element.81.a_ref, ...), custom_call_target="tpu_custom_call" | custom-call | flops 1000000 | bytes 20000000 | tf_op jit(solution)/shard_map/unpack/pallas_call | solution.py:510
  (279 shorter events, 56.9 us)
Async XLA Ops:
  0.6 50.4 %copy-start = (bf16[1024,1024]{1,0:T(8,128)(2,1)S(1)}, bf16[1024,1024]{1,0:T(8,128)(2,1)}, u32[]{:S(2)}) copy-start(bf16[1024,1024]{1,0:T(8,128)(2,1)} %param.23) | copy-start | bytes 6291460
  3.0 4.2 %copy-start.50 = (bf16[1,1024,1024]{2,1,0:T(8,128)(2,1)S(1)}, bf16[1,1024,1024]{2,1,0:T(8,128)(2,1)}, u32[]{:S(2)}) copy-start(bf16[1,1024,1024]{2,1,0:T(8,128)(2,1)} %param.16) | copy-start | bytes 6291460
  14.8 13.6 %copy-start.43 = (f32[3,1024]{1,0:T(4,128)S(1)}, f32[3,1024]{1,0:T(4,128)}, u32[]{:S(2)}) copy-start(f32[3,1024]{1,0:T(4,128)} %param.31) | copy-start | bytes 36868
  14.8 14.4 %copy-start.46 = (f32[4096]{0:T(1024)S(1)}, f32[4096]{0:T(1024)}, u32[]{:S(2)}) copy-start(f32[4096]{0:T(1024)} %param.29) | copy-start | bytes 49156
  25.6 10.2 %collective-permute-start = (bf16[256,512]{1,0:T(8,128)(2,1)S(1)}, bf16[256,512]{1,0:T(8,128)(2,1)S(1)}, u32[]{:S(2)}, u32[]{:S(2)}) collective-permute-start(bf16[256,512]{1,0:T(8,128)(2,1)S(1)} %get-tuple-element.148), channel_id=1, source_target_pairs={{0,1},{1,0},{2,3},{3,2},{4,5},{5,4},{6,7},{7,6},{8,9},{9,8},{10,11... | collective-permute-start | bytes 786440 | tf_op jit(solution)/shard_map/ppermute | solution.py:253
  26.1 15.0 %collective-permute-start.2 = (bf16[256,1024]{1,0:T(8,128)(2,1)}, bf16[256,1024]{1,0:T(8,128)(2,1)}, u32[]{:S(2)}, u32[]{:S(2)}) collective-permute-start(bf16[256,1024]{1,0:T(8,128)(2,1)} %bitcast.12), channel_id=1, source_target_pairs={{0,2},{1,3},{2,0},{3,1},{4,6},{5,7},{6,4},{7,5},{8,10},{9,11},{10,... | collective-permute-start | bytes 1572872 | tf_op jit(solution)/shard_map/ppermute | solution.py:253
  29.5 19.5 %copy-start.45 = (f32[1,1,4,256]{3,1,2,0:T(1,128)}, f32[1,1,4,256]{3,1,2,0:T(1,128)S(1)}, u32[]{:S(2)}) copy-start(f32[1,1,4,256]{3,1,2,0:T(1,128)S(1)} %copy.47) | copy-start | bytes 12292
  29.5 6.2 %copy-start.44 = (f32[3,1024]{1,0:T(4,128)S(1)}, f32[3,1024]{1,0:T(4,128)}, u32[]{:S(2)}) copy-start(f32[3,1024]{1,0:T(4,128)} %param.30) | copy-start | bytes 36868
  35.9 38.2 %copy-start.15 = (bf16[256,1024]{1,0:T(8,128)(2,1)}, bf16[256,1024]{1,0:T(8,128)(2,1)S(1)}, u32[]{:S(2)}) copy-start(bf16[256,1024]{1,0:T(8,128)(2,1)S(1)} %maximum_select_fusion) | copy-start | bytes 1572868
  42.4 10.1 %collective-permute-start.3 = (bf16[512,1024]{1,0:T(8,128)(2,1)S(1)}, bf16[512,1024]{1,0:T(8,128)(2,1)S(1)}, u32[]{:S(2)}, u32[]{:S(2)}) collective-permute-start(bf16[512,1024]{1,0:T(8,128)(2,1)S(1)} %pad_maximum_fusion.11), channel_id=1, source_target_pairs={{0,1},{1,0},{2,3},{3,2},{4,5},{5,4},{6,7},{7,6},{8,9},{9,8},{10,11... | collective-permute-start | bytes 3145736 | tf_op jit(solution)/shard_map/ppermute | solution.py:253
  42.8 29.3 %copy-start.9 = (bf16[256,1024]{1,0:T(8,128)(2,1)}, bf16[256,1024]{1,0:T(8,128)(2,1)S(1)}, u32[]{:S(2)}) copy-start(bf16[256,1024]{1,0:T(8,128)(2,1)S(1)} %fusion.95) | copy-start | bytes 1572868
  42.8 8.2 %collective-permute-start.1 = (bf16[256,1024]{1,0:T(8,128)(2,1)S(1)}, bf16[256,1024]{1,0:T(8,128)(2,1)S(1)}, u32[]{:S(2)}, u32[]{:S(2)}) collective-permute-start(bf16[256,1024]{1,0:T(8,128)(2,1)S(1)} %fusion.95), channel_id=1, source_target_pairs={{0,1},{1,0},{2,3},{3,2},{4,5},{5,4},{6,7},{7,6},{8,9},{9,8},{10,11... | collective-permute-start | bytes 1572872 | tf_op jit(solution)/shard_map/ppermute | solution.py:253
  49.0 23.1 %collective-permute-start.11 = (bf16[256,1024]{1,0:T(8,128)(2,1)S(1)}, bf16[256,1024]{1,0:T(8,128)(2,1)S(1)}, u32[]{:S(2)}, u32[]{:S(2)}) collective-permute-start(bf16[256,1024]{1,0:T(8,128)(2,1)S(1)} %fusion.95), channel_id=1, source_target_pairs={{0,2},{1,3},{2,0},{3,1},{4,6},{5,7},{6,4},{7,5},{8,10},{9,11},{10,... | collective-permute-start | bytes 1572872 | tf_op jit(solution)/shard_map/ppermute | solution.py:253
  50.7 23.4 %collective-permute-start.25 = (bf16[256,1024]{1,0:T(8,128)(2,1)S(1)}, bf16[256,1024]{1,0:T(8,128)(2,1)S(1)}, u32[]{:S(2)}, u32[]{:S(2)}) collective-permute-start(bf16[256,1024]{1,0:T(8,128)(2,1)S(1)} %maximum_select_fusion), channel_id=1, source_target_pairs={{0,2},{1,3},{2,0},{3,1},{4,6},{5,7},{6,4},{7,5},{8,10},{9,11},{10,... | collective-permute-start | bytes 1572872 | tf_op jit(solution)/shard_map/ppermute | solution.py:253
  72.0 3.3 collective-permute-start.4
  73.2 4.8 %copy-start.49 = (bf16[1024,1024]{1,0:T(8,128)(2,1)S(1)}, bf16[1024,1024]{1,0:T(8,128)(2,1)}, u32[]{:S(2)}) copy-start(bf16[1024,1024]{1,0:T(8,128)(2,1)} %param.25) | copy-start | bytes 6291460
  73.2 43.9 %collective-permute-start.12 = (bf16[512,1024]{1,0:T(8,128)(2,1)}, bf16[512,1024]{1,0:T(8,128)(2,1)}, u32[]{:S(2)}, u32[]{:S(2)}) collective-permute-start(bf16[512,1024]{1,0:T(8,128)(2,1)} %pad_maximum_fusion.9), channel_id=1, source_target_pairs={{0,1},{1,0},{2,3},{3,2},{4,5},{5,4},{6,7},{7,6},{8,9},{9,8},{10,11... | collective-permute-start | bytes 3145736 | tf_op jit(solution)/shard_map/ppermute | solution.py:253
  74.2 5.8 %copy-start.32 = (bf16[256,1024]{1,0:T(8,128)(2,1)}, bf16[256,1024]{1,0:T(8,128)(2,1)S(1)}, u32[]{:S(2)}) copy-start(bf16[256,1024]{1,0:T(8,128)(2,1)S(1)} %collective-permute-done.25) | copy-start | bytes 1572868
  76.2 51.3 %collective-permute-start.7 = (bf16[256,1024]{1,0:T(8,128)(2,1)}, bf16[256,1024]{1,0:T(8,128)(2,1)}, u32[]{:S(2)}, u32[]{:S(2)}) collective-permute-start(bf16[256,1024]{1,0:T(8,128)(2,1)} %maximum_select_fusion.1), channel_id=1, source_target_pairs={{0,2},{1,3},{2,0},{3,1},{4,6},{5,7},{6,4},{7,5},{8,10},{9,11},{10,... | collective-permute-start | bytes 1572872 | tf_op jit(solution)/shard_map/ppermute | solution.py:253
  80.2 6.7 %slice-start.2 = ((s8[8388608]{0:T(1024)(128)(4,1)}), s8[4194304]{0:T(1024)(128)(4,1)S(1)}, s32[]{:S(2)}) async-start(s8[8388608]{0:T(1024)(128)(4,1)} %bitcast.259), calls=%async_computation.2 | async-start | bytes 8388608
  80.5 25.9 %copy-start.12 = (bf16[256,1024]{1,0:T(8,128)(2,1)}, bf16[256,1024]{1,0:T(8,128)(2,1)S(1)}, u32[]{:S(2)}) copy-start(bf16[256,1024]{1,0:T(8,128)(2,1)S(1)} %fusion.96) | copy-start | bytes 1572868
  80.5 6.5 %slice-start.3 = ((s8[8388608]{0:T(1024)(128)(4,1)}), s8[4194304]{0:T(1024)(128)(4,1)S(1)}, s32[]{:S(2)}) async-start(s8[8388608]{0:T(1024)(128)(4,1)} %bitcast.259), calls=%async_computation.3 | async-start | bytes 8388608
  86.6 19.8 %collective-permute-start.13 = (bf16[256,1024]{1,0:T(8,128)(2,1)S(1)}, bf16[256,1024]{1,0:T(8,128)(2,1)S(1)}, u32[]{:S(2)}, u32[]{:S(2)}) collective-permute-start(bf16[256,1024]{1,0:T(8,128)(2,1)S(1)} %fusion.96), channel_id=1, source_target_pairs={{0,2},{1,3},{2,0},{3,1},{4,6},{5,7},{6,4},{7,5},{8,10},{9,11},{10,... | collective-permute-start | bytes 1572872 | tf_op jit(solution)/shard_map/ppermute | solution.py:253
  90.5 10.4 %slice-start = ((s8[8388608]{0:T(1024)(128)(4,1)}), s8[4194304]{0:T(1024)(128)(4,1)S(1)}, s32[]{:S(2)}) async-start(s8[8388608]{0:T(1024)(128)(4,1)} %bitcast.232), calls=%async_computation | async-start | bytes 8388608
  92.0 8.9 %slice-start.1 = ((s8[8388608]{0:T(1024)(128)(4,1)}), s8[4194304]{0:T(1024)(128)(4,1)S(1)}, s32[]{:S(2)}) async-start(s8[8388608]{0:T(1024)(128)(4,1)} %bitcast.232), calls=%async_computation.1 | async-start | bytes 8388608
  98.9 15.2 %collective-permute-start.15 = (bf16[256,1024]{1,0:T(8,128)(2,1)}, bf16[256,1024]{1,0:T(8,128)(2,1)}, u32[]{:S(2)}, u32[]{:S(2)}) collective-permute-start(bf16[256,1024]{1,0:T(8,128)(2,1)} %get-tuple-element.107), channel_id=1, source_target_pairs={{0,2},{1,3},{2,0},{3,1},{4,6},{5,7},{6,4},{7,5},{8,10},{9,11},{10,... | collective-permute-start | bytes 1572872 | tf_op jit(solution)/shard_map/ppermute | solution.py:253
  100.7 24.6 %collective-permute-start.5 = (bf16[256,1024]{1,0:T(8,128)(2,1)}, bf16[256,1024]{1,0:T(8,128)(2,1)}, u32[]{:S(2)}, u32[]{:S(2)}) collective-permute-start(bf16[256,1024]{1,0:T(8,128)(2,1)} %get-tuple-element.124), channel_id=1, source_target_pairs={{0,2},{1,3},{2,0},{3,1},{4,6},{5,7},{6,4},{7,5},{8,10},{9,11},{10,... | collective-permute-start | bytes 1572872 | tf_op jit(solution)/shard_map/ppermute | solution.py:253
  107.5 28.4 %collective-permute-start.14 = (bf16[512,1024]{1,0:T(8,128)(2,1)}, bf16[512,1024]{1,0:T(8,128)(2,1)}, u32[]{:S(2)}, u32[]{:S(2)}) collective-permute-start(bf16[512,1024]{1,0:T(8,128)(2,1)} %pad_maximum_fusion.15), channel_id=1, source_target_pairs={{0,1},{1,0},{2,3},{3,2},{4,5},{5,4},{6,7},{7,6},{8,9},{9,8},{10,11... | collective-permute-start | bytes 3145736 | tf_op jit(solution)/shard_map/ppermute | solution.py:253
  109.1 8.1 %copy-start.10 = (bf16[256,1024]{1,0:T(8,128)(2,1)S(1)}, bf16[256,1024]{1,0:T(8,128)(2,1)}, u32[]{:S(2)}) copy-start(bf16[256,1024]{1,0:T(8,128)(2,1)} %copy-done.9) | copy-start | bytes 1572868
  109.1 8.1 %copy-start.35 = (bf16[256,1024]{1,0:T(8,128)(2,1)S(1)}, bf16[256,1024]{1,0:T(8,128)(2,1)}, u32[]{:S(2)}) copy-start(bf16[256,1024]{1,0:T(8,128)(2,1)} %copy-done.34) | copy-start | bytes 1572868
  114.0 20.7 %collective-permute-start.9 = (bf16[256,1024]{1,0:T(8,128)(2,1)}, bf16[256,1024]{1,0:T(8,128)(2,1)S(1)}, u32[]{:S(2)}, u32[]{:S(2)}) collective-permute-start(bf16[256,1024]{1,0:T(8,128)(2,1)} %get-tuple-element.109), channel_id=1, source_target_pairs={{0,2},{1,3},{2,0},{3,1},{4,6},{5,7},{6,4},{7,5},{8,10},{9,11},{10,... | collective-permute-start | bytes 1572872 | tf_op jit(solution)/shard_map/ppermute | solution.py:253
  117.1 24.8 %collective-permute-start.16 = (bf16[512,1024]{1,0:T(8,128)(2,1)S(1)}, bf16[512,1024]{1,0:T(8,128)(2,1)S(1)}, u32[]{:S(2)}, u32[]{:S(2)}) collective-permute-start(bf16[512,1024]{1,0:T(8,128)(2,1)S(1)} %pad_maximum_fusion.16), channel_id=1, source_target_pairs={{0,1},{1,0},{2,3},{3,2},{4,5},{5,4},{6,7},{7,6},{8,9},{9,8},{10,11... | collective-permute-start | bytes 3145736 | tf_op jit(solution)/shard_map/ppermute | solution.py:253
  119.9 14.8 %copy-start.1 = (bf16[256,1024]{1,0:T(8,128)(2,1)S(1)}, bf16[256,1024]{1,0:T(8,128)(2,1)}, u32[]{:S(2)}) copy-start(bf16[256,1024]{1,0:T(8,128)(2,1)} %get-tuple-element.109) | copy-start | bytes 1572868
  125.3 120.9 %collective-permute-start.26 = (bf16[512,1024]{1,0:T(8,128)(2,1)}, bf16[512,1024]{1,0:T(8,128)(2,1)}, u32[]{:S(2)}, u32[]{:S(2)}) collective-permute-start(bf16[512,1024]{1,0:T(8,128)(2,1)} %pad_maximum_fusion.18), channel_id=1, source_target_pairs={{0,1},{1,0},{2,3},{3,2},{4,5},{5,4},{6,7},{7,6},{8,9},{9,8},{10,11... | collective-permute-start | bytes 3145736 | tf_op jit(solution)/shard_map/ppermute | solution.py:253
  127.5 8.8 %copy-start.13 = (bf16[256,1024]{1,0:T(8,128)(2,1)S(1)}, bf16[256,1024]{1,0:T(8,128)(2,1)}, u32[]{:S(2)}) copy-start(bf16[256,1024]{1,0:T(8,128)(2,1)} %copy-done.12) | copy-start | bytes 1572868
  127.5 8.8 %copy-start.14 = (bf16[1024,1024]{1,0:T(8,128)(2,1)S(1)}, bf16[1024,1024]{1,0:T(8,128)(2,1)}, u32[]{:S(2)}) copy-start(bf16[1024,1024]{1,0:T(8,128)(2,1)} %pick_columns.1) | copy-start | bytes 6291460
  127.5 8.8 %copy-start.38 = (bf16[256,1024]{1,0:T(8,128)(2,1)S(1)}, bf16[256,1024]{1,0:T(8,128)(2,1)}, u32[]{:S(2)}) copy-start(bf16[256,1024]{1,0:T(8,128)(2,1)} %copy-done.37) | copy-start | bytes 1572868
  127.5 47.3 %collective-permute-start.6 = (bf16[512,1024]{1,0:T(8,128)(2,1)}, bf16[512,1024]{1,0:T(8,128)(2,1)}, u32[]{:S(2)}, u32[]{:S(2)}) collective-permute-start(bf16[512,1024]{1,0:T(8,128)(2,1)} %pad_maximum_fusion.12), channel_id=1, source_target_pairs={{0,1},{1,0},{2,3},{3,2},{4,5},{5,4},{6,7},{7,6},{8,9},{9,8},{10,11... | collective-permute-start | bytes 3145736 | tf_op jit(solution)/shard_map/ppermute | solution.py:253
  134.7 36.8 %collective-permute-start.8 = (bf16[512,1024]{1,0:T(8,128)(2,1)}, bf16[512,1024]{1,0:T(8,128)(2,1)}, u32[]{:S(2)}, u32[]{:S(2)}) collective-permute-start(bf16[512,1024]{1,0:T(8,128)(2,1)} %pad_maximum_fusion.13), channel_id=1, source_target_pairs={{0,1},{1,0},{2,3},{3,2},{4,5},{5,4},{6,7},{7,6},{8,9},{9,8},{10,11... | collective-permute-start | bytes 3145736 | tf_op jit(solution)/shard_map/ppermute | solution.py:253
  135.9 27.6 %collective-permute-start.10 = (bf16[512,1024]{1,0:T(8,128)(2,1)}, bf16[512,1024]{1,0:T(8,128)(2,1)}, u32[]{:S(2)}, u32[]{:S(2)}) collective-permute-start(bf16[512,1024]{1,0:T(8,128)(2,1)} %pad_maximum_fusion.14), channel_id=1, source_target_pairs={{0,1},{1,0},{2,3},{3,2},{4,5},{5,4},{6,7},{7,6},{8,9},{9,8},{10,11... | collective-permute-start | bytes 3145736 | tf_op jit(solution)/shard_map/ppermute | solution.py:253
  166.4 34.2 %collective-permute-start.17 = (bf16[4,128,1024]{2,1,0:T(8,128)(2,1)}, bf16[4,128,1024]{2,1,0:T(8,128)(2,1)}, u32[]{:S(2)}, u32[]{:S(2)}) collective-permute-start(bf16[4,128,1024]{2,1,0:T(8,128)(2,1)} %fusion.72), channel_id=1, source_target_pairs={{0,4},{4,0},{8,12},{12,8},{16,20},{20,16},{24,28},{28,24},{1,5},{5... | collective-permute-start | bytes 3145736 | tf_op jit(solution)/shard_map/ppermute | solution.py:253
  168.6 32.1 %collective-permute-start.18 = (bf16[4,128,1024]{2,1,0:T(8,128)(2,1)}, bf16[4,128,1024]{2,1,0:T(8,128)(2,1)}, u32[]{:S(2)}, u32[]{:S(2)}) collective-permute-start(bf16[4,128,1024]{2,1,0:T(8,128)(2,1)} %bitcast.43), channel_id=1, source_target_pairs={{0,8},{4,12},{8,0},{12,4},{16,24},{20,28},{24,16},{28,20},{1,9},{5... | collective-permute-start | bytes 3145736 | tf_op jit(solution)/shard_map/ppermute | solution.py:253
  179.2 22.6 %copy-start.11 = (bf16[256,1024]{1,0:T(8,128)(2,1)S(1)}, bf16[256,1024]{1,0:T(8,128)(2,1)}, u32[]{:S(2)}) copy-start(bf16[256,1024]{1,0:T(8,128)(2,1)} %copy-done.9) | copy-start | bytes 1572868
  179.2 22.6 %copy-start.36 = (bf16[256,1024]{1,0:T(8,128)(2,1)S(1)}, bf16[256,1024]{1,0:T(8,128)(2,1)}, u32[]{:S(2)}) copy-start(bf16[256,1024]{1,0:T(8,128)(2,1)} %copy-done.34) | copy-start | bytes 1572868
  201.9 4.4 %copy-start.6 = (f32[1024,1024]{1,0:T(8,128)S(1)}, f32[1024,1024]{1,0:T(8,128)}, u32[]{:S(2)}) copy-start(f32[1024,1024]{1,0:T(8,128)} %fusion.97) | copy-start | bytes 12582916
  205.0 11.1 %collective-permute-start.19 = (bf16[512,256]{1,0:T(8,128)(2,1)S(1)}, bf16[512,256]{1,0:T(8,128)(2,1)S(1)}, u32[]{:S(2)}, u32[]{:S(2)}) collective-permute-start(bf16[512,256]{1,0:T(8,128)(2,1)S(1)} %pad_maximum_fusion.31), channel_id=1, source_target_pairs={{0,2},{1,3},{2,0},{3,1},{4,6},{5,7},{6,4},{7,5},{8,10},{9,11},{10,... | collective-permute-start | bytes 786440 | tf_op jit(solution)/shard_map/ppermute | solution.py:253
  207.9 43.8 %collective-permute-start.23 = (bf16[2,128,1024]{2,1,0:T(8,128)(2,1)S(1)}, bf16[2,128,1024]{2,1,0:T(8,128)(2,1)S(1)}, u32[]{:S(2)}, u32[]{:S(2)}) collective-permute-start(bf16[2,128,1024]{2,1,0:T(8,128)(2,1)S(1)} %fusion.100), channel_id=1, source_target_pairs={{0,8},{4,12},{8,0},{12,4},{16,24},{20,28},{24,16},{28,20},{1,9},{5... | collective-permute-start | bytes 1572872 | tf_op jit(solution)/shard_map/ppermute | solution.py:253
  211.8 13.1 %collective-permute-start.30 = (bf16[512,512]{1,0:T(8,128)(2,1)S(1)}, bf16[512,512]{1,0:T(8,128)(2,1)S(1)}, u32[]{:S(2)}, u32[]{:S(2)}) collective-permute-start(bf16[512,512]{1,0:T(8,128)(2,1)S(1)} %pad_maximum_fusion.29), channel_id=1, source_target_pairs={{0,2},{1,3},{2,0},{3,1},{4,6},{5,7},{6,4},{7,5},{8,10},{9,11},{10,... | collective-permute-start | bytes 1572872 | tf_op jit(solution)/shard_map/ppermute | solution.py:253
  214.5 37.1 %collective-permute-start.24 = (bf16[2,128,1024]{2,1,0:T(8,128)(2,1)S(1)}, bf16[2,128,1024]{2,1,0:T(8,128)(2,1)S(1)}, u32[]{:S(2)}, u32[]{:S(2)}) collective-permute-start(bf16[2,128,1024]{2,1,0:T(8,128)(2,1)S(1)} %fusion.101), channel_id=1, source_target_pairs={{0,4},{4,0},{8,12},{12,8},{16,20},{20,16},{24,28},{28,24},{1,5},{5... | collective-permute-start | bytes 1572872 | tf_op jit(solution)/shard_map/ppermute | solution.py:253
  216.2 9.0 %collective-permute-start.20 = (bf16[512,256]{1,0:T(8,128)(2,1)S(1)}, bf16[512,256]{1,0:T(8,128)(2,1)S(1)}, u32[]{:S(2)}, u32[]{:S(2)}) collective-permute-start(bf16[512,256]{1,0:T(8,128)(2,1)S(1)} %pad_maximum_fusion.32), channel_id=1, source_target_pairs={{0,1},{1,0},{2,3},{3,2},{4,5},{5,4},{6,7},{7,6},{8,9},{9,8},{10,11... | collective-permute-start | bytes 786440 | tf_op jit(solution)/shard_map/ppermute | solution.py:253
  225.1 5.7 %collective-permute-start.31 = (bf16[512,512]{1,0:T(8,128)(2,1)S(1)}, bf16[512,512]{1,0:T(8,128)(2,1)S(1)}, u32[]{:S(2)}, u32[]{:S(2)}) collective-permute-start(bf16[512,512]{1,0:T(8,128)(2,1)S(1)} %pad_maximum_fusion.30), channel_id=1, source_target_pairs={{0,1},{1,0},{2,3},{3,2},{4,5},{5,4},{6,7},{7,6},{8,9},{9,8},{10,11... | collective-permute-start | bytes 1572872 | tf_op jit(solution)/shard_map/ppermute | solution.py:253
  229.8 13.4 %collective-permute-start.21 = (bf16[256,1024]{1,0:T(8,128)(2,1)S(1)}, bf16[256,1024]{1,0:T(8,128)(2,1)S(1)}, u32[]{:S(2)}, u32[]{:S(2)}) collective-permute-start(bf16[256,1024]{1,0:T(8,128)(2,1)S(1)} %get-tuple-element.112), channel_id=1, source_target_pairs={{0,2},{1,3},{2,0},{3,1},{4,6},{5,7},{6,4},{7,5},{8,10},{9,11},{10,... | collective-permute-start | bytes 1572872 | tf_op jit(solution)/shard_map/ppermute | solution.py:253
  231.1 12.4 %copy-start.48 = (bf16[1024,2048]{1,0:T(8,128)(2,1)S(1)}, bf16[1024,2048]{1,0:T(8,128)(2,1)}, u32[]{:S(2)}) copy-start(bf16[1024,2048]{1,0:T(8,128)(2,1)} %param.24) | copy-start | bytes 12582916
  243.2 2.7 collective-permute-start.22
  251.7 42.5 %collective-permute-start.29 = (bf16[4,128,1280]{2,1,0:T(8,128)(2,1)S(1)}, bf16[4,128,1280]{2,1,0:T(8,128)(2,1)S(1)}, u32[]{:S(2)}, u32[]{:S(2)}) collective-permute-start(bf16[4,128,1280]{2,1,0:T(8,128)(2,1)S(1)} %pad_maximum_fusion.7), channel_id=1, source_target_pairs={{0,8},{4,12},{8,0},{12,4},{16,24},{20,28},{24,16},{28,20},{1,9},{5... | collective-permute-start | bytes 3932168 | tf_op jit(solution)/shard_map/ppermute | solution.py:253
  254.7 32.6 %collective-permute-start.27 = (bf16[1,128,1024]{2,1,0:T(8,128)(2,1)S(1)}, bf16[1,128,1024]{2,1,0:T(8,128)(2,1)S(1)}, u32[]{:S(2)}, u32[]{:S(2)}) collective-permute-start(bf16[1,128,1024]{2,1,0:T(8,128)(2,1)S(1)} %dynamic-slice_convert_fusion.3), channel_id=1, source_target_pairs={{0,16},{4,20},{8,24},{12,28},{16,0},{20,4},{24,8},{28,12},{1,17},{... | collective-permute-start | bytes 786440 | tf_op jit(solution)/shard_map/ppermute | solution.py:253
  257.3 35.1 %collective-permute-start.28 = (bf16[1,128,1024]{2,1,0:T(8,128)(2,1)S(1)}, bf16[1,128,1024]{2,1,0:T(8,128)(2,1)S(1)}, u32[]{:S(2)}, u32[]{:S(2)}) collective-permute-start(bf16[1,128,1024]{2,1,0:T(8,128)(2,1)S(1)} %dynamic-slice_convert_fusion.2), channel_id=1, source_target_pairs={{0,16},{4,20},{8,24},{12,28},{16,0},{20,4},{24,8},{28,12},{1,17},{... | collective-permute-start | bytes 786440 | tf_op jit(solution)/shard_map/ppermute | solution.py:253
  274.0 21.8 %copy-start.8 = (bf16[1024,256]{1,0:T(8,128)(2,1)S(1)}, bf16[1024,256]{1,0:T(8,128)(2,1)}, u32[]{:S(2)}) copy-start(bf16[1024,256]{1,0:T(8,128)(2,1)} %get-tuple-element.76) | copy-start | bytes 1572868
  274.0 21.9 %copy-start.7 = (bf16[1024,256]{1,0:T(8,128)(2,1)S(1)}, bf16[1024,256]{1,0:T(8,128)(2,1)}, u32[]{:S(2)}) copy-start(bf16[1024,256]{1,0:T(8,128)(2,1)} %get-tuple-element.78) | copy-start | bytes 1572868
  274.0 22.1 %copy-start.31 = (bf16[1024,256]{1,0:T(8,128)(2,1)S(1)}, bf16[1024,256]{1,0:T(8,128)(2,1)}, u32[]{:S(2)}) copy-start(bf16[1024,256]{1,0:T(8,128)(2,1)} %get-tuple-element.77) | copy-start | bytes 1572868
  287.3 9.0 %copy-start.39 = (bf16[1,128,1024]{2,1,0:T(8,128)(2,1)}, bf16[1,128,1024]{2,1,0:T(8,128)(2,1)S(1)}, u32[]{:S(2)}) copy-start(bf16[1,128,1024]{2,1,0:T(8,128)(2,1)S(1)} %collective-permute-done.27) | copy-start | bytes 786436
  300.4 8.1 %copy-start.3 = (f32[2,1,2,128,512]{4,3,2,1,0:T(8,128)S(1)}, f32[2,1,2,128,512]{4,3,2,1,0:T(8,128)}, u32[]{:S(2)}) copy-start(f32[2,1,2,128,512]{4,3,2,1,0:T(8,128)} %constant_dynamic-slice_fusion.4) | copy-start | bytes 3145732
  307.8 4.0 copy-start.17
  307.8 4.0 copy-start.18
  (27 other events, 63.5 us)

commit v3 on v2

--- a/solution.py
+++ b/solution.py
@@ -228,6 +228,58 @@
     )(info, q, k, v, g, g, g, g, bias)
 
 
+def self_weights_kernel(info, x_ref, q_ref, k_ref, v_ref, wq_ref, wk_ref, wv_ref, grad_ref, part_ref, sums_ref):
+    block = part_ref.shape[0]
+    size = q_ref.shape[1]
+    at = pl.ds(pl.multiple_of(pl.program_id(0) * block, block), block)
+    total = None
+    for n, (d_ref, w_ref) in enumerate(((q_ref, wq_ref), (k_ref, wk_ref), (v_ref, wv_ref))):
+        grad_ref[:, n * size : (n + 1) * size] = product_tn(x_ref[...], d_ref[...]).astype(low)
+        part = product_nt(d_ref[at, :], w_ref[...])
+        total = part if total is None else total + part
+    part_ref[...] = total.astype(low)
+
+    @pl.when(pl.program_id(0) == 0)
+    def _():
+        sums_ref[...] = jnp.zeros_like(sums_ref)
+        sums_ref[0:1, :] = jnp.sum(q_ref[...].astype(jnp.float32), axis=0, keepdims=True)
+        sums_ref[1:2, :] = jnp.sum(v_ref[...].astype(jnp.float32), axis=0, keepdims=True)
+
+
+def self_weights(quart, x, dq, dk, dv, weight):
+    rows, width = x.shape
+    size = dq.shape[1]
+    block = 256
+    whole = pl.BlockSpec((rows, size), lambda i, s: (0, 0))
+
+    def slab(n):
+        return pl.BlockSpec((width, size), lambda i, s: (0, n * (width // size) + s[0]))
+
+    return pl.pallas_call(
+        self_weights_kernel,
+        out_shape=[
+            jax.ShapeDtypeStruct((width, 3 * size), low),
+            jax.ShapeDtypeStruct((rows, width), low),
+            jax.ShapeDtypeStruct((8, size), jnp.float32),
+        ],
+        grid_spec=pltpu.PrefetchScalarGridSpec(
+            num_scalar_prefetch=1,
+            grid=(rows // block,),
+            in_specs=[pl.BlockSpec((rows, block), lambda i, s: (0, i)), whole, whole, whole, slab(0), slab(1), slab(2)],
+            out_specs=[
+                pl.BlockSpec((block, 3 * size), lambda i, s: (i, 0)),
+                pl.BlockSpec((block, width), lambda i, s: (i, 0)),
+                pl.BlockSpec((8, size), lambda i, s: (0, 0)),
+            ],
+        ),
+        compiler_params=pltpu.CompilerParams(vmem_limit_bytes=VMEM_LIMIT),
+        cost_estimate=pl.CostEstimate(
+            flops=12 * rows * width * size, bytes_accessed=20 * rows * width, transcendentals=0
+        ),
+        name="self_weights",
+    )(quart.astype(jnp.int32).reshape(1), x, dq, dk, dv, weight, weight, weight)
+
+
 def pick_kernel(info, in_ref, out_ref):
     out_ref[...] = in_ref[...]
 
@@ -266,6 +318,11 @@
     return [first] + [d for d in every if d != first]
 
 
+def join(part, far):
+    pair = jnp.concatenate([part, far], axis=0)
+    return jnp.concatenate([pair, swap(pair, "mem", 1)], axis=0)
+
+
 class Halving:
     def __init__(self, parts, first):
         count = lax.axis_size("dp")
@@ -311,14 +368,15 @@
     return lax.optimization_barrier(values)
 
 
-def finale_kernel(a_ref, b_ref, f_ref, g_ref, h_ref, v_ref,
-                  oa_ref, ob_ref, of_ref, og_ref, ov_ref,
-                  ay, by, az, bz, gc, gs, gx, vs, vc, vx, vy, vz, send, recv):
+def finale_kernel(c_ref, f_ref, e_ref, s_ref, b_ref, g_ref, h_ref, v_ref,
+                  oc_ref, of_ref, os_ref, ob_ref, og_ref, ov_ref,
+                  by, bz, sz, gc, gs, gx, vs, vc, vx, vy, vz, send, recv):
     dp, mem = lax.axis_index("dp"), lax.axis_index("mem")
     y, row = dp % 2, dp // 2
-    chip, core = mem // 2, mem % 2
     groups = b_ref.shape[0]
-    far = a_ref.shape[0]
+    f32 = jnp.float32
+    wide = b_ref.shape[3] // 2
+    tall = h_ref.shape[0] // 2
 
     def quarter_of(m):
         return 2 * (m % 2) + m // 2
@@ -327,18 +385,17 @@
         return (m // 2) + (m % 2) * (3 - 2 * (m // 2))
 
     barrier = pltpu.get_barrier_semaphore()
-    peers = [{"mem": mem ^ 1}, {"mem": mem ^ 2}, {"dp": dp ^ 1}]
-    peers += [{"dp": (row ^ j) * 2 + y} for j in range(1, groups)]
+    core_peer, chip_peer, y_peer = {"mem": mem ^ 1}, {"mem": mem ^ 2}, {"dp": dp ^ 1}
+    row_peers = [{"dp": (row ^ j) * 2 + y} for j in range(1, groups)]
+    peers = [core_peer, chip_peer, y_peer] + row_peers
     for peer in peers:
         pl.semaphore_signal(barrier, inc=1, device_id=peer, device_id_type=pl.DeviceIdType.MESH)
     pl.semaphore_wait(barrier, len(peers))
 
-    count = [0]
     sent = []
 
     def start(src, dst, peer):
-        n = count[0]
-        count[0] += 1
+        n = len(sent)
         copy = pltpu.make_async_remote_copy(
             src_ref=src, dst_ref=dst, send_sem=send.at[n], recv_sem=recv.at[n],
             device_id=peer, device_id_type=pl.DeviceIdType.MESH,
@@ -347,123 +404,142 @@
         sent.append(copy)
         return copy
 
-    core_peer, chip_peer, y_peer = peers[:3]
-    f32 = jnp.float32
-
-    copy_ay = start(a_ref.at[:, 1 - y], ay, y_peer)
-    copy_by = start(b_ref.at[:, 1 - y], by, y_peer)
-    mine_q = quarter_of(mem)
+    def to_rows(source, target, own):
+        return [start(source(row ^ j), target(own), row_peers[j - 1]) for j in range(1, groups)]
+
+    def wait_all(copies):
+        for copy in copies:
+            copy.wait_recv()
+
+    def columns(n):
+        return pl.ds(n * wide, wide)
+
+    def lines(n):
+        return pl.ds(n * tall, tall)
+
+    mine_q, other_q = quarter_of(mem), quarter_of(mem ^ 2)
+    block, other = block_of(mem), block_of(mem ^ 2)
+
+    copy_vy = start(v_ref, vy, y_peer)
+    copies_by = [start(b_ref.at[:, 1 - y, :, columns(n)], by.at[:, :, columns(n)], y_peer) for n in range(2)]
+    copy_g3 = start(g_ref.at[block_of(mem ^ 3)], gc.at[1], core_peer)
+    copy_cx = start(c_ref, oc_ref.at[mine_q], chip_peer)
+    copies_sz = to_rows(lambda t: s_ref.at[t], lambda t: sz.at[t], row)
+    copy_g1 = start(g_ref.at[block_of(mem ^ 1)], gc.at[0], core_peer)
+    copy_cc = start(c_ref, oc_ref.at[mine_q], core_peer)
+    copy_f0 = start(f_ref, of_ref.at[mine_q], core_peer)
+    copy_f1 = start(e_ref, of_ref.at[other_q], core_peer)
+    sz[row] = s_ref[row]
+
+    copy_g3.wait_recv()
+    copies_gx = []
+    for n in range(2):
+        gs[lines(n)] = (g_ref[other, lines(n)].astype(f32) + gc[1, lines(n)].astype(f32)).astype(low)
+        copies_gx.append(start(gs.at[lines(n)], gx.at[lines(n)], chip_peer))
+    copy_vy.wait_recv()
+    vs[0] = v_ref[...] + vy[...]
+    vz[row] = vs[0]
+    copies_vz = to_rows(lambda t: vs.at[0], lambda t: vz.at[t], row)
+    oc_ref[mine_q] = c_ref[...]
     of_ref[mine_q] = f_ref[...]
-    copy_fx = start(f_ref, of_ref.at[mine_q], chip_peer)
-    copy_fc = start(f_ref, of_ref.at[mine_q], core_peer)
-    copy_g1 = start(g_ref.at[block_of(mem ^ 1)], gc.at[0], core_peer)
-    copy_g3 = start(g_ref.at[block_of(mem ^ 3)], gc.at[1], core_peer)
-    copy_vc = start(v_ref, vc, core_peer)
-
-    copy_g3.wait_recv()
-    gs[...] = (g_ref[block_of(mem ^ 2)].astype(f32) + gc[1].astype(f32)).astype(low)
-    copy_gx = start(gs, gx, chip_peer)
-    copy_vc.wait_recv()
-    vs[0] = v_ref[...] + vc[...]
-    copy_vx = start(vs.at[0], vx, chip_peer)
+    of_ref[other_q] = e_ref[...]
     copy_g1.wait_recv()
 
-    copy_vx.wait_recv()
-    vs[1] = vs[0] + vx[...]
-    copy_vy = start(vs.at[1], vy, y_peer)
-
-    copy_ay.wait_recv()
-    own_far = row // 2
-    for t in range(far):
-        ay[t] = (ay[t].astype(f32) + a_ref[t, y].astype(f32)).astype(low)
-    az[own_far] = ay[own_far]
-    copies_az = [
-        start(ay.at[own_far ^ j], az.at[own_far], {"dp": ((own_far ^ j) * 2 + row % 2) * 2 + y})
-        for j in range(1, far)
-    ]
-    copy_vy.wait_recv()
-    vs[2] = vs[1] + vy[...]
-    vz[row] = vs[2]
-    copies_vz = [start(vs.at[2], vz.at[row], {"dp": (row ^ j) * 2 + y}) for j in range(1, groups)]
-    copy_gx.wait_recv()
-    block = block_of(mem)
-    total = h_ref[...] + g_ref[block].astype(f32) + gc[0].astype(f32) + gx[...].astype(f32)
-    og_ref[block] = total.astype(low)
-    copy_gax = start(og_ref.at[block], og_ref.at[block], chip_peer)
-    copy_gac = start(og_ref.at[block], og_ref.at[block], core_peer)
-    copy_by.wait_recv()
-    for t in range(groups):
-        by[t] = (by[t].astype(f32) + b_ref[t, y].astype(f32)).astype(low)
-    bz[row] = by[row]
-    copies_bz = [start(by.at[row ^ j], bz.at[row], {"dp": (row ^ j) * 2 + y}) for j in range(1, groups)]
-
-    other_q = quarter_of(mem ^ 2)
-    copy_fx.wait_recv()
-    copy_fr = start(of_ref.at[other_q], of_ref.at[other_q], core_peer)
-    for copy in copies_az:
-        copy.wait_recv()
-    total = az[0].astype(f32)
-    for t in range(1, far):
-        total = total + az[t].astype(f32)
-    oa_ref[mine_q] = total.astype(low)
-    copy_aax = start(oa_ref.at[mine_q], oa_ref.at[mine_q], chip_peer)
-    copy_aac = start(oa_ref.at[mine_q], oa_ref.at[mine_q], core_peer)
-    copy_gax.wait_recv()
-    other = block_of(mem ^ 2)
-    copy_gr = start(og_ref.at[other], og_ref.at[other], core_peer)
-    for copy in copies_vz:
-        copy.wait_recv()
+    copies_bz = []
+
+    def first_half(n):
+        copies_by[n].wait_recv()
+        for t in range(groups):
+            by[t, :, columns(n)] = (
+                by[t, :, columns(n)].astype(f32) + b_ref[t, y, :, columns(n)].astype(f32)
+            ).astype(low)
+        bz[row, :, columns(n)] = by[row, :, columns(n)]
+        copies_bz.append(
+            to_rows(lambda t: by.at[t, :, columns(n)], lambda t: bz.at[t, :, columns(n)], row)
+        )
+
+    def rows_total(n):
+        copies_gx[n].wait_recv()
+        total = h_ref[lines(n)] + g_ref[block, lines(n)].astype(f32)
+        total = total + gc[0, lines(n)].astype(f32) + gx[lines(n)].astype(f32)
+        og_ref[block, lines(n)] = total.astype(low)
+        piece = og_ref.at[block, lines(n)]
+        return [start(piece, piece, chip_peer), start(piece, piece, core_peer)]
+
+    first_half(0)
+    wait_all(copies_vz)
     total = vz[0]
     for t in range(1, groups):
         total = total + vz[t]
-    ov_ref[...] = total
-    for copy in copies_bz:
-        copy.wait_recv()
-    total = bz[0].astype(f32)
+    vs[1] = total
+    copy_vc = start(vs.at[1], vc, core_peer)
+    wait_all(copies_sz)
+    total = sz[0].astype(f32)
     for t in range(1, groups):
-        total = total + bz[t].astype(f32)
-    ob_ref[mine_q] = total.astype(low)
-    copy_bax = start(ob_ref.at[mine_q], ob_ref.at[mine_q], chip_peer)
-    copy_bac = start(ob_ref.at[mine_q], ob_ref.at[mine_q], core_peer)
-    copy_aax.wait_recv()
-    copy_ar = start(oa_ref.at[other_q], oa_ref.at[other_q], core_peer)
-    copy_bax.wait_recv()
-    copy_br = start(ob_ref.at[other_q], ob_ref.at[other_q], core_peer)
-    for copy in (copy_fc, copy_gac, copy_aac, copy_bac, copy_fr, copy_gr, copy_ar, copy_br):
-        copy.wait_recv()
+        total = total + sz[t].astype(f32)
+    os_ref[mine_q] = total.astype(low)
+    piece_s = os_ref.at[mine_q]
+    copy_sx, copy_sc = start(piece_s, piece_s, chip_peer), start(piece_s, piece_s, core_peer)
+    copies_g0 = rows_total(0)
+    copy_vc.wait_recv()
+    vs[2] = vs[1] + vc[...]
+    copy_vx = start(vs.at[2], vx, chip_peer)
+    copy_cx.wait_recv()
+    copy_cr = start(oc_ref.at[other_q], oc_ref.at[other_q], core_peer)
+    first_half(1)
+    copies_g1 = rows_total(1)
+    copy_sx.wait_recv()
+    copy_sr = start(os_ref.at[other_q], os_ref.at[other_q], core_peer)
+
+    copies_b, relays = [], []
+    for n in range(2):
+        wait_all(copies_bz[n])
+        total = bz[0, :, columns(n)].astype(f32)
+        for t in range(1, groups):
+            total = total + bz[t, :, columns(n)].astype(f32)
+        ob_ref[mine_q, :, columns(n)] = total.astype(low)
+        piece = ob_ref.at[mine_q, :, columns(n)]
+        copies_b.append([start(piece, piece, chip_peer), start(piece, piece, core_peer)])
+        (copies_g0, copies_g1)[n][0].wait_recv()
+        piece = og_ref.at[other, lines(n)]
+        relays.append(start(piece, piece, core_peer))
+    copy_vx.wait_recv()
+    ov_ref[...] = vs[2] + vx[...]
+    for n in range(2):
+        copies_b[n][0].wait_recv()
+        piece = ob_ref.at[other_q, :, columns(n)]
+        relays.append(start(piece, piece, core_peer))
+    wait_all([copy_cc, copy_f0, copy_f1, copy_cr, copy_sc, copy_sr])
+    wait_all([copies_g0[1], copies_g1[1], copies_b[0][1], copies_b[1][1]] + relays)
     for copy in sent:
         copy.wait_send()
 
 
-def finale(a, b, f, g, h, v):
-    far, groups = a.shape[0], b.shape[0]
-    r, wa, wb, wf = a.shape[2], a.shape[3], b.shape[3], f.shape[1]
-    copies = 17 + (far - 1) + 2 * (groups - 1) + 4
+def finale(c, f, e, s, b, g, h, v):
+    groups, _, r, wb = b.shape
+    ws = s.shape[2]
+    copies = 29 + 4 * (groups - 1)
     vmem = pl.BlockSpec(memory_space=pltpu.VMEM)
     f32 = jnp.float32
+    half_rows = pltpu.VMEM(g.shape[1:], low)
+    vector = pltpu.VMEM(v.shape, f32)
     return pl.pallas_call(
         finale_kernel,
-        out_shape=[
-            jax.ShapeDtypeStruct((4, r, wa), low),
-            jax.ShapeDtypeStruct((4, r, wb), low),
-            jax.ShapeDtypeStruct((4, r, wf), low),
-            jax.ShapeDtypeStruct(g.shape, low),
-            jax.ShapeDtypeStruct(v.shape, f32),
-        ],
-        in_specs=[vmem] * 6,
-        out_specs=[vmem] * 5,
+        out_shape=[jax.ShapeDtypeStruct((4, r, a.shape[-1]), low) for a in (c, f, s, b)]
+        + [jax.ShapeDtypeStruct(g.shape, low), jax.ShapeDtypeStruct(v.shape, f32)],
+        in_specs=[vmem] * 8,
+        out_specs=[vmem] * 6,
         scratch_shapes=[
-            pltpu.VMEM((far, r, wa), low),
             pltpu.VMEM((groups, r, wb), low),
-            pltpu.VMEM((far, r, wa), low),
             pltpu.VMEM((groups, r, wb), low),
+            pltpu.VMEM((groups, r, ws), low),
             pltpu.VMEM((2,) + g.shape[1:], low),
-            pltpu.VMEM(g.shape[1:], low),
-            pltpu.VMEM(g.shape[1:], low),
+            half_rows,
+            half_rows,
             pltpu.VMEM((3,) + v.shape, f32),
-            pltpu.VMEM(v.shape, f32),
-            pltpu.VMEM(v.shape, f32),
-            pltpu.VMEM(v.shape, f32),
+            vector,
+            vector,
+            vector,
             pltpu.VMEM((groups,) + v.shape, f32),
             pltpu.SemaphoreType.DMA((copies,)),
             pltpu.SemaphoreType.DMA((copies,)),
@@ -473,10 +549,11 @@
         ),
         cost_estimate=pl.CostEstimate(flops=10**6, bytes_accessed=10**8, transcendentals=0),
         name="finale",
-    )(a, b, f, g, h, v)
-
-
-def unpack_kernel(a_ref, b_ref, f_ref, g_ref, qkv_ref, so_ref, cq_ref, ckv_ref, co_ref, fi_ref, fo_ref, gd_ref, *, quarter, piece):
+    )(c, f, e, s, b, g, h, v)
+
+
+def unpack_kernel(c_ref, f_ref, s_ref, b_ref, g_ref, v_ref, qkv_ref, so_ref, cq_ref, ckv_ref, co_ref, fi_ref, fo_ref, gd_ref,
+                  pb_ref, ng_ref, ns_ref, fb_ref, *, quarter, piece):
     f32 = jnp.float32
 
     def spread(source, start, count, size, target):
@@ -487,18 +564,22 @@
                 ].astype(f32)
 
     spread(b_ref, 0, 3, quarter, qkv_ref)
-    spread(a_ref, 0, 1, quarter, co_ref)
-    spread(a_ref, quarter, 1, quarter, cq_ref)
-    spread(a_ref, 2 * quarter, 2, quarter, ckv_ref)
-    spread(a_ref, 4 * quarter, 1, quarter, so_ref)
+    spread(c_ref, 0, 1, quarter, co_ref)
+    spread(c_ref, quarter, 1, quarter, cq_ref)
+    spread(c_ref, 2 * quarter, 2, quarter, ckv_ref)
+    spread(s_ref, 0, 1, quarter, so_ref)
     spread(f_ref, 0, quarter * 4 // piece, piece, fi_ref)
     for p in range(4):
         fo_ref[p] = f_ref[p, :, 4 * quarter :].astype(f32)
         gd_ref[p] = g_ref[p].astype(f32)
-
-
-def unpack(a, b, f, g, width, hidden, piece):
-    r = a.shape[1]
+    at = 0
+    for target in (pb_ref, ng_ref, ns_ref, fb_ref):
+        target[...] = v_ref[at : at + target.shape[0], :]
+        at += target.shape[0]
+
+
+def unpack(c, f, s, b, g, v, width, hidden, piece):
+    r = c.shape[1]
     steps = 4 if r % 64 == 0 else 1
     h, gh = r // steps, g.shape[1] // steps
     f32 = jnp.float32
@@ -507,18 +588,21 @@
         return pl.BlockSpec((4, n, x.shape[2]), lambda i: (0, i, 0))
 
     wide = [3 * width, width, width, 2 * width, width, hidden]
+    counts = [7, 3, 3, hidden // width]
     return pl.pallas_call(
         functools.partial(unpack_kernel, quarter=width // 4, piece=piece),
         out_shape=[jax.ShapeDtypeStruct((r, w), f32) for w in wide]
-        + [jax.ShapeDtypeStruct((4, r, width), f32), jax.ShapeDtypeStruct(g.shape, f32)],
+        + [jax.ShapeDtypeStruct((4, r, width), f32), jax.ShapeDtypeStruct(g.shape, f32)]
+        + [jax.ShapeDtypeStruct((n, width), f32) for n in counts],
         grid=(steps,),
-        in_specs=[slots(a, h), slots(b, h), slots(f, h), slots(g, gh)],
+        in_specs=[slots(c, h), slots(f, h), slots(s, h), slots(b, h), slots(g, gh), pl.BlockSpec(v.shape, lambda i: (0, 0))],
         out_specs=[pl.BlockSpec((h, w), lambda i: (i, 0)) for w in wide]
-        + [pl.BlockSpec((4, h, width), lambda i: (0, i, 0)), slots(g, gh)],
+        + [pl.BlockSpec((4, h, width), lambda i: (0, i, 0)), slots(g, gh)]
+        + [pl.BlockSpec((n, width), lambda i: (0, 0)) for n in counts],
         compiler_params=pltpu.CompilerParams(vmem_limit_bytes=VMEM_LIMIT),
         cost_estimate=pl.CostEstimate(flops=10**6, bytes_accessed=2 * 10**7, transcendentals=0),
         name="unpack",
-    )(a, b, f, g)
+    )(c, f, s, b, g, v)
 
 
 def per_device(
@@ -635,9 +719,11 @@
     )
     dco = dh2.astype(low)
 
+    crossed_far = swap(crossed, "mem", 2)
+    dz, crossed_far = tie(dz, crossed_far)
     second_full = gather_rows(second_low)
     dz_full = gather_rows(dz)
-    dco_full = gather_rows(dco)
+    dco_far = swap(dco, "mem", 2)
     piece = hidden // groups // 4
     if piece % 128 == 0:
         w_in_q = pick_columns(ffn_in, piece, groups, 4, quart)
@@ -650,6 +736,9 @@
     act_q, slope_q = gelu_parts(product(second_full, w_in_q) + b_in_q)
     act_q = act_q.astype(low)
     du_q = (product_nt(dz_full, w_out_q) * slope_q).astype(low)
+    du_q, dco_far, third_low = tie(du_q, dco_far, third.astype(low))
+    dco_full = join(dco, dco_far)
+    third_far = swap(third_low, "mem", 2)
     sum_in = Halving([product_tn(second_full, du_q)], 1)
     sum_out = Halving([product_tn(act_q, dz_full)], min(2, groups // 2))
     send_in, send_out = sum_in.send(), sum_out.send()
@@ -661,7 +750,7 @@
     pair_base = chip * (quarter // 128)
     info_c = jnp.stack([pair_base]).astype(jnp.int32)
     bias_col = jnp.broadcast_to(mem_bias[:, None], (mem_bias.shape[0], 128))
-    dx4, send_in, send_out = tie(dx4, send_in, send_out)
+    dx4, send_in, send_out, third_far = tie(dx4, send_in, send_out, third_far)
     got_in, got_out = sum_in.move(send_in), sum_out.move(send_out)
     dq4, dkc4, dvc4 = attention_back(info_c, cq4, kc8, vc8, dx4, bias_col, False)
     dq4, dkc4, dvc4, got_in, got_out = tie(dq4, dkc4, dvc4, got_in, got_out)
@@ -669,70 +758,89 @@
     sum_out.add(got_out)
     dkv4 = jnp.concatenate([dkc4, dvc4], axis=1)
 
-    def to_rows(a):
+    def over_chips(a):
         b0, b2, b1, b3 = jnp.split(a, 4, axis=0)
-        over = swap(jnp.concatenate([b2, b3], axis=0), "mem", 2)
+        return jnp.concatenate([b2, b3], axis=0), b0, b1
+
+    def to_rows(over, b0, b1):
         size = b0.shape[0]
         mine = jnp.concatenate([b0, over[:size]], axis=0)
         other = swap(jnp.concatenate([b1, over[size:]], axis=0), "mem", 1)
         return by_quarter([mine[:size], mine[size:], other[:size], other[size:]])
 
-    dq_own = jnp.concatenate(to_rows(dq4), axis=1)
-    dkv_parts = to_rows(dkv4)
-    dkv_own = jnp.concatenate(
-        [a[:, :quarter] for a in dkv_parts] + [a[:, quarter:] for a in dkv_parts], axis=1
-    )
-    grad_memory = product_nt(dkv_own, cross_kv)[None]
-    crossed_full = gather_rows(crossed)
-    attended_full = gather_rows(attended)
+    dq_leave, dq_0, dq_1 = over_chips(dq4)
+    dq_own = jnp.concatenate(to_rows(swap(dq_leave, "mem", 2), dq_0, dq_1), axis=1)
     send_in, send_out = sum_in.send(), sum_out.send()
     got_in, got_out = sum_in.move(send_in), sum_out.move(send_out)
+    crossed_full = join(crossed, crossed_far)
+    attended_full = gather_rows(attended)
+    sum_q = Halving(
+        [product_tn(crossed_full, cut(dco_full, wide, quarter)), product_tn(first_full, dq4)], 1
+    )
+    sum_kv = Halving([product_tn(mem_full, dkv4)], min(2, groups // 2))
+    send_q, send_kv = sum_q.send(), sum_kv.send()
+    got_q = sum_q.move(send_q)
 
     dh1, gain_one, shift_one = norm_back(
         dh2 + product_nt(dq_own, cross_q), first_norm, first_inv, norm_gain[0]
     )
     do = dh1.astype(low)
-    do_full = gather_rows(do)
-    sum_cross = Halving(
-        [
-            product_tn(crossed_full, cut(dco_full, wide, quarter)),
-            product_tn(first_full, dq4),
-            product_tn(mem_full, dkv4),
-            product_tn(attended_full, cut(do_full, wide, quarter)),
-        ],
-        min(2, groups // 2),
-    )
-    send_cross = sum_cross.send()
+    sum_in.add(got_in)
+    sum_out.add(got_out)
+    send_in, send_out = sum_in.send(), sum_out.send()
+    do, send_in, send_out, send_kv = tie(do, send_in, send_out, send_kv)
+    got_in, got_out = sum_in.move(send_in), sum_out.move(send_out)
+    got_kv = sum_kv.move(send_kv)
+    dkv_leave, dkv_0, dkv_1 = over_chips(dkv4)
+    do_far = swap(do, "mem", 2)
+    do_far, got_in, got_out, got_q, dkv_leave = tie(do_far, got_in, got_out, got_q, dkv_leave)
+    do_full = join(do, do_far)
+    dkv_far = swap(dkv_leave, "mem", 2)
+    sum_so = Halving([product_tn(attended_full, cut(do_full, wide, quarter))], 1)
 
     da4 = product_nt(do_full, cut(self_out, wide, quarter, 0)).astype(low)
     where = [0, 2, 3, 1]
     slots = [((me ^ n) % 2) * 2 + (me ^ n) // 2 for n in where]
     info_s = jnp.stack([pair_base, dec_len[0]] + slots).astype(jnp.int32)
-    da4, got_in, got_out, send_cross = tie(da4, got_in, got_out, send_cross)
     sum_in.add(got_in)
     sum_out.add(got_out)
-    send_in, send_out = sum_in.send(), sum_out.send()
-    da4, send_in, send_out = tie(da4, send_in, send_out)
-    got_in, got_out, got_cross = sum_in.move(send_in), sum_out.move(send_out), sum_cross.move(send_cross)
+    sum_q.add(got_q)
+    da4, got_kv = tie(da4, got_kv)
+    sum_kv.add(got_kv)
+    (g_in,), (g_out,) = sum_in.finish(), sum_out.finish()
+    ffn_grad = jnp.concatenate([g_in.astype(low), g_out.astype(low)], axis=1)
+    send_q, send_kv, send_so = sum_q.send(), sum_kv.send(), sum_so.send()
+    da4, send_q, send_kv, send_so, ffn_grad = tie(da4, send_q, send_kv, send_so, ffn_grad)
+    got_q, got_kv, got_so = sum_q.move(send_q), sum_kv.move(send_kv), sum_so.move(send_so)
+    ffn_far = swap(ffn_grad, "mem", 2)
     sq4, sk4, sv4 = attention_back(info_s, q8, k8, v8, da4, bias_col[:8], True)
-    sq4, sk4, sv4, got_in, got_out, got_cross = tie(sq4, sk4, sv4, got_in, got_out, got_cross)
-    sum_in.add(got_in)
-    sum_out.add(got_out)
-    sum_cross.add(got_cross)
-    (g_in,), (g_out,) = sum_in.finish(), sum_out.finish()
-
-    dqkv4 = jnp.concatenate([sq4, sk4, sv4], axis=1)
+    sq4, sk4, sv4, got_q, got_kv, got_so, ffn_far, dkv_far = tie(
+        sq4, sk4, sv4, got_q, got_kv, got_so, ffn_far, dkv_far
+    )
+    sum_q.add(got_q)
+    sum_kv.add(got_kv)
+    sum_so.add(got_so)
+    sum_q.kept = sum_q.kept + sum_kv.kept
+    send_q = sum_q.send()
+    sq4, sk4, sv4, send_q = tie(sq4, sk4, sv4, send_q)
+    sum_q.add(sum_q.move(send_q))
+
     per = width // groups
-    qkv_grad = product_tn(x_full, dqkv4).astype(low).reshape(groups // 2, 2, per, 3 * quarter)
-    qkv_q = jnp.concatenate([cut(self_qkv, n * width + wide, quarter) for n in range(3)], axis=1)
-    partial = product_nt(dqkv4, qkv_q).astype(low).reshape(4, block, width)
-    cross_grad = jnp.concatenate([part.astype(low) for part in sum_cross.kept], axis=2)
-    cross_grad = cross_grad.reshape(groups // 4, 2, per, cross_grad.shape[2])
-    ffn_grad = jnp.concatenate([g_in.astype(low), g_out.astype(low)], axis=1)
-    layer_out = by_block(gather_rows(third.astype(low)))[None]
+    qkv_grad, partial, own_sums = self_weights(quart, x_full, sq4, sk4, sv4, self_qkv)
+    qkv_grad = qkv_grad.reshape(groups // 2, 2, per, 3 * quarter)
+    partial = partial.reshape(4, block, width)
+    cross_grad = jnp.concatenate([part.astype(low) for part in sum_q.finish()], axis=1)
+    (so_grad,) = sum_so.kept
+    so_grad = so_grad.astype(low)
+    layer_out = by_block(join(third_low, third_far))[None]
+    dkv_parts = to_rows(dkv_far, dkv_0, dkv_1)
+    dkv_own = jnp.concatenate(
+        [a[:, :quarter] for a in dkv_parts] + [a[:, quarter:] for a in dkv_parts], axis=1
+    )
+    grad_memory = product_nt(dkv_own, cross_kv)[None]
 
     place = jnp.zeros((2, width), jnp.float32)
-    own_sums = jnp.stack([column_sum(sq4), column_sum(sv4)])
+    own_sums = own_sums[:2]
     place = lax.dynamic_update_slice(place, own_sums, (0, quart * quarter))
     packed = jnp.concatenate(
         [
@@ -757,9 +865,11 @@
         axis=0,
     )
     packed = jnp.pad(packed, ((0, -packed.shape[0] % 8), (0, 0)))
-    cross_w, qkv_w, ffn_w, grad_rows, packed = finale(cross_grad, qkv_grad, ffn_grad, partial, dh1, packed)
-    w_qkv, w_so, w_cq, w_ckv, w_co, w_fi, w_fo, grad_dec = unpack(
-        cross_w, qkv_w, ffn_w, grad_rows, width, hidden, piece
+    cross_w, ffn_w, so_w, qkv_w, grad_rows, packed = finale(
+        cross_grad, ffn_grad, ffn_far, so_grad, qkv_grad, partial, dh1, packed
+    )
+    w_qkv, w_so, w_cq, w_ckv, w_co, w_fi, w_fo, grad_dec, p_bias, n_gain, n_shift, f_bias = unpack(
+        cross_w, ffn_w, so_w, qkv_w, grad_rows, packed, width, hidden, piece
     )
     return (
         layer_out,
@@ -772,10 +882,10 @@
         w_co,
         w_fi,
         w_fo.reshape(-1, width),
-        packed[:7],
-        packed[13 : 13 + hidden // width].reshape(hidden),
-        packed[7:10],
-        packed[10:13],
+        p_bias,
+        f_bias.reshape(hidden),
+        n_gain,
+        n_shift,
     )
 
 

time: 414 us -> 351 us (0.85)
  Pallas kernels: 148 us -> 125 us
  waiting for transfers between devices: 57.4 us -> 42.6 us
  matrix products: 95.5 us -> 81.8 us
  local copies, waits for them, and re-layouts: 39.3 us -> 27.7 us
  starting transfers between devices: 24.7 us -> 33.3 us
  other arithmetic: 37.4 us -> 32.9 us
    pallas_call x1 -> x2, Pallas kernels: 77.9 us -> 53.8 us  [the longest x1 46.1 us: finale(): pl.pallas_call(finale_kernel, out_shape=[jax.ShapeDtypeStruct((4, r, a.sh...]
    ppermute x32 -> x38, waiting for transfers between devices: 57.4 us -> 42.6 us  [swap(): return lax.ppermute(part, axis, [(i, i ^ distance) for i in range(count)])]
    dot_general x7 -> x6, matrix products: 28.6 us -> 14 us  [product_tn(): lax.dot_general(left_rows, right_rows, (((0,), (0,)), ((), ())), preferre...]
    ppermute x32 -> x38, starting transfers between devices: 24.7 us -> 33.3 us  [swap(): return lax.ppermute(part, axis, [(i, i ^ distance) for i in range(count)])]
    concatenate x9 -> x5, other arithmetic: 11.8 us -> 8.9 us  [gather_rows(): pair = jnp.concatenate([part, swap(part, 'mem', 2)], axis=0)]
    unnamed x132 -> x105, local copies, waits for them, and re-layouts: 10.6 us -> 9.41 us
  transfers between devices with their start and end apart: 32 -> 38, of which waited for: 11 -> 10; matrix products, arithmetic and copies ran while one was open for 30% -> 33% of each run, Pallas kernels for 13% -> 18%
where the time goes in v3:
time: 351 us; the launch traced here: 347 us
  Pallas kernels  125 us (36%)
  matrix products  81.8 us (23%)
  waiting for transfers between devices  42.6 us (12%)
  starting transfers between devices  33.3 us (9%)
  other arithmetic  32.9 us (9%)
  local copies, waits for them, and re-layouts  27.7 us (8%)
  between operations  3.57 us (1%)
    pallas_call x1, Pallas kernels, finale(): pl.pallas_call(finale_kernel, out_shape=[jax.ShapeDtypeStruct((4, r, a.sh...  46.1 us
    ppermute x38, waiting for transfers between devices, swap(): return lax.ppermute(part, axis, [(i, i ^ distance) for i in range(count)])  42.6 us
    dot_general x12, matrix products, product(): return jnp.dot(left_rows, right_rows, preferred_element_type=jnp.float32)  41.6 us
    pallas_call x2, Pallas kernels, attention_back(): pl.pallas_call(functools.partial(back_kernel, causal=causal), out_shape=[...  37.6 us
    ppermute x38, starting transfers between devices, swap(): return lax.ppermute(part, axis, [(i, i ^ distance) for i in range(count)])  33.3 us
    dot_general x7, matrix products, product_nt(): lax.dot_general(left_rows, right_rows, (((1,), (1,)), ((), ())), preferre...  26.2 us
    dot_general x6, matrix products, product_tn(): lax.dot_general(left_rows, right_rows, (((0,), (0,)), ((), ())), preferre...  14 us
    pallas_call x1, Pallas kernels, cross_forward(): pl.pallas_call(cross_fwd_kernel, out_shape=jax.ShapeDtypeStruct((rows, wi...  10.6 us
  transfers between devices with their start and end apart: 38, of which 10 were waited for; matrix products, arithmetic and copies ran while one was open for 33% of the time, Pallas kernels for 18%

profile of v3, /device:TPU:0, one launch (start us, length us, event | category | flops | bytes accessed | tf_op | source)
XLA Modules:
  0.0 347.0 jit_solution(4573824517560926525)
XLA Ops:
  3.0 4.2 %fusion.27.k_ref = bf16[1024,512]{1,0:T(8,128)(2,1)} fusion(bf16[1024,3072]{1,0:T(8,128)(2,1)} %wv_ref.1, s32[]{:T(128)S(6)} %select_n.325, bf16[1,1024,1024]{2,1,0:T(8,128)(2,1)} %param.16), kind=kOutput, calls=%fused_computation.50 | convolution fusion | flops 1074266112 | bytes 4194308 | tf_op jit(solution)/shard_map/dot_general | solution.py:18
  7.2 3.5 fusion.28.q_ref
  10.7 4.1 %fusion.29.v_ref = bf16[1024,512]{1,0:T(8,128)(2,1)} fusion(f32[512]{0:T(512)S(1)} %bitcast.320, bf16[1024,3072]{1,0:T(8,128)(2,1)} %wv_ref.1, s32[]{:T(128)S(6)} %select_n.326, bf16[1,1024,1024]{2,1,0:T(8,128)(2,1)} %param.16), kind=kOutput, calls=%fused_computation.52 | convolution fusion | flops 1074790400 | bytes 4196356 | tf_op jit(solution)/shard_map/dot_general | solution.py:18
  14.8 9.8 %self_forward.1 = bf16[512,512]{1,0:T(8,128)(2,1)} custom-call(s32[2]{0:T(128)} %pad_add_fusion.info, bf16[1024,512]{1,0:T(8,128)(2,1)} %fusion.28.q_ref, bf16[1024,512]{1,0:T(8,128)(2,1)} %fusion.27.k_ref, bf16[1024,512]{1,0:T(8,128)(2,1)} %fusion.29.v_ref), custom_call_target="tpu_custom_call" | custom-call | flops 3221225472 | bytes 4194304 | tf_op jit(solution)/shard_map/self_forward/pallas_call | solution.py:106
  26.2 2.2 collective-permute-start.2
  29.4 2.7 fusion.114
  32.4 8.8 %collective-permute-done.2 = bf16[256,1024]{1,0:T(8,128)(2,1)} collective-permute-done((bf16[256,1024]{1,0:T(8,128)(2,1)}, bf16[256,1024]{1,0:T(8,128)(2,1)}, u32[]{:S(2)}, u32[]{:S(2)}) %collective-permute-start.2) | collective-permute-done | bytes 524320 | tf_op jit(solution)/shard_map/ppermute | solution.py:305
  41.2 2.2 pad_maximum_fusion.6
  45.1 5.7 %pick_columns.1 = bf16[1024,1024]{1,0:T(8,128)(2,1)} custom-call(s32[1]{0:T(128)} %bitcast.28.info, bf16[1024,4096]{1,0:T(8,128)(2,1)} %in_ref.1), custom_call_target="tpu_custom_call" | custom-call | bytes 4194304 | tf_op jit(solution)/shard_map/pick_columns/pallas_call | solution.py:289
  51.4 3.1 constant_dynamic-slice_fusion.8
  54.6 1.7 collective-permute-start.15
  56.6 3.2 fusion.37.q_ref
  59.8 3.8 %convolution_convert_fusion.1.k_ref = bf16[1024,512]{1,0:T(8,128)(2,1)} fusion(bf16[1024,2048]{1,0:T(8,128)(2,1)S(1)} %copy-done.38, s32[]{:T(128)S(6)} %select_n.332, bf16[512,1024]{1,0:T(8,128)(2,1)} %collective-permute-done.3, bf16[256,1024]{1,0:T(8,128)(2,1)} %collective-permute-done.2, bf16[256,1024]{1,0:T(8,128)(2,1)} %bitcast.12), kind=kOutput, calls=%fused_computation.49 | convolution fusion | flops 1080557568 | bytes 4194308 | tf_op jit(solution)/shard_map/dot_general | solution.py:18
  63.5 3.7 %add_convert_fusion.v_ref = bf16[1024,512]{1,0:T(8,128)(2,1)} fusion(f32[512]{0:T(512)S(1)} %bitcast.322, bf16[1024,2048]{1,0:T(8,128)(2,1)S(1)} %copy-done.38, s32[]{:T(128)S(6)} %select_n.333, bf16[512,1024]{1,0:T(8,128)(2,1)} %collective-permute-done.3, bf16[256,1024]{1,0:T(8,128)(2,1)} %collective-permute-done.2, bf16[256,1024]{1,0:T(8,128)(2,1)} %bitcast.12), kind=kOutput, calls=%fused_computation.45 | convolution fusion | flops 1081081856 | bytes 4196356 | tf_op jit(solution)/shard_map/dot_general | solution.py:18
  67.3 10.6 %cross_forward.1 = bf16[512,512]{1,0:T(8,128)(2,1)} custom-call(bf16[512,512]{1,0:T(8,128)(2,1)} %fusion.37.q_ref, bf16[1024,512]{1,0:T(8,128)(2,1)} %convolution_convert_fusion.1.k_ref, bf16[1024,512]{1,0:T(8,128)(2,1)} %add_convert_fusion.v_ref, f32[1,1024]{1,0:T(1,128)} %bitcast.315), custom_call_target="tpu_custom_call" | custom-call | flops 4294967296 | bytes 2097152 | tf_op jit(solution)/shard_map/cross_forward/pallas_call | solution.py:140
  79.0 2.3 pad_maximum_fusion.4
  84.6 1.8 collective-permute-start.8
  86.4 6.3 %convolution_add_fusion = f32[256,4096]{1,0:T(8,128)S(1)} fusion(bf16[256,1024]{1,0:T(8,128)(2,1)S(1)} %fusion.63, bf16[1024,4096]{1,0:T(8,128)(2,1)} %in_ref.1, f32[4096]{0:T(1024)S(1)} %copy-done.37), kind=kOutput, calls=%fused_computation.3 | convolution fusion | flops 2148532224 | bytes 13123584 | tf_op jit(solution)/shard_map/dot_general | solution.py:18
  93.1 2.7 fusion.116
  96.6 1.5 add_convert_fusion.2
  98.1 6.5 %convert_reduce_fusion = (f32[4096]{0:T(1024)S(1)}, bf16[256,4096]{1,0:T(8,128)(2,1)}) fusion(f32[256,4096]{1,0:T(8,128)S(1)} %convolution_add_fusion, bf16[256,1024]{1,0:T(8,128)(2,1)} %get-tuple-element.83, bf16[4096,1024]{1,0:T(8,128)(2,1)S(1)} %bitcast.281), kind=kOutput, calls=%fused_computation.16 | convolution fusion | flops 2162159616 | bytes 15220736 | tf_op jit(solution)/shard_map/dot_general | solution.py:28
  104.7 4.7 %multiply_reduce_fusion = (f32[1024]{0:T(1024)S(1)}, f32[256]{0:T(256)S(1)}, f32[256]{0:T(256)S(1)}, f32[1024]{0:T(1024)S(1)}, f32[256,1024]{1,0:T(8,128)S(1)}) fusion(f32[256,1024]{1,0:T(8,128)S(1)} %get-tuple-element.235, f32[256]{0:T(256)S(1)} %add_rsqrt_fusion.1, f32[256]{0:T(256)S(1)} %broadcast_multiply_fusion.7, f32[1024]{0:T(1024)S(1)} %bitcast.292, ...), kind=kOutput, calls=%fused_computation.103 | convolution fusion | flops 2152461824 | bytes 14180612 | tf_op jit(solution)/shard_map/dot_general | solution.py:28
  110.5 1.7 collective-permute-start.6
  112.3 2.1 pad_maximum_fusion.8
  114.4 1.6 convert_reduce_fusion.2
  116.2 9.4 %collective-permute-done.6 = bf16[256,1024]{1,0:T(8,128)(2,1)} collective-permute-done((bf16[256,1024]{1,0:T(8,128)(2,1)}, bf16[256,1024]{1,0:T(8,128)(2,1)}, u32[]{:S(2)}, u32[]{:S(2)}) %collective-permute-start.6) | collective-permute-done | bytes 524320 | tf_op jit(solution)/shard_map/ppermute | solution.py:305
  127.0 3.0 fusion.36.q_ref
  134.1 3.7 %fusion.65 = f32[1024,1024]{1,0:T(8,128)S(1)} fusion(bf16[1024,1024]{1,0:T(8,128)(2,1)S(1)} %copy-done.10, bf16[512,1024]{1,0:T(8,128)(2,1)} %collective-permute-done.9, bf16[256,1024]{1,0:T(8,128)(2,1)} %collective-permute-done.8, bf16[256,1024]{1,0:T(8,128)(2,1)S(1)} %copy-done.9), kind=kOutput, calls=%fused_computation.136 | convolution fusion | flops 2153775104 | bytes 8388608 | tf_op jit(solution)/shard_map/dot_general | solution.py:18
  137.9 1.5 copy-done.7
  139.4 4.0 %fusion.6 = bf16[1024,1024]{1,0:T(8,128)(2,1)S(1)} fusion(f32[1024,1024]{1,0:T(8,128)S(1)} %fusion.65, bf16[1024,1024]{1,0:T(8,128)(2,1)S(1)} %constant_dynamic-update-slice_fusion, bf16[1024,1024]{1,0:T(8,128)(2,1)S(1)} %bitcast.265, f32[1024]{0:T(1024)S(1)} %bitcast.312), kind=kOutput, calls=%fused_computation.10 | convolution fusion | flops 2159017984 | bytes 10489856 | tf_op jit(solution)/shard_map/dot_general | solution.py:28
  143.4 1.3 pad_maximum_fusion.9
  144.9 1.8 collective-permute-start.12
  146.7 3.8 %fusion.64 = f32[1024,1024]{1,0:T(8,128)S(1)} fusion(bf16[1024,1024]{1,0:T(8,128)(2,1)S(1)} %fusion.6, bf16[512,1024]{1,0:T(8,128)(2,1)} %collective-permute-done.9, bf16[256,1024]{1,0:T(8,128)(2,1)} %collective-permute-done.8, bf16[256,1024]{1,0:T(8,128)(2,1)S(1)} %copy-done.9), kind=kOutput, calls=%fused_computation.135 | convolution fusion | flops 2153775104 | bytes 8388608 | tf_op jit(solution)/shard_map/dot_general | solution.py:22
  150.5 2.0 copy-done.4
  153.6 2.5 fusion.13
  157.4 2.9 convolution_convert_fusion.3.g0_ref.g1_ref.g2_ref.g3_ref
  161.5 1.5 collective-permute-start.17
  163.0 1.6 collective-permute-start.18
  164.6 2.2 pad_maximum_fusion.2
  168.8 21.9 %cross_back.1 = (bf16[1024,256]{1,0:T(8,128)(2,1)}, bf16[1024,256]{1,0:T(8,128)(2,1)}, bf16[1024,256]{1,0:T(8,128)(2,1)}) custom-call(s32[1]{0:T(128)} %bitcast.39.info, bf16[1024,256]{1,0:T(8,128)(2,1)} %fusion.36.q_ref, bf16[1024,512]{1,0:T(8,128)(2,1)} %convolution_convert_fusion.1.k_ref, bf16[1024,512]{1,0:T(8,128)(2,1)} %add_convert_fusion.v_ref, ...), custom_call_target="tpu_custom_call" | custom-call | flops 10737418240 | bytes 3670016 | tf_op jit(solution)/shard_map/cross_back/pallas_call | solution.py:207
  192.9 2.2 bitcast_add_fusion.1
  195.7 1.7 bitcast_add_fusion
  197.7 2.2 fusion.66
  200.1 2.8 fusion.108
  203.0 1.9 collective-permute-start.26
  204.9 1.3 constant_dynamic-update-slice_fusion.3
  209.6 2.8 collective-permute-done.22
  212.6 1.3 fusion.110
  215.9 1.5 maximum_bitcast_fusion
  217.4 2.6 collective-permute-start.24
  220.4 1.4 collective-permute-done.26
  221.9 1.6 collective-permute-start.28
  223.5 12.6 %collective-permute-done.24 = bf16[1,128,1024]{2,1,0:T(8,128)(2,1)S(1)} collective-permute-done((bf16[1,128,1024]{2,1,0:T(8,128)(2,1)S(1)}, bf16[1,128,1024]{2,1,0:T(8,128)(2,1)S(1)}, u32[]{:S(2)}, u32[]{:S(2)}) %collective-permute-start.24) | collective-permute-done | bytes 262176 | tf_op jit(solution)/shard_map/ppermute | solution.py:305
  236.0 4.5 %collective-permute-done.25 = bf16[1,128,1024]{2,1,0:T(8,128)(2,1)S(1)} collective-permute-done((bf16[1,128,1024]{2,1,0:T(8,128)(2,1)S(1)}, bf16[1,128,1024]{2,1,0:T(8,128)(2,1)S(1)}, u32[]{:S(2)}, u32[]{:S(2)}) %collective-permute-start.25) | collective-permute-done | bytes 262176 | tf_op jit(solution)/shard_map/ppermute | solution.py:305
  243.5 2.6 convolution_convert_fusion.2.g0_ref.g1_ref.g2_ref.g3_ref
  247.3 2.0 fusion.20
  251.0 1.4 collective-permute-start.32
  253.7 15.7 %self_back.1 = (bf16[1024,256]{1,0:T(8,128)(2,1)}, bf16[1024,256]{1,0:T(8,128)(2,1)}, bf16[1024,256]{1,0:T(8,128)(2,1)}) custom-call(s32[6]{0:T(128)} %stack.117.info, bf16[1024,512]{1,0:T(8,128)(2,1)} %fusion.28.q_ref, bf16[1024,512]{1,0:T(8,128)(2,1)} %fusion.27.k_ref, bf16[1024,512]{1,0:T(8,128)(2,1)} %fusion.29.v_ref, ...), custom_call_target="tpu_custom_call" | custom-call | flops 5368709120 | bytes 3670016 | tf_op jit(solution)/shard_map/self_back/pallas_call | solution.py:207
  270.4 3.5 %collective-permute-start.36 = (bf16[1,128,1024]{2,1,0:T(8,128)(2,1)S(1)}, bf16[1,128,1024]{2,1,0:T(8,128)(2,1)S(1)}, u32[]{:S(2)}, u32[]{:S(2)}) collective-permute-start(bf16[1,128,1024]{2,1,0:T(8,128)(2,1)S(1)} %pad_maximum_fusion.28), channel_id=1, source_target_pairs={{0,16},{4,20},{8,24},{12,28},{16,0},{20,4},{24,8},{28,12},{1,17},{... | collective-permute-start | bytes 786440 | tf_op jit(solution)/shard_map/ppermute | solution.py:305
  275.1 7.7 %self_weights.1 = (bf16[1024,768]{1,0:T(8,128)(2,1)}, bf16[1024,1024]{1,0:T(8,128)(2,1)}, f32[8,256]{1,0:T(8,128)}) custom-call(s32[1]{0:T(128)} %bitcast.28.info, bf16[1024,1024]{1,0:T(8,128)(2,1)} %bitcast.263, bf16[1024,256]{1,0:T(8,128)(2,1)} %get-tuple-element.127.q_ref, bf16[1024,256]{1,0:T(8,128)(2,1)} %get-tuple-element.128.k_ref, ...), custom_call_target="tpu_custom_call" | custom-call | flops 3221225472 | bytes 20971520 | tf_op jit(solution)/shard_map/self_weights/pallas_call | solution.py:258
  287.2 4.4 %convolution_bitcast_fusion = f32[1,256,1024]{2,1,0:T(8,128)} fusion(bf16[256,2048]{1,0:T(8,128)(2,1)S(1)} %get-tuple-element.201, bf16[1024,2048]{1,0:T(8,128)(2,1)} %param.24), kind=kOutput, calls=%fused_computation.53 | convolution fusion | flops 1073741824 | bytes 6291456 | tf_op jit(solution)/shard_map/dot_general | solution.py:28
  291.7 46.1 %finale.1 = (bf16[4,128,1024]{2,1,0:T(8,128)(2,1)}, bf16[4,128,2048]{2,1,0:T(8,128)(2,1)}, bf16[4,128,256]{2,1,0:T(8,128)(2,1)}, bf16[4,128,768]{2,1,0:T(8,128)(...) custom-call(bf16[128,1024]{1,0:T(8,128)(2,1)} %pad_maximum_fusion.29.c_ref, bf16[128,2048]{1,0:T(8,128)(2,1)} %copy-done.6, ...), custom_call_target="tpu_custom_call" | custom-call | flops 1000000 | bytes 100000000 | tf_op jit(solution)/shard_map/finale/pallas_call | solution.py:526
  337.8 7.7 %unpack.1 = (f32[128,3072]{1,0:T(8,128)}, f32[128,1024]{1,0:T(8,128)}, f32[128,1024]{1,0:T(8,128)}, f32[128,2048]{1,0:T(8,128)}, f32[128,1024]{1,0:T(8,128)}, /*...) custom-call(bf16[4,128,1024]{2,1,0:T(8,128)(2,1)} %get-tuple-element, ...), custom_call_target="tpu_custom_call" | custom-call | flops 1000000 | bytes 20000000 | tf_op jit(solution)/shard_map/unpack/pallas_call | solution.py:592
  345.5 1.3 copy.63
  (270 shorter events, 47.2 us)
Async XLA Ops:
  0.6 56.0 %copy-start = (bf16[1024,1024]{1,0:T(8,128)(2,1)S(1)}, bf16[1024,1024]{1,0:T(8,128)(2,1)}, u32[]{:S(2)}) copy-start(bf16[1024,1024]{1,0:T(8,128)(2,1)} %param.23) | copy-start | bytes 6291460
  3.0 4.2 %copy-start.5 = (bf16[1,1024,1024]{2,1,0:T(8,128)(2,1)S(1)}, bf16[1,1024,1024]{2,1,0:T(8,128)(2,1)}, u32[]{:S(2)}) copy-start(bf16[1,1024,1024]{2,1,0:T(8,128)(2,1)} %param.16) | copy-start | bytes 6291460
  14.8 13.6 %copy-start.34 = (f32[3,1024]{1,0:T(4,128)S(1)}, f32[3,1024]{1,0:T(4,128)}, u32[]{:S(2)}) copy-start(f32[3,1024]{1,0:T(4,128)} %param.31) | copy-start | bytes 36868
  14.8 14.5 %copy-start.35 = (f32[3,1024]{1,0:T(4,128)S(1)}, f32[3,1024]{1,0:T(4,128)}, u32[]{:S(2)}) copy-start(f32[3,1024]{1,0:T(4,128)} %param.30) | copy-start | bytes 36868
  25.6 3.6 %collective-permute-start = (bf16[256,512]{1,0:T(8,128)(2,1)S(1)}, bf16[256,512]{1,0:T(8,128)(2,1)S(1)}, u32[]{:S(2)}, u32[]{:S(2)}) collective-permute-start(bf16[256,512]{1,0:T(8,128)(2,1)S(1)} %get-tuple-element.200), channel_id=1, source_target_pairs={{0,1},{1,0},{2,3},{3,2},{4,5},{5,4},{6,7},{7,6},{8,9},{9,8},{10,11... | collective-permute-start | bytes 786440 | tf_op jit(solution)/shard_map/ppermute | solution.py:305
  26.2 15.0 %collective-permute-start.2 = (bf16[256,1024]{1,0:T(8,128)(2,1)}, bf16[256,1024]{1,0:T(8,128)(2,1)}, u32[]{:S(2)}, u32[]{:S(2)}) collective-permute-start(bf16[256,1024]{1,0:T(8,128)(2,1)} %bitcast.12), channel_id=1, source_target_pairs={{0,2},{1,3},{2,0},{3,1},{4,6},{5,7},{6,4},{7,5},{8,10},{9,11},{10,... | collective-permute-start | bytes 1572872 | tf_op jit(solution)/shard_map/ppermute | solution.py:305
  43.4 16.3 %collective-permute-start.3 = (bf16[512,1024]{1,0:T(8,128)(2,1)}, bf16[512,1024]{1,0:T(8,128)(2,1)}, u32[]{:S(2)}, u32[]{:S(2)}) collective-permute-start(bf16[512,1024]{1,0:T(8,128)(2,1)} %pad_maximum_fusion.6), channel_id=1, source_target_pairs={{0,1},{1,0},{2,3},{3,2},{4,5},{5,4},{6,7},{7,6},{8,9},{9,8},{10,11... | collective-permute-start | bytes 3145736 | tf_op jit(solution)/shard_map/ppermute | solution.py:305
  44.5 12.1 %collective-permute-start.1 = (bf16[256,1024]{1,0:T(8,128)(2,1)}, bf16[256,1024]{1,0:T(8,128)(2,1)}, u32[]{:S(2)}, u32[]{:S(2)}) collective-permute-start(bf16[256,1024]{1,0:T(8,128)(2,1)} %fusion.62), channel_id=1, source_target_pairs={{0,1},{1,0},{2,3},{3,2},{4,5},{5,4},{6,7},{7,6},{8,9},{9,8},{10,11... | collective-permute-start | bytes 1572872 | tf_op jit(solution)/shard_map/ppermute | solution.py:305
  45.0 9.5 %copy-start.36 = (f32[1,1,4,256]{3,1,2,0:T(1,128)}, f32[1,1,4,256]{3,1,2,0:T(1,128)S(1)}, u32[]{:S(2)}) copy-start(f32[1,1,4,256]{3,1,2,0:T(1,128)S(1)} %copy.58) | copy-start | bytes 12292
  45.1 6.3 %copy-start.37 = (f32[4096]{0:T(1024)S(1)}, f32[4096]{0:T(1024)}, u32[]{:S(2)}) copy-start(f32[4096]{0:T(1024)} %param.29) | copy-start | bytes 49156
  51.4 4.9 %copy-start.12 = (bf16[256,1024]{1,0:T(8,128)(2,1)S(1)}, bf16[256,1024]{1,0:T(8,128)(2,1)}, u32[]{:S(2)}) copy-start(bf16[256,1024]{1,0:T(8,128)(2,1)} %copy-done.11) | copy-start | bytes 1572868
  54.6 24.5 %collective-permute-start.15 = (bf16[256,1024]{1,0:T(8,128)(2,1)}, bf16[256,1024]{1,0:T(8,128)(2,1)S(1)}, u32[]{:S(2)}, u32[]{:S(2)}) collective-permute-start(bf16[256,1024]{1,0:T(8,128)(2,1)} %fusion.62), channel_id=1, source_target_pairs={{0,2},{1,3},{2,0},{3,1},{4,6},{5,7},{6,4},{7,5},{8,10},{9,11},{10,... | collective-permute-start | bytes 1572872 | tf_op jit(solution)/shard_map/ppermute | solution.py:305
  56.3 25.5 %collective-permute-start.29 = (bf16[256,1024]{1,0:T(8,128)(2,1)S(1)}, bf16[256,1024]{1,0:T(8,128)(2,1)S(1)}, u32[]{:S(2)}, u32[]{:S(2)}) collective-permute-start(bf16[256,1024]{1,0:T(8,128)(2,1)S(1)} %copy-done.12), channel_id=1, source_target_pairs={{0,2},{1,3},{2,0},{3,1},{4,6},{5,7},{6,4},{7,5},{8,10},{9,11},{10,... | collective-permute-start | bytes 1572872 | tf_op jit(solution)/shard_map/ppermute | solution.py:305
  56.6 3.2 copy-start.38
  78.9 3.9 %collective-permute-start.4 = (bf16[256,512]{1,0:T(8,128)(2,1)S(1)}, bf16[256,512]{1,0:T(8,128)(2,1)S(1)}, u32[]{:S(2)}, u32[]{:S(2)}) collective-permute-start(bf16[256,512]{1,0:T(8,128)(2,1)S(1)} %get-tuple-element.198), channel_id=1, source_target_pairs={{0,1},{1,0},{2,3},{3,2},{4,5},{5,4},{6,7},{7,6},{8,9},{9,8},{10,11... | collective-permute-start | bytes 786440 | tf_op jit(solution)/shard_map/ppermute | solution.py:305
  79.0 3.8 %copy-start.27 = (bf16[256,1024]{1,0:T(8,128)(2,1)}, bf16[256,1024]{1,0:T(8,128)(2,1)S(1)}, u32[]{:S(2)}) copy-start(bf16[256,1024]{1,0:T(8,128)(2,1)S(1)} %collective-permute-done.15) | copy-start | bytes 1572868
  81.3 45.7 %collective-permute-start.16 = (bf16[512,1024]{1,0:T(8,128)(2,1)}, bf16[512,1024]{1,0:T(8,128)(2,1)}, u32[]{:S(2)}, u32[]{:S(2)}) collective-permute-start(bf16[512,1024]{1,0:T(8,128)(2,1)} %pad_maximum_fusion.4), channel_id=1, source_target_pairs={{0,1},{1,0},{2,3},{3,2},{4,5},{5,4},{6,7},{7,6},{8,9},{9,8},{10,11... | collective-permute-start | bytes 3145736 | tf_op jit(solution)/shard_map/ppermute | solution.py:305
  82.8 163.5 %collective-permute-start.30 = (bf16[512,1024]{1,0:T(8,128)(2,1)}, bf16[512,1024]{1,0:T(8,128)(2,1)}, u32[]{:S(2)}, u32[]{:S(2)}) collective-permute-start(bf16[512,1024]{1,0:T(8,128)(2,1)} %pad_maximum_fusion.13), channel_id=1, source_target_pairs={{0,1},{1,0},{2,3},{3,2},{4,5},{5,4},{6,7},{7,6},{8,9},{9,8},{10,11... | collective-permute-start | bytes 3145736 | tf_op jit(solution)/shard_map/ppermute | solution.py:305
  83.0 9.7 %copy-start.14 = (bf16[256,1024]{1,0:T(8,128)(2,1)}, bf16[256,1024]{1,0:T(8,128)(2,1)S(1)}, u32[]{:S(2)}) copy-start(bf16[256,1024]{1,0:T(8,128)(2,1)S(1)} %maximum_select_fusion.1) | copy-start | bytes 1572868
  84.3 8.7 %slice-start.2 = ((s8[8388608]{0:T(1024)(128)(4,1)}), s8[4194304]{0:T(1024)(128)(4,1)S(1)}, s32[]{:S(2)}) async-start(s8[8388608]{0:T(1024)(128)(4,1)} %bitcast.280), calls=%async_computation.2 | async-start | bytes 8388608
  84.6 27.7 %copy-start.8 = (bf16[256,1024]{1,0:T(8,128)(2,1)}, bf16[256,1024]{1,0:T(8,128)(2,1)S(1)}, u32[]{:S(2)}) copy-start(bf16[256,1024]{1,0:T(8,128)(2,1)S(1)} %fusion.63) | copy-start | bytes 1572868
  84.6 8.4 %slice-start.3 = ((s8[8388608]{0:T(1024)(128)(4,1)}), s8[4194304]{0:T(1024)(128)(4,1)S(1)}, s32[]{:S(2)}) async-start(s8[8388608]{0:T(1024)(128)(4,1)} %bitcast.280), calls=%async_computation.3 | async-start | bytes 8388608
  84.6 27.6 %collective-permute-start.8 = (bf16[256,1024]{1,0:T(8,128)(2,1)S(1)}, bf16[256,1024]{1,0:T(8,128)(2,1)}, u32[]{:S(2)}, u32[]{:S(2)}) collective-permute-start(bf16[256,1024]{1,0:T(8,128)(2,1)S(1)} %fusion.63), channel_id=1, source_target_pairs={{0,2},{1,3},{2,0},{3,1},{4,6},{5,7},{6,4},{7,5},{8,10},{9,11},{10,... | collective-permute-start | bytes 1572872 | tf_op jit(solution)/shard_map/ppermute | solution.py:305
  92.7 17.8 %collective-permute-start.5 = (bf16[256,1024]{1,0:T(8,128)(2,1)S(1)}, bf16[256,1024]{1,0:T(8,128)(2,1)S(1)}, u32[]{:S(2)}, u32[]{:S(2)}) collective-permute-start(bf16[256,1024]{1,0:T(8,128)(2,1)S(1)} %maximum_select_fusion.1), channel_id=1, source_target_pairs={{0,2},{1,3},{2,0},{3,1},{4,6},{5,7},{6,4},{7,5},{8,10},{9,11},{10,... | collective-permute-start | bytes 1572872 | tf_op jit(solution)/shard_map/ppermute | solution.py:305
  96.6 8.0 %slice-start = ((s8[8388608]{0:T(1024)(128)(4,1)}), s8[4194304]{0:T(1024)(128)(4,1)S(1)}, s32[]{:S(2)}) async-start(s8[8388608]{0:T(1024)(128)(4,1)} %bitcast.251), calls=%async_computation | async-start | bytes 8388608
  98.1 6.6 %slice-start.1 = ((s8[8388608]{0:T(1024)(128)(4,1)}), s8[4194304]{0:T(1024)(128)(4,1)S(1)}, s32[]{:S(2)}) async-start(s8[8388608]{0:T(1024)(128)(4,1)} %bitcast.251), calls=%async_computation.1 | async-start | bytes 8388608
  110.5 5.4 %copy-start.30 = (bf16[256,1024]{1,0:T(8,128)(2,1)}, bf16[256,1024]{1,0:T(8,128)(2,1)S(1)}, u32[]{:S(2)}) copy-start(bf16[256,1024]{1,0:T(8,128)(2,1)S(1)} %collective-permute-done.5) | copy-start | bytes 1572868
  110.5 15.1 %collective-permute-start.6 = (bf16[256,1024]{1,0:T(8,128)(2,1)}, bf16[256,1024]{1,0:T(8,128)(2,1)}, u32[]{:S(2)}, u32[]{:S(2)}) collective-permute-start(bf16[256,1024]{1,0:T(8,128)(2,1)} %get-tuple-element.83), channel_id=1, source_target_pairs={{0,2},{1,3},{2,0},{3,1},{4,6},{5,7},{6,4},{7,5},{8,10},{9,11},{10,... | collective-permute-start | bytes 1572872 | tf_op jit(solution)/shard_map/ppermute | solution.py:305
  114.3 19.7 %collective-permute-start.9 = (bf16[512,1024]{1,0:T(8,128)(2,1)}, bf16[512,1024]{1,0:T(8,128)(2,1)}, u32[]{:S(2)}, u32[]{:S(2)}) collective-permute-start(bf16[512,1024]{1,0:T(8,128)(2,1)} %pad_maximum_fusion.8), channel_id=1, source_target_pairs={{0,1},{1,0},{2,3},{3,2},{4,5},{5,4},{6,7},{7,6},{8,9},{9,8},{10,11... | collective-permute-start | bytes 3145736 | tf_op jit(solution)/shard_map/ppermute | solution.py:305
  115.9 27.5 %collective-permute-start.10 = (bf16[256,1024]{1,0:T(8,128)(2,1)}, bf16[256,1024]{1,0:T(8,128)(2,1)}, u32[]{:S(2)}, u32[]{:S(2)}) collective-permute-start(bf16[256,1024]{1,0:T(8,128)(2,1)} %get-tuple-element.165), channel_id=1, source_target_pairs={{0,2},{1,3},{2,0},{3,1},{4,6},{5,7},{6,4},{7,5},{8,10},{9,11},{10,... | collective-permute-start | bytes 1572872 | tf_op jit(solution)/shard_map/ppermute | solution.py:305
  116.2 10.8 %copy-start.28 = (bf16[256,1024]{1,0:T(8,128)(2,1)S(1)}, bf16[256,1024]{1,0:T(8,128)(2,1)}, u32[]{:S(2)}) copy-start(bf16[256,1024]{1,0:T(8,128)(2,1)} %copy-done.27) | copy-start | bytes 1572868
  126.9 10.9 %collective-permute-start.7 = (bf16[512,1024]{1,0:T(8,128)(2,1)S(1)}, bf16[512,1024]{1,0:T(8,128)(2,1)S(1)}, u32[]{:S(2)}, u32[]{:S(2)}) collective-permute-start(bf16[512,1024]{1,0:T(8,128)(2,1)S(1)} %pad_maximum_fusion.7), channel_id=1, source_target_pairs={{0,1},{1,0},{2,3},{3,2},{4,5},{5,4},{6,7},{7,6},{8,9},{9,8},{10,11... | collective-permute-start | bytes 3145736 | tf_op jit(solution)/shard_map/ppermute | solution.py:305
  127.0 3.0 copy-start.15
  130.0 4.1 %copy-start.9 = (bf16[256,1024]{1,0:T(8,128)(2,1)S(1)}, bf16[256,1024]{1,0:T(8,128)(2,1)}, u32[]{:S(2)}) copy-start(bf16[256,1024]{1,0:T(8,128)(2,1)} %copy-done.8) | copy-start | bytes 1572868
  130.0 4.1 %copy-start.10 = (bf16[1024,1024]{1,0:T(8,128)(2,1)S(1)}, bf16[1024,1024]{1,0:T(8,128)(2,1)}, u32[]{:S(2)}) copy-start(bf16[1024,1024]{1,0:T(8,128)(2,1)} %pick_columns.1) | copy-start | bytes 6291460
  130.1 36.8 %collective-permute-start.14 = (bf16[512,1024]{1,0:T(8,128)(2,1)S(1)}, bf16[512,1024]{1,0:T(8,128)(2,1)S(1)}, u32[]{:S(2)}, u32[]{:S(2)}) collective-permute-start(bf16[512,1024]{1,0:T(8,128)(2,1)S(1)} %pad_maximum_fusion.11), channel_id=1, source_target_pairs={{0,1},{1,0},{2,3},{3,2},{4,5},{5,4},{6,7},{7,6},{8,9},{9,8},{10,11... | collective-permute-start | bytes 3145736 | tf_op jit(solution)/shard_map/ppermute | solution.py:305
  144.8 12.6 %collective-permute-start.11 = (bf16[512,1024]{1,0:T(8,128)(2,1)S(1)}, bf16[512,1024]{1,0:T(8,128)(2,1)S(1)}, u32[]{:S(2)}, u32[]{:S(2)}) collective-permute-start(bf16[512,1024]{1,0:T(8,128)(2,1)S(1)} %pad_maximum_fusion.9), channel_id=1, source_target_pairs={{0,1},{1,0},{2,3},{3,2},{4,5},{5,4},{6,7},{7,6},{8,9},{9,8},{10,11... | collective-permute-start | bytes 3145736 | tf_op jit(solution)/shard_map/ppermute | solution.py:305
  144.9 15.5 %collective-permute-start.12 = (bf16[256,1024]{1,0:T(8,128)(2,1)S(1)}, bf16[256,1024]{1,0:T(8,128)(2,1)S(1)}, u32[]{:S(2)}, u32[]{:S(2)}) collective-permute-start(bf16[256,1024]{1,0:T(8,128)(2,1)S(1)} %copy-done.1), channel_id=1, source_target_pairs={{0,2},{1,3},{2,0},{3,1},{4,6},{5,7},{6,4},{7,5},{8,10},{9,11},{10,... | collective-permute-start | bytes 1572872 | tf_op jit(solution)/shard_map/ppermute | solution.py:305
  161.4 41.6 %collective-permute-start.13 = (bf16[512,1024]{1,0:T(8,128)(2,1)}, bf16[512,1024]{1,0:T(8,128)(2,1)}, u32[]{:S(2)}, u32[]{:S(2)}) collective-permute-start(bf16[512,1024]{1,0:T(8,128)(2,1)} %pad_maximum_fusion.10), channel_id=1, source_target_pairs={{0,1},{1,0},{2,3},{3,2},{4,5},{5,4},{6,7},{7,6},{8,9},{9,8},{10,11... | collective-permute-start | bytes 3145736 | tf_op jit(solution)/shard_map/ppermute | solution.py:305
  161.5 29.2 %collective-permute-start.17 = (bf16[4,128,1024]{2,1,0:T(8,128)(2,1)}, bf16[4,128,1024]{2,1,0:T(8,128)(2,1)}, u32[]{:S(2)}, u32[]{:S(2)}) collective-permute-start(bf16[4,128,1024]{2,1,0:T(8,128)(2,1)} %fusion.40), channel_id=1, source_target_pairs={{0,4},{4,0},{8,12},{12,8},{16,20},{20,16},{24,28},{28,24},{1,5},{5... | collective-permute-start | bytes 3145736 | tf_op jit(solution)/shard_map/ppermute | solution.py:305
  163.0 27.7 %collective-permute-start.18 = (bf16[4,128,1024]{2,1,0:T(8,128)(2,1)}, bf16[4,128,1024]{2,1,0:T(8,128)(2,1)}, u32[]{:S(2)}, u32[]{:S(2)}) collective-permute-start(bf16[4,128,1024]{2,1,0:T(8,128)(2,1)} %bitcast.35), channel_id=1, source_target_pairs={{0,8},{4,12},{8,0},{12,4},{16,24},{20,28},{24,16},{28,20},{1,9},{5... | collective-permute-start | bytes 3145736 | tf_op jit(solution)/shard_map/ppermute | solution.py:305
  167.7 23.0 %copy-start.18 = (f32[1024,256]{1,0:T(8,128)}, f32[1024,256]{1,0:T(8,128)S(1)}, u32[]{:S(2)}) copy-start(f32[1024,256]{1,0:T(8,128)S(1)} %fusion.14) | copy-start | bytes 3145732
  191.9 14.5 %collective-permute-start.19 = (bf16[512,256]{1,0:T(8,128)(2,1)S(1)}, bf16[512,256]{1,0:T(8,128)(2,1)S(1)}, u32[]{:S(2)}, u32[]{:S(2)}) collective-permute-start(bf16[512,256]{1,0:T(8,128)(2,1)S(1)} %pad_maximum_fusion.25), channel_id=1, source_target_pairs={{0,2},{1,3},{2,0},{3,1},{4,6},{5,7},{6,4},{7,5},{8,10},{9,11},{10,... | collective-permute-start | bytes 786440 | tf_op jit(solution)/shard_map/ppermute | solution.py:305
  195.2 14.1 %collective-permute-start.21 = (bf16[2,128,1024]{2,1,0:T(8,128)(2,1)S(1)}, bf16[2,128,1024]{2,1,0:T(8,128)(2,1)S(1)}, u32[]{:S(2)}, u32[]{:S(2)}) collective-permute-start(bf16[2,128,1024]{2,1,0:T(8,128)(2,1)S(1)} %fusion.67), channel_id=1, source_target_pairs={{0,8},{4,12},{8,0},{12,4},{16,24},{20,28},{24,16},{28,20},{1,9},{5... | collective-permute-start | bytes 1572872 | tf_op jit(solution)/shard_map/ppermute | solution.py:305
  197.5 14.9 %collective-permute-start.22 = (bf16[2,128,1024]{2,1,0:T(8,128)(2,1)S(1)}, bf16[2,128,1024]{2,1,0:T(8,128)(2,1)S(1)}, u32[]{:S(2)}, u32[]{:S(2)}) collective-permute-start(bf16[2,128,1024]{2,1,0:T(8,128)(2,1)S(1)} %fusion.68), channel_id=1, source_target_pairs={{0,4},{4,0},{8,12},{12,8},{16,20},{20,16},{24,28},{28,24},{1,5},{5... | collective-permute-start | bytes 1572872 | tf_op jit(solution)/shard_map/ppermute | solution.py:305
  203.0 18.9 %collective-permute-start.26 = (bf16[4,128,512]{2,1,0:T(8,128)(2,1)S(1)}, bf16[4,128,512]{2,1,0:T(8,128)(2,1)S(1)}, u32[]{:S(2)}, u32[]{:S(2)}) collective-permute-start(bf16[4,128,512]{2,1,0:T(8,128)(2,1)S(1)} %pad_maximum_fusion.21), channel_id=1, source_target_pairs={{0,4},{4,0},{8,12},{12,8},{16,20},{20,16},{24,28},{28,24},{1,5},{5... | collective-permute-start | bytes 1572872 | tf_op jit(solution)/shard_map/ppermute | solution.py:305
  206.4 1.6 collective-permute-start.20
  213.9 26.6 %collective-permute-start.23 = (bf16[256,1024]{1,0:T(8,128)(2,1)S(1)}, bf16[256,1024]{1,0:T(8,128)(2,1)S(1)}, u32[]{:S(2)}, u32[]{:S(2)}) collective-permute-start(bf16[256,1024]{1,0:T(8,128)(2,1)S(1)} %get-tuple-element.100), channel_id=1, source_target_pairs={{0,2},{1,3},{2,0},{3,1},{4,6},{5,7},{6,4},{7,5},{8,10},{9,11},{10,... | collective-permute-start | bytes 1572872 | tf_op jit(solution)/shard_map/ppermute | solution.py:305
  217.4 18.6 %collective-permute-start.24 = (bf16[1,128,1024]{2,1,0:T(8,128)(2,1)S(1)}, bf16[1,128,1024]{2,1,0:T(8,128)(2,1)S(1)}, u32[]{:S(2)}, u32[]{:S(2)}) collective-permute-start(bf16[1,128,1024]{2,1,0:T(8,128)(2,1)S(1)} %dynamic-slice_convert_fusion.3), channel_id=1, source_target_pairs={{0,16},{4,20},{8,24},{12,28},{16,0},{20,4},{24,8},{28,12},{1,17},{... | collective-permute-start | bytes 786440 | tf_op jit(solution)/shard_map/ppermute | solution.py:305
  219.9 20.6 %collective-permute-start.25 = (bf16[1,128,1024]{2,1,0:T(8,128)(2,1)S(1)}, bf16[1,128,1024]{2,1,0:T(8,128)(2,1)S(1)}, u32[]{:S(2)}, u32[]{:S(2)}) collective-permute-start(bf16[1,128,1024]{2,1,0:T(8,128)(2,1)S(1)} %dynamic-slice_convert_fusion.2), channel_id=1, source_target_pairs={{0,16},{4,20},{8,24},{12,28},{16,0},{20,4},{24,8},{28,12},{1,17},{... | collective-permute-start | bytes 786440 | tf_op jit(solution)/shard_map/ppermute | solution.py:305
  220.3 20.4 %copy-start.19 = (f32[1024,256]{1,0:T(8,128)S(1)}, f32[1024,256]{1,0:T(8,128)}, u32[]{:S(2)}) copy-start(f32[1024,256]{1,0:T(8,128)} %copy-done.18) | copy-start | bytes 3145732
  221.9 24.2 %collective-permute-start.28 = (bf16[4,128,512]{2,1,0:T(8,128)(2,1)S(1)}, bf16[4,128,512]{2,1,0:T(8,128)(2,1)S(1)}, u32[]{:S(2)}, u32[]{:S(2)}) collective-permute-start(bf16[4,128,512]{2,1,0:T(8,128)(2,1)S(1)} %bitcast.282), channel_id=1, source_target_pairs={{0,8},{4,12},{8,0},{12,4},{16,24},{20,28},{24,16},{28,20},{1,9},{5... | collective-permute-start | bytes 1572872 | tf_op jit(solution)/shard_map/ppermute | solution.py:305
  240.7 2.7 collective-permute-start.27
  240.9 28.5 %collective-permute-start.35 = (bf16[512,512]{1,0:T(8,128)(2,1)}, bf16[512,512]{1,0:T(8,128)(2,1)}, u32[]{:S(2)}, u32[]{:S(2)}) collective-permute-start(bf16[512,512]{1,0:T(8,128)(2,1)} %pad_maximum_fusion.22), channel_id=1, source_target_pairs={{0,2},{1,3},{2,0},{3,1},{4,6},{5,7},{6,4},{7,5},{8,10},{9,11},{10,... | collective-permute-start | bytes 1572872 | tf_op jit(solution)/shard_map/ppermute | solution.py:305
  242.0 7.2 %copy-start.6 = (bf16[128,2048]{1,0:T(8,128)(2,1)}, bf16[128,2048]{1,0:T(8,128)(2,1)S(1)}, u32[]{:S(2)}) copy-start(bf16[128,2048]{1,0:T(8,128)(2,1)S(1)} %pad_maximum_fusion.23.f_ref) | copy-start | bytes 1572868
  249.3 20.2 %collective-permute-start.34 = (bf16[128,2048]{1,0:T(8,128)(2,1)S(1)}, bf16[128,2048]{1,0:T(8,128)(2,1)S(1)}, u32[]{:S(2)}, u32[]{:S(2)}) collective-permute-start(bf16[128,2048]{1,0:T(8,128)(2,1)S(1)} %pad_maximum_fusion.23.f_ref), channel_id=1, source_target_pairs={{0,2},{1,3},{2,0},{3,1},{4,6},{5,7},{6,4},{7,5},{8,10},{9,11},{10,... | collective-permute-start | bytes 1572872 | tf_op jit(solution)/shard_map/ppermute | solution.py:305
  250.3 19.1 %collective-permute-start.31 = (bf16[2,128,512]{2,1,0:T(8,128)(2,1)}, bf16[2,128,512]{2,1,0:T(8,128)(2,1)S(1)}, u32[]{:S(2)}, u32[]{:S(2)}) collective-permute-start(bf16[2,128,512]{2,1,0:T(8,128)(2,1)} %pad_maximum_fusion.27), channel_id=1, source_target_pairs={{0,8},{4,12},{8,0},{12,4},{16,24},{20,28},{24,16},{28,20},{1,9},{5... | collective-permute-start | bytes 786440 | tf_op jit(solution)/shard_map/ppermute | solution.py:305
  251.0 18.4 %collective-permute-start.32 = (bf16[2,128,512]{2,1,0:T(8,128)(2,1)S(1)}, bf16[2,128,512]{2,1,0:T(8,128)(2,1)S(1)}, u32[]{:S(2)}, u32[]{:S(2)}) collective-permute-start(bf16[2,128,512]{2,1,0:T(8,128)(2,1)S(1)} %fusion.79), channel_id=1, source_target_pairs={{0,4},{4,0},{8,12},{12,8},{16,20},{20,16},{24,28},{28,24},{1,5},{5... | collective-permute-start | bytes 786440 | tf_op jit(solution)/shard_map/ppermute | solution.py:305
  252.4 17.0 %collective-permute-start.33 = (bf16[4,128,256]{2,1,0:T(8,128)(2,1)S(1)}, bf16[4,128,256]{2,1,0:T(8,128)(2,1)S(1)}, u32[]{:S(2)}, u32[]{:S(2)}) collective-permute-start(bf16[4,128,256]{2,1,0:T(8,128)(2,1)S(1)} %fusion.80), channel_id=1, source_target_pairs={{0,4},{4,0},{8,12},{12,8},{16,20},{20,16},{24,28},{28,24},{1,5},{5... | collective-permute-start | bytes 786440 | tf_op jit(solution)/shard_map/ppermute | solution.py:305
  269.5 5.5 %copy-start.20 = (bf16[128,2048]{1,0:T(8,128)(2,1)}, bf16[128,2048]{1,0:T(8,128)(2,1)S(1)}, u32[]{:S(2)}) copy-start(bf16[128,2048]{1,0:T(8,128)(2,1)S(1)} %collective-permute-done.34.e_ref) | copy-start | bytes 1572868
  270.4 14.6 %collective-permute-start.36 = (bf16[1,128,1024]{2,1,0:T(8,128)(2,1)S(1)}, bf16[1,128,1024]{2,1,0:T(8,128)(2,1)S(1)}, u32[]{:S(2)}, u32[]{:S(2)}) collective-permute-start(bf16[1,128,1024]{2,1,0:T(8,128)(2,1)S(1)} %pad_maximum_fusion.28), channel_id=1, source_target_pairs={{0,16},{4,20},{8,24},{12,28},{16,0},{20,4},{24,8},{28,12},{1,17},{... | collective-permute-start | bytes 786440 | tf_op jit(solution)/shard_map/ppermute | solution.py:305
  275.0 10.8 %collective-permute-start.37 = (bf16[512,512]{1,0:T(8,128)(2,1)S(1)}, bf16[512,512]{1,0:T(8,128)(2,1)S(1)}, u32[]{:S(2)}, u32[]{:S(2)}) collective-permute-start(bf16[512,512]{1,0:T(8,128)(2,1)S(1)} %pad_maximum_fusion.24), channel_id=1, source_target_pairs={{0,1},{1,0},{2,3},{3,2},{4,5},{5,4},{6,7},{7,6},{8,9},{9,8},{10,11... | collective-permute-start | bytes 1572872 | tf_op jit(solution)/shard_map/ppermute | solution.py:305
  275.1 8.5 %copy-start.33 = (bf16[4,128,256]{2,1,0:T(8,128)(2,1)S(1)}, bf16[4,128,256]{2,1,0:T(8,128)(2,1)}, u32[]{:S(2)}) copy-start(bf16[4,128,256]{2,1,0:T(8,128)(2,1)} %copy-done.32) | copy-start | bytes 786436
  282.8 3.0 copy-start.17
  (18 other events, 36.7 us)
